TPU v7x, 128 devices: a whole 4x4x4 slice. The times are simulated.
128 devices in a mesh: dp: 4 (over z), table: 32 (over x, y, core).
Axes of the slice: x: 4, y: 4, z: 4, core: 2. Of those that a mesh axis runs over, the one named last changes fastest.
Arguments:
- core_ids: int32 [16384, 32, 3, 2], P(('dp', 'table')), may hold values from 0 to 249
- bag_lengths: int32 [16384, 32], P(('dp', 'table')), may hold values from 1 to 2
- first_core: bfloat16 [32, 250, 512], P('table'), may hold values from -6 to 6
- middle_core: bfloat16 [32, 250, 64, 128], P('table'), may hold values from -0.75 to 0.75
- last_core: bfloat16 [32, 250, 512], P('table'), may hold values from -0.75 to 0.75
- grad_hidden: bfloat16 [16384, 1024], P(('dp', 'table')), may hold values from -0.1875 to 0.1875
Outputs:
- pooled: bfloat16 [16384, 4096], P(('dp', 'table'))
- weight_grad: float32 [4096, 1024], P('table', 'dp')
Inputs may be any that keep to these rules, and one draw needn't show every extreme that they name: `core_ids`: slots j >= bag_lengths[n, t] hold ids that are not used.
All inputs are finite; a program needn't handle non-finite values.
Results may differ from a plain program's by a relative error of at most 0.005.
Values may be sent and summed in bfloat16 or wider, within the bound.
No kernel may reach another device: no remote copies, remote signals or barrier semaphores. Data moves between devices by JAX's collectives and lax.ppermute only.
A program may use at most 128 MiB of HBM per device.

v0:
```python
import jax
import jax.numpy as jnp
from jax import lax
from jax.sharding import PartitionSpec as P

D1 = 8
D2 = 2
D3 = 8
RANK = 64
BAG = 2


def build_rows(wanted, counts, first, middle, last):
    block = wanted.shape[0]
    head = jnp.take(first, wanted[:, 0, :], axis=0).reshape(block, BAG, D1, RANK)
    centre = jnp.take(middle, wanted[:, 1, :], axis=0)
    prefix = jnp.einsum("njar,njrs->njas", head, centre, preferred_element_type=jnp.float32)
    prefix = prefix.astype(jnp.bfloat16).reshape(block, BAG, D1 * D2, RANK)
    tail = jnp.take(last, wanted[:, 2, :], axis=0).reshape(block, BAG, RANK, D3)
    rows = jnp.einsum("njps,njsc->njpc", prefix, tail, preferred_element_type=jnp.float32)
    rows = rows.reshape(block, BAG, D1 * D2 * D3)
    live = (jnp.arange(BAG, dtype=jnp.int32)[None, :] < counts[:, None]).astype(jnp.float32)
    return jnp.sum(rows * live[:, :, None], axis=1).astype(jnp.bfloat16)


def body(core_ids, bag_lengths, first_core, middle_core, last_core, grad_hidden):
    width = D1 * D2 * D3
    got_ids, got_counts = (
        lax.all_to_all(core_ids, "table", split_axis=1, concat_axis=0, tiled=True),
        lax.all_to_all(bag_lengths, "table", split_axis=1, concat_axis=0, tiled=True),
    )
    group_rows = got_ids.shape[0]
    block = min(group_rows, 512)
    steps_count = group_rows // block
    wanted = got_ids.reshape(steps_count, block, 3, BAG)
    counts = got_counts.reshape(steps_count, block)
    first = first_core[0]
    middle = middle_core[0]
    last = last_core[0]
    table_rows = lax.map(
        lambda pair: build_rows(pair[0], pair[1], first, middle, last), (wanted, counts)
    )
    table_rows = table_rows.reshape(group_rows, width)
    returned = lax.all_to_all(
        table_rows.reshape(group_rows, 1, width), "table", split_axis=0, concat_axis=1, tiled=True
    )
    pooled = returned.reshape(returned.shape[0], returned.shape[1] * width)
    hidden_units = grad_hidden.shape[1]
    n_data = lax.axis_size("dp")
    n_tables = lax.axis_size("table")
    whole = lax.dot_general(
        pooled, grad_hidden, (((0,), (0,)), ((), ())), preferred_element_type=jnp.float32
    )
    arranged = whole.reshape(n_tables, width, n_data, hidden_units // n_data)
    arranged = jnp.transpose(arranged, (2, 0, 1, 3)).reshape(
        n_data * n_tables * width, hidden_units // n_data
    )
    weight_grad = lax.psum_scatter(arranged, ("dp", "table"), scatter_dimension=0, tiled=True)
    return (pooled, weight_grad)


def solution(mesh):
    placed = (
        P(("dp", "table"), None, None, None),
        P(("dp", "table"), None),
        P("table", None, None),
        P("table", None, None, None),
        P("table", None, None),
        P(("dp", "table"), None),
    )
    return jax.shard_map(
        body,
        mesh=mesh,
        in_specs=placed,
        out_specs=(P(("dp", "table"), None), P("table", "dp")),
        check_vma=False,
    )
```

profile of v0, /device:TPU:1, one launch (start us, length us, event | category | flops | bytes accessed | tf_op | source)
XLA Modules:
  0.0 1253.0 jit_solution(1560222185661063051)
XLA Ops:
  7.2 8.6 all-to-all-start.1
  15.8 6.9 all-to-all-done.1
  26.9 7.5 all-to-all-done
  35.0 516.5 %while.10 = (s32[]{:T(128)}, bf16[8,512,128]{2,1,0:T(8,128)(2,1)}, s32[8,512,3,2]{1,0,3,2:T(8,128)}, bf16[250,512]{1,0:T(8,128)(2,1)}, bf16[250,64,128]{2,1,0:T(...) while((s32[]{:T(128)}, bf16[8,512,128]{2,1,0:T(8,128)(2,1)}, ...), condition=%wide.region_2.4_spmd, body=%wide.region_0.3_spmd.sunk | while | flops 161710080 | bytes 93331672 | solution.py:40
  58.2 15.8 %gather_fusion.1 = bf16[1024,64,128]{2,1,0:T(8,128)(2,1)} fusion(bf16[250,64,128]{2,1,0:T(8,128)(2,1)} %get-tuple-element.176, s32[1024]{0:T(1024)S(1)} %broadcast_clamp_fusion.7), kind=kCustom, calls=%fused_computation.2.clone.1 | custom fusion | bytes 33558528 | tf_op jit(solution)/shard_map/while/body/eval_jaxpr/jit(_take)/gather | solution.py:16
  74.0 9.1 fusion.24
  86.1 6.6 copy.112
  122.8 15.8 %gather_fusion.1 = bf16[1024,64,128]{2,1,0:T(8,128)(2,1)} fusion(bf16[250,64,128]{2,1,0:T(8,128)(2,1)} %get-tuple-element.176, s32[1024]{0:T(1024)S(1)} %broadcast_clamp_fusion.7), kind=kCustom, calls=%fused_computation.2.clone.1 | custom fusion | bytes 33558528 | tf_op jit(solution)/shard_map/while/body/eval_jaxpr/jit(_take)/gather | solution.py:16
  138.5 9.1 fusion.24
  150.6 6.6 copy.112
  187.3 15.8 %gather_fusion.1 = bf16[1024,64,128]{2,1,0:T(8,128)(2,1)} fusion(bf16[250,64,128]{2,1,0:T(8,128)(2,1)} %get-tuple-element.176, s32[1024]{0:T(1024)S(1)} %broadcast_clamp_fusion.7), kind=kCustom, calls=%fused_computation.2.clone.1 | custom fusion | bytes 33558528 | tf_op jit(solution)/shard_map/while/body/eval_jaxpr/jit(_take)/gather | solution.py:16
  203.1 9.1 fusion.24
  251.9 15.8 %gather_fusion.1 = bf16[1024,64,128]{2,1,0:T(8,128)(2,1)} fusion(bf16[250,64,128]{2,1,0:T(8,128)(2,1)} %get-tuple-element.176, s32[1024]{0:T(1024)S(1)} %broadcast_clamp_fusion.7), kind=kCustom, calls=%fused_computation.2.clone.1 | custom fusion | bytes 33558528 | tf_op jit(solution)/shard_map/while/body/eval_jaxpr/jit(_take)/gather | solution.py:16
  267.6 9.1 fusion.24
  316.4 15.8 %gather_fusion.1 = bf16[1024,64,128]{2,1,0:T(8,128)(2,1)} fusion(bf16[250,64,128]{2,1,0:T(8,128)(2,1)} %get-tuple-element.176, s32[1024]{0:T(1024)S(1)} %broadcast_clamp_fusion.7), kind=kCustom, calls=%fused_computation.2.clone.1 | custom fusion | bytes 33558528 | tf_op jit(solution)/shard_map/while/body/eval_jaxpr/jit(_take)/gather | solution.py:16
  332.2 9.1 fusion.24
  381.0 15.8 %gather_fusion.1 = bf16[1024,64,128]{2,1,0:T(8,128)(2,1)} fusion(bf16[250,64,128]{2,1,0:T(8,128)(2,1)} %get-tuple-element.176, s32[1024]{0:T(1024)S(1)} %broadcast_clamp_fusion.7), kind=kCustom, calls=%fused_computation.2.clone.1 | custom fusion | bytes 33558528 | tf_op jit(solution)/shard_map/while/body/eval_jaxpr/jit(_take)/gather | solution.py:16
  396.7 9.1 fusion.24
  445.5 15.8 %gather_fusion.1 = bf16[1024,64,128]{2,1,0:T(8,128)(2,1)} fusion(bf16[250,64,128]{2,1,0:T(8,128)(2,1)} %get-tuple-element.176, s32[1024]{0:T(1024)S(1)} %broadcast_clamp_fusion.7), kind=kCustom, calls=%fused_computation.2.clone.1 | custom fusion | bytes 33558528 | tf_op jit(solution)/shard_map/while/body/eval_jaxpr/jit(_take)/gather | solution.py:16
  461.3 9.1 fusion.24
  510.1 15.8 %gather_fusion.1 = bf16[1024,64,128]{2,1,0:T(8,128)(2,1)} fusion(bf16[250,64,128]{2,1,0:T(8,128)(2,1)} %get-tuple-element.176, s32[1024]{0:T(1024)S(1)} %broadcast_clamp_fusion.7), kind=kCustom, calls=%fused_computation.2.clone.1 | custom fusion | bytes 33558528 | tf_op jit(solution)/shard_map/while/body/eval_jaxpr/jit(_take)/gather | solution.py:16
  525.9 9.1 fusion.24
  560.0 16.8 %all-to-all-done.2 = bf16[32,2,8192]{2,1,0:T(2,128)(2,1)S(1)} async-done(((bf16[32,2,8192]{2,1,0:T(2,128)(2,1)}), bf16[32,2,8192]{2,1,0:T(2,128)(2,1)S(1)}, u32[]{:S(2)}, u32[]{:S(2)}) %all-to-all-start.2) | async-done | bytes 1048608 | tf_op jit(solution)/shard_map/all_to_all | solution.py:44
  588.7 657.4 %reduce-scatter.2.cloned.1.call-done = f32[128,256]{1,0:T(8,128)} async-done(((f32[16384,256]{1,0:T(8,128)}), f32[128,256]{1,0:T(8,128)}) %reduce-scatter.2.cloned.1.call-update) | async-done | bytes 131088 | tf_op jit(solution)/shard_map/reduce_scatter | solution.py:58
  (331 shorter events, 328.1 us)
Async XLA Ops:
  7.2 15.5 %all-to-all-start.1 = ((s32[128,32,1]{0,2,1:T(1,128)}), s32[128,32,1]{0,2,1:T(1,128)S(1)}, u32[]{:S(2)}, u32[]{:S(2)}) async-start(s32[128,32,1]{0,2,1:T(1,128)} %bitcast.113), calls=%async_computation.1 | async-start | bytes 32768 | tf_op jit(solution)/shard_map/all_to_all | solution.py:30
  22.6 11.7 all-to-all-start
  35.0 3.2 copy-start.1
  58.2 15.8 %copy-start.2 = (bf16[512,2,8,64]{3,2,1,0:T(8,128)(2,1)S(1)}, bf16[512,2,8,64]{3,2,1,0:T(8,128)(2,1)}, u32[]{:S(2)}) copy-start(bf16[512,2,8,64]{3,2,1,0:T(8,128)(2,1)} %copy.110) | copy-start | bytes 3145732 | tf_op jit(solution)/shard_map/while
  86.1 6.6 copy-start.3
  122.8 15.8 %copy-start.2 = (bf16[512,2,8,64]{3,2,1,0:T(8,128)(2,1)S(1)}, bf16[512,2,8,64]{3,2,1,0:T(8,128)(2,1)}, u32[]{:S(2)}) copy-start(bf16[512,2,8,64]{3,2,1,0:T(8,128)(2,1)} %copy.110) | copy-start | bytes 3145732 | tf_op jit(solution)/shard_map/while
  150.6 6.6 copy-start.3
  164.2 3.2 copy-start.1
  187.3 15.8 %copy-start.2 = (bf16[512,2,8,64]{3,2,1,0:T(8,128)(2,1)S(1)}, bf16[512,2,8,64]{3,2,1,0:T(8,128)(2,1)}, u32[]{:S(2)}) copy-start(bf16[512,2,8,64]{3,2,1,0:T(8,128)(2,1)} %copy.110) | copy-start | bytes 3145732 | tf_op jit(solution)/shard_map/while
  215.2 6.6 copy-start.3
  228.7 3.2 copy-start.1
  251.9 15.8 %copy-start.2 = (bf16[512,2,8,64]{3,2,1,0:T(8,128)(2,1)S(1)}, bf16[512,2,8,64]{3,2,1,0:T(8,128)(2,1)}, u32[]{:S(2)}) copy-start(bf16[512,2,8,64]{3,2,1,0:T(8,128)(2,1)} %copy.110) | copy-start | bytes 3145732 | tf_op jit(solution)/shard_map/while
  279.7 6.6 copy-start.3
  316.4 15.8 %copy-start.2 = (bf16[512,2,8,64]{3,2,1,0:T(8,128)(2,1)S(1)}, bf16[512,2,8,64]{3,2,1,0:T(8,128)(2,1)}, u32[]{:S(2)}) copy-start(bf16[512,2,8,64]{3,2,1,0:T(8,128)(2,1)} %copy.110) | copy-start | bytes 3145732 | tf_op jit(solution)/shard_map/while
  344.3 6.6 copy-start.3
  381.0 15.8 %copy-start.2 = (bf16[512,2,8,64]{3,2,1,0:T(8,128)(2,1)S(1)}, bf16[512,2,8,64]{3,2,1,0:T(8,128)(2,1)}, u32[]{:S(2)}) copy-start(bf16[512,2,8,64]{3,2,1,0:T(8,128)(2,1)} %copy.110) | copy-start | bytes 3145732 | tf_op jit(solution)/shard_map/while
  408.9 6.6 copy-start.3
  445.5 15.8 %copy-start.2 = (bf16[512,2,8,64]{3,2,1,0:T(8,128)(2,1)S(1)}, bf16[512,2,8,64]{3,2,1,0:T(8,128)(2,1)}, u32[]{:S(2)}) copy-start(bf16[512,2,8,64]{3,2,1,0:T(8,128)(2,1)} %copy.110) | copy-start | bytes 3145732 | tf_op jit(solution)/shard_map/while
  473.4 6.6 copy-start.3
  510.1 15.8 %copy-start.2 = (bf16[512,2,8,64]{3,2,1,0:T(8,128)(2,1)S(1)}, bf16[512,2,8,64]{3,2,1,0:T(8,128)(2,1)}, u32[]{:S(2)}) copy-start(bf16[512,2,8,64]{3,2,1,0:T(8,128)(2,1)} %copy.110) | copy-start | bytes 3145732 | tf_op jit(solution)/shard_map/while
  538.0 6.6 copy-start.3
  551.5 8.3 copy-start.4
  555.8 21.0 %all-to-all-start.2 = ((bf16[32,2,8192]{2,1,0:T(2,128)(2,1)}), bf16[32,2,8192]{2,1,0:T(2,128)(2,1)S(1)}, u32[]{:S(2)}, u32[]{:S(2)}) async-start(bf16[32,2,8192]{2,1,0:T(2,128)(2,1)} %reshape.163), calls=%async_computation.2 | async-start | bytes 2097152 | tf_op jit(solution)/shard_map/all_to_all | solution.py:44
  559.8 686.4 %reduce-scatter.2.cloned.1.call-start = ((), (), s32[]{:S(2)}) async-start(), calls=%async_computation.4 | async-start | bytes 16908288 | tf_op jit(solution)/shard_map/reduce_scatter | solution.py:58
  (13 other events, 32.4 us)
Sparse Core Ops, SparseCore 0:
  587.5 658.5 reduce-scatter.1
where the time goes:
time: 1260 us; the launch traced here: 1250 us
  waiting for transfers between devices  689 us (55%)
  local copies, waits for them, and re-layouts  401 us (32%)
  matrix products  117 us (9%)
  starting transfers between devices  16.8 us (1%)
  between operations  14.1 us (1%)
  other arithmetic  13.7 us (1%)
    reduce_scatter x1, waiting for transfers between devices, body(): lax.psum_scatter(arranged, ('dp', 'table'), scatter_dimension=0, tiled=True)  657 us
    gather x8, local copies, waits for them, and re-layouts, build_rows(): centre = jnp.take(middle, wanted[:, 1, :], axis=0)  126 us
    dot_general x8, matrix products, build_rows(): jnp.einsum('njar,njrs->njas', head, centre, preferred_element_type=jnp.fl...  72.8 us
    gather x24, local copies, waits for them, and re-layouts, build_rows(): jnp.take(first, wanted[:, 0, :], axis=0).reshape(block, BAG, D1, RANK)  61 us
    reshape x8, local copies, waits for them, and re-layouts, build_rows(): prefix = prefix.astype(jnp.bfloat16).reshape(block, BAG, D1 * D2, RANK)  53.1 us
    gather x24, local copies, waits for them, and re-layouts, build_rows(): tail = jnp.take(last, wanted[:, 2, :], axis=0).reshape(block, BAG, RANK, D3)  46.9 us
    dot_general x8, matrix products, build_rows(): jnp.einsum('njps,njsc->njpc', prefix, tail, preferred_element_type=jnp.fl...  42 us
    reshape x8, local copies, waits for them, and re-layouts, build_rows(): tail = jnp.take(last, wanted[:, 2, :], axis=0).reshape(block, BAG, RANK, D3)  26.3 us
  transfers between devices with their start and end apart: 4, of which 4 were waited for; matrix products, arithmetic and copies ran while one was open for 0% of the time, Pallas kernels for 0%

commit v1 on v0

v1 whole, which is shorter than its diff:
```python
import jax
import jax.numpy as jnp
from jax import lax
from jax.sharding import PartitionSpec as P

D1 = 8
D2 = 2
D3 = 8
RANK = 64
BAG = 2


def build_rows(wanted, first, middle, last):
    block = wanted.shape[0]
    head = jnp.take(first, wanted[:, 0, :], axis=0).reshape(block, BAG, D1, RANK)
    centre = jnp.take(middle, wanted[:, 1, :], axis=0)
    prefix = jnp.einsum("njar,njrs->njas", head, centre, preferred_element_type=jnp.float32)
    prefix = prefix.astype(jnp.bfloat16).reshape(block, BAG, D1 * D2, RANK)
    tail = jnp.take(last, wanted[:, 2, :], axis=0).reshape(block, BAG, RANK, D3)
    rows = jnp.einsum("njps,njsc->njpc", prefix, tail, preferred_element_type=jnp.float32)
    rows = rows.reshape(block, BAG, D1 * D2 * D3)
    return jnp.sum(rows, axis=1).astype(jnp.bfloat16)


def body(core_ids, bag_lengths, first_core, middle_core, last_core, grad_hidden):
    width = D1 * D2 * D3
    own, tables = bag_lengths.shape
    ncore = first_core.shape[1]
    n_data = lax.axis_size("dp")
    hidden_units = grad_hidden.shape[1]

    gathered = lax.all_gather(grad_hidden, "table", axis=0, tiled=True)

    ids = jnp.transpose(core_ids, (1, 2, 3, 0))
    lengths = jnp.transpose(bag_lengths)
    live = jnp.arange(BAG, dtype=jnp.int32)[None, :, None] < lengths[:, None, :]
    heads = jnp.where(live, ids[:, 0], ncore)
    sent = jnp.concatenate([heads, ids[:, 1], ids[:, 2]], axis=1)
    got = lax.all_to_all(sent, "table", split_axis=0, concat_axis=0, tiled=True)
    wanted = jnp.transpose(got.reshape(tables, 3, BAG, own), (0, 3, 1, 2))
    group_rows = tables * own
    block = min(group_rows, 512)
    wanted = wanted.reshape(group_rows // block, block, 3, BAG)

    first = jnp.pad(first_core[0], ((0, 8), (0, 0)))
    middle = middle_core[0]
    last = last_core[0]
    rows = lax.map(lambda w: build_rows(w, first, middle, last), wanted)
    rows = rows.reshape(group_rows, width)

    partial = lax.dot_general(
        rows, gathered, (((0,), (0,)), ((), ())), preferred_element_type=jnp.float32
    )
    partial = partial.reshape(width, n_data, hidden_units // n_data).transpose(1, 0, 2)
    weight_grad = lax.psum_scatter(partial, "dp", scatter_dimension=0, tiled=False)

    returned = lax.all_to_all(
        rows.reshape(group_rows, 1, width), "table", split_axis=0, concat_axis=1, tiled=True
    )
    pooled = returned.reshape(own, tables * width)
    return (pooled, weight_grad)


def solution(mesh):
    placed = (
        P(("dp", "table"), None, None, None),
        P(("dp", "table"), None),
        P("table", None, None),
        P("table", None, None, None),
        P("table", None, None),
        P(("dp", "table"), None),
    )
    return jax.shard_map(
        body,
        mesh=mesh,
        in_specs=placed,
        out_specs=(P(("dp", "table"), None), P("table", "dp")),
        check_vma=False,
    )
```

time: 1260 us -> 712 us (0.57)
  waiting for transfers between devices: 689 us -> 6.63 us
  local copies, waits for them, and re-layouts: 401 us -> 485 us
  matrix products: 117 us -> 170 us
  blocking collectives: 0 us -> 20.1 us
    reduce_scatter x1, waiting for transfers between devices: 657 us -> 0.01 us  [body(): lax.psum_scatter(partial, 'dp', scatter_dimension=0, tiled=False)]
    gather x24 -> x16, local copies, waits for them, and re-layouts: 46.9 us -> 197 us  [build_rows(): tail = jnp.take(last, wanted[:, 2, :], axis=0).reshape(block, BAG, RANK, D3)]
    reshape x18 -> x1, local copies, waits for them, and re-layouts: 49.7 us -> 0.02 us  [body(): wanted = wanted.reshape(group_rows // block, block, 3, BAG)]
    dot_general x8, matrix products: 42 us -> 79.3 us  [build_rows(): jnp.einsum('njps,njsc->njpc', prefix, tail, preferred_element_type=jnp.fl...]
    all_to_all x3 -> x1, waiting for transfers between devices: 31.1 us -> 5.93 us  [body(): got = lax.all_to_all(sent, 'table', split_axis=0, concat_axis=0, tiled=True)]
    all_to_all x0 -> x1, blocking collectives: none -> 20.1 us  [body(): lax.all_to_all(rows.reshape(group_rows, 1, width), 'table', split_axis=0,...]
    gather x24 -> x16, local copies, waits for them, and re-layouts: 61 us -> 48.2 us  [build_rows(): jnp.take(first, wanted[:, 0, :], axis=0).reshape(block, BAG, D1, RANK)]
  transfers between devices with their start and end apart: 4 -> 3, of which waited for: 4 -> 1; matrix products, arithmetic and copies ran while one was open for 0% -> 90% of each run, Pallas kernels for 0% -> 0%
where the time goes in v1:
time: 712 us; the launch traced here: 710 us
  local copies, waits for them, and re-layouts  485 us (68%)
  matrix products  170 us (24%)
  blocking collectives  20.1 us (3%)
  between operations  14.1 us (2%)
  starting transfers between devices  8.67 us (1%)
    gather x16, local copies, waits for them, and re-layouts, build_rows(): tail = jnp.take(last, wanted[:, 2, :], axis=0).reshape(block, BAG, RANK, D3)  197 us
    gather x8, local copies, waits for them, and re-layouts, build_rows(): centre = jnp.take(middle, wanted[:, 1, :], axis=0)  125 us
    dot_general x8, matrix products, build_rows(): jnp.einsum('njar,njrs->njas', head, centre, preferred_element_type=jnp.fl...  83.4 us
    dot_general x8, matrix products, build_rows(): jnp.einsum('njps,njsc->njpc', prefix, tail, preferred_element_type=jnp.fl...  79.3 us
    reshape x8, local copies, waits for them, and re-layouts, build_rows(): prefix = prefix.astype(jnp.bfloat16).reshape(block, BAG, D1 * D2, RANK)  53.2 us
    gather x16, local copies, waits for them, and re-layouts, build_rows(): jnp.take(first, wanted[:, 0, :], axis=0).reshape(block, BAG, D1, RANK)  48.2 us
    convert_element_type x8, local copies, waits for them, and re-layouts, build_rows(): prefix = prefix.astype(jnp.bfloat16).reshape(block, BAG, D1 * D2, RANK)  24.3 us
    all_to_all x1, blocking collectives, body(): lax.all_to_all(rows.reshape(group_rows, 1, width), 'table', split_axis=0,...  20.1 us
  transfers between devices with their start and end apart: 3, of which 1 were waited for; matrix products, arithmetic and copies ran while one was open for 90% of the time, Pallas kernels for 0%

profile of v1, /device:TPU:1, one launch (start us, length us, event | category | flops | bytes accessed | tf_op | source)
XLA Modules:
  0.0 710.3 jit_solution(13898430818379159608)
XLA Ops:
  25.9 633.0 %while.10 = (s32[]{:T(128)}, bf16[8,512,128]{2,1,0:T(8,128)(2,1)}, s32[8,512,3,2]{1,0,3,2:T(8,128)S(1)}, bf16[258,512]{1,0:T(8,128)(2,1)S(1)}, bf16[250,64,128]{...) while((s32[]{:T(128)}, bf16[8,512,128]{2,1,0:T(8,128)(2,1)}, s32[8,512,3,2]{1,0,3,2:T(8,128)S(1)}, ...), condition=%wide.region_1.2_spmd, body=%wide.region_0.1_spmd.sunk | while | flops 161576960 | bytes 75496048 | solution.py:48
  26.5 15.6 %gather_fusion = bf16[1024,64,128]{2,1,0:T(8,128)(2,1)} fusion(bf16[250,64,128]{2,1,0:T(8,128)(2,1)} %get-tuple-element.152, s32[1024]{0:T(1024)S(1)} %broadcast_clamp_fusion.6), kind=kCustom, calls=%fused_computation.1.clone.1 | custom fusion | bytes 33558528 | tf_op jit(solution)/shard_map/while/body/eval_jaxpr/jit(_take)/gather | solution.py:16
  48.6 11.0 %fusion.32 = bf16[512,2,8,128]{3,2,1,0:T(8,128)(2,1)} fusion(bf16[512,2,64,128]{3,2,1,0:T(8,128)(2,1)} %bitcast.87, pred[512,2]{1,0:T(8,128)(4,1)S(1)} %get-tuple-element.129, bf16[512,2,8,64]{3,2,1,0:T(8,128)(2,1)} %gather.30, pred[512,2]{1,0:T(8,128)(4,1)S(1)} %get-tuple-element.131), kind=kOutput, calls=%fused_computation.14.clone.1 | convolution fusion | flops 144179200 | bytes 19924992 | tf_op jit(solution)/shard_map/while/body/eval_jaxpr/njar,njrs->njas/dot_general | solution.py:17
  73.4 20.6 %gather.31 = bf16[512,2,64,8]{3,2,1,0:T(8,128)(2,1)} reshape(bf16[1024,512]{1,0:T(8,128)(2,1)S(1)} %gather_fusion.2) | data formatting | bytes 2097152 | tf_op jit(solution)/shard_map/while/body/eval_jaxpr/jit(_take)/gather | solution.py:19
  106.2 15.6 %gather_fusion = bf16[1024,64,128]{2,1,0:T(8,128)(2,1)} fusion(bf16[250,64,128]{2,1,0:T(8,128)(2,1)} %get-tuple-element.152, s32[1024]{0:T(1024)S(1)} %broadcast_clamp_fusion.6), kind=kCustom, calls=%fused_computation.1.clone.1 | custom fusion | bytes 33558528 | tf_op jit(solution)/shard_map/while/body/eval_jaxpr/jit(_take)/gather | solution.py:16
  128.3 10.3 %fusion.32 = bf16[512,2,8,128]{3,2,1,0:T(8,128)(2,1)} fusion(bf16[512,2,64,128]{3,2,1,0:T(8,128)(2,1)} %bitcast.87, pred[512,2]{1,0:T(8,128)(4,1)S(1)} %get-tuple-element.129, bf16[512,2,8,64]{3,2,1,0:T(8,128)(2,1)} %gather.30, pred[512,2]{1,0:T(8,128)(4,1)S(1)} %get-tuple-element.131), kind=kOutput, calls=%fused_computation.14.clone.1 | convolution fusion | flops 144179200 | bytes 19924992 | tf_op jit(solution)/shard_map/while/body/eval_jaxpr/njar,njrs->njas/dot_general | solution.py:17
  152.5 20.6 %gather.31 = bf16[512,2,64,8]{3,2,1,0:T(8,128)(2,1)} reshape(bf16[1024,512]{1,0:T(8,128)(2,1)S(1)} %gather_fusion.2) | data formatting | bytes 2097152 | tf_op jit(solution)/shard_map/while/body/eval_jaxpr/jit(_take)/gather | solution.py:19
  185.2 15.6 %gather_fusion = bf16[1024,64,128]{2,1,0:T(8,128)(2,1)} fusion(bf16[250,64,128]{2,1,0:T(8,128)(2,1)} %get-tuple-element.152, s32[1024]{0:T(1024)S(1)} %broadcast_clamp_fusion.6), kind=kCustom, calls=%fused_computation.1.clone.1 | custom fusion | bytes 33558528 | tf_op jit(solution)/shard_map/while/body/eval_jaxpr/jit(_take)/gather | solution.py:16
  207.3 10.3 %fusion.32 = bf16[512,2,8,128]{3,2,1,0:T(8,128)(2,1)} fusion(bf16[512,2,64,128]{3,2,1,0:T(8,128)(2,1)} %bitcast.87, pred[512,2]{1,0:T(8,128)(4,1)S(1)} %get-tuple-element.129, bf16[512,2,8,64]{3,2,1,0:T(8,128)(2,1)} %gather.30, pred[512,2]{1,0:T(8,128)(4,1)S(1)} %get-tuple-element.131), kind=kOutput, calls=%fused_computation.14.clone.1 | convolution fusion | flops 144179200 | bytes 19924992 | tf_op jit(solution)/shard_map/while/body/eval_jaxpr/njar,njrs->njas/dot_general | solution.py:17
  231.5 20.6 %gather.31 = bf16[512,2,64,8]{3,2,1,0:T(8,128)(2,1)} reshape(bf16[1024,512]{1,0:T(8,128)(2,1)S(1)} %gather_fusion.2) | data formatting | bytes 2097152 | tf_op jit(solution)/shard_map/while/body/eval_jaxpr/jit(_take)/gather | solution.py:19
  264.3 15.6 %gather_fusion = bf16[1024,64,128]{2,1,0:T(8,128)(2,1)} fusion(bf16[250,64,128]{2,1,0:T(8,128)(2,1)} %get-tuple-element.152, s32[1024]{0:T(1024)S(1)} %broadcast_clamp_fusion.6), kind=kCustom, calls=%fused_computation.1.clone.1 | custom fusion | bytes 33558528 | tf_op jit(solution)/shard_map/while/body/eval_jaxpr/jit(_take)/gather | solution.py:16
  286.3 10.3 %fusion.32 = bf16[512,2,8,128]{3,2,1,0:T(8,128)(2,1)} fusion(bf16[512,2,64,128]{3,2,1,0:T(8,128)(2,1)} %bitcast.87, pred[512,2]{1,0:T(8,128)(4,1)S(1)} %get-tuple-element.129, bf16[512,2,8,64]{3,2,1,0:T(8,128)(2,1)} %gather.30, pred[512,2]{1,0:T(8,128)(4,1)S(1)} %get-tuple-element.131), kind=kOutput, calls=%fused_computation.14.clone.1 | convolution fusion | flops 144179200 | bytes 19924992 | tf_op jit(solution)/shard_map/while/body/eval_jaxpr/njar,njrs->njas/dot_general | solution.py:17
  310.5 20.6 %gather.31 = bf16[512,2,64,8]{3,2,1,0:T(8,128)(2,1)} reshape(bf16[1024,512]{1,0:T(8,128)(2,1)S(1)} %gather_fusion.2) | data formatting | bytes 2097152 | tf_op jit(solution)/shard_map/while/body/eval_jaxpr/jit(_take)/gather | solution.py:19
  343.3 15.6 %gather_fusion = bf16[1024,64,128]{2,1,0:T(8,128)(2,1)} fusion(bf16[250,64,128]{2,1,0:T(8,128)(2,1)} %get-tuple-element.152, s32[1024]{0:T(1024)S(1)} %broadcast_clamp_fusion.6), kind=kCustom, calls=%fused_computation.1.clone.1 | custom fusion | bytes 33558528 | tf_op jit(solution)/shard_map/while/body/eval_jaxpr/jit(_take)/gather | solution.py:16
  365.4 10.3 %fusion.32 = bf16[512,2,8,128]{3,2,1,0:T(8,128)(2,1)} fusion(bf16[512,2,64,128]{3,2,1,0:T(8,128)(2,1)} %bitcast.87, pred[512,2]{1,0:T(8,128)(4,1)S(1)} %get-tuple-element.129, bf16[512,2,8,64]{3,2,1,0:T(8,128)(2,1)} %gather.30, pred[512,2]{1,0:T(8,128)(4,1)S(1)} %get-tuple-element.131), kind=kOutput, calls=%fused_computation.14.clone.1 | convolution fusion | flops 144179200 | bytes 19924992 | tf_op jit(solution)/shard_map/while/body/eval_jaxpr/njar,njrs->njas/dot_general | solution.py:17
  389.6 20.6 %gather.31 = bf16[512,2,64,8]{3,2,1,0:T(8,128)(2,1)} reshape(bf16[1024,512]{1,0:T(8,128)(2,1)S(1)} %gather_fusion.2) | data formatting | bytes 2097152 | tf_op jit(solution)/shard_map/while/body/eval_jaxpr/jit(_take)/gather | solution.py:19
  422.4 15.6 %gather_fusion = bf16[1024,64,128]{2,1,0:T(8,128)(2,1)} fusion(bf16[250,64,128]{2,1,0:T(8,128)(2,1)} %get-tuple-element.152, s32[1024]{0:T(1024)S(1)} %broadcast_clamp_fusion.6), kind=kCustom, calls=%fused_computation.1.clone.1 | custom fusion | bytes 33558528 | tf_op jit(solution)/shard_map/while/body/eval_jaxpr/jit(_take)/gather | solution.py:16
  468.6 20.6 %gather.31 = bf16[512,2,64,8]{3,2,1,0:T(8,128)(2,1)} reshape(bf16[1024,512]{1,0:T(8,128)(2,1)S(1)} %gather_fusion.2) | data formatting | bytes 2097152 | tf_op jit(solution)/shard_map/while/body/eval_jaxpr/jit(_take)/gather | solution.py:19
  501.4 15.6 %gather_fusion = bf16[1024,64,128]{2,1,0:T(8,128)(2,1)} fusion(bf16[250,64,128]{2,1,0:T(8,128)(2,1)} %get-tuple-element.152, s32[1024]{0:T(1024)S(1)} %broadcast_clamp_fusion.6), kind=kCustom, calls=%fused_computation.1.clone.1 | custom fusion | bytes 33558528 | tf_op jit(solution)/shard_map/while/body/eval_jaxpr/jit(_take)/gather | solution.py:16
  547.7 20.6 %gather.31 = bf16[512,2,64,8]{3,2,1,0:T(8,128)(2,1)} reshape(bf16[1024,512]{1,0:T(8,128)(2,1)S(1)} %gather_fusion.2) | data formatting | bytes 2097152 | tf_op jit(solution)/shard_map/while/body/eval_jaxpr/jit(_take)/gather | solution.py:19
  580.5 15.6 %gather_fusion = bf16[1024,64,128]{2,1,0:T(8,128)(2,1)} fusion(bf16[250,64,128]{2,1,0:T(8,128)(2,1)} %get-tuple-element.152, s32[1024]{0:T(1024)S(1)} %broadcast_clamp_fusion.6), kind=kCustom, calls=%fused_computation.1.clone.1 | custom fusion | bytes 33558528 | tf_op jit(solution)/shard_map/while/body/eval_jaxpr/jit(_take)/gather | solution.py:16
  626.7 20.6 %gather.31 = bf16[512,2,64,8]{3,2,1,0:T(8,128)(2,1)} reshape(bf16[1024,512]{1,0:T(8,128)(2,1)S(1)} %gather_fusion.2) | data formatting | bytes 2097152 | tf_op jit(solution)/shard_map/while/body/eval_jaxpr/jit(_take)/gather | solution.py:19
  658.9 11.9 %copy.57 = bf16[1024,4096]{1,0:T(8,128)(2,1)} copy(bf16[1024,4096]{0,1:T(8,128)(2,1)} %bitcast.93) | data formatting | bytes 16777216 | tf_op jit(solution)/shard_map/dot_general | solution.py:51
  680.2 20.1 %all_to_all.20 = bf16[32,2,8192]{2,1,0:T(2,128)(2,1)S(1)} all-to-all(bf16[32,2,8192]{2,1,0:T(2,128)(2,1)S(1)} %reshape.178), channel_id=1, replica_groups=mesh['dp'=4,'table'=32] {'table'}, dimensions={0} | all-to-all | bytes 2097152 | tf_op jit(solution)/shard_map/all_to_all | solution.py:57
  (197 shorter events, 321.2 us)
Async XLA Ops:
  9.6 16.3 %all-to-all-start = ((s32[32,6,128]{2,1,0:T(8,128)}), s32[32,6,128]{2,1,0:T(8,128)S(1)}, u32[]{:S(2)}, u32[]{:S(2)}) async-start(s32[32,6,128]{2,1,0:T(8,128)} %pad_add_fusion), calls=%async_computation | async-start | bytes 262144 | tf_op jit(solution)/shard_map/all_to_all | solution.py:39
  18.2 640.8 %all-gather.2.cloned.1.call-start = ((), (), s32[]{:S(2)}) async-start(), calls=%async_computation.3 | async-start | bytes 8650752 | tf_op jit(solution)/shard_map/all_gather | solution.py:32
  18.9 684.6 %reduce-scatter.2.cloned.1.call-start = ((), (), s32[]{:S(2)}) async-start(), calls=%async_computation.4 | async-start | bytes 655360 | tf_op jit(solution)/shard_map/reduce_scatter | solution.py:55
  59.5 9.9 %copy-start = (bf16[250,512]{1,0:T(8,128)(2,1)S(1)}, bf16[250,512]{1,0:T(8,128)(2,1)}, u32[]{:S(2)}) copy-start(bf16[250,512]{1,0:T(8,128)(2,1)} %get-tuple-element.153) | copy-start | bytes 768004 | tf_op jit(solution)/shard_map/while
  138.6 9.9 %copy-start = (bf16[250,512]{1,0:T(8,128)(2,1)S(1)}, bf16[250,512]{1,0:T(8,128)(2,1)}, u32[]{:S(2)}) copy-start(bf16[250,512]{1,0:T(8,128)(2,1)} %get-tuple-element.153) | copy-start | bytes 768004 | tf_op jit(solution)/shard_map/while
  217.6 9.9 %copy-start = (bf16[250,512]{1,0:T(8,128)(2,1)S(1)}, bf16[250,512]{1,0:T(8,128)(2,1)}, u32[]{:S(2)}) copy-start(bf16[250,512]{1,0:T(8,128)(2,1)} %get-tuple-element.153) | copy-start | bytes 768004 | tf_op jit(solution)/shard_map/while
  296.7 9.9 %copy-start = (bf16[250,512]{1,0:T(8,128)(2,1)S(1)}, bf16[250,512]{1,0:T(8,128)(2,1)}, u32[]{:S(2)}) copy-start(bf16[250,512]{1,0:T(8,128)(2,1)} %get-tuple-element.153) | copy-start | bytes 768004 | tf_op jit(solution)/shard_map/while
  375.7 9.9 %copy-start = (bf16[250,512]{1,0:T(8,128)(2,1)S(1)}, bf16[250,512]{1,0:T(8,128)(2,1)}, u32[]{:S(2)}) copy-start(bf16[250,512]{1,0:T(8,128)(2,1)} %get-tuple-element.153) | copy-start | bytes 768004 | tf_op jit(solution)/shard_map/while
  454.8 9.9 %copy-start = (bf16[250,512]{1,0:T(8,128)(2,1)S(1)}, bf16[250,512]{1,0:T(8,128)(2,1)}, u32[]{:S(2)}) copy-start(bf16[250,512]{1,0:T(8,128)(2,1)} %get-tuple-element.153) | copy-start | bytes 768004 | tf_op jit(solution)/shard_map/while
  533.8 9.9 %copy-start = (bf16[250,512]{1,0:T(8,128)(2,1)S(1)}, bf16[250,512]{1,0:T(8,128)(2,1)}, u32[]{:S(2)}) copy-start(bf16[250,512]{1,0:T(8,128)(2,1)} %get-tuple-element.153) | copy-start | bytes 768004 | tf_op jit(solution)/shard_map/while
  612.9 9.9 %copy-start = (bf16[250,512]{1,0:T(8,128)(2,1)S(1)}, bf16[250,512]{1,0:T(8,128)(2,1)}, u32[]{:S(2)}) copy-start(bf16[250,512]{1,0:T(8,128)(2,1)} %get-tuple-element.153) | copy-start | bytes 768004 | tf_op jit(solution)/shard_map/while
  658.9 11.9 %copy-start.1 = (bf16[8,512,128]{2,1,0:T(8,128)(2,1)S(1)}, bf16[8,512,128]{2,1,0:T(8,128)(2,1)}, u32[]{:S(2)}) copy-start(bf16[8,512,128]{2,1,0:T(8,128)(2,1)} %get-tuple-element.34) | copy-start | bytes 3145732
Sparse Core Ops, SparseCore 0:
  21.3 55.1 all-gather.1
  678.1 17.8 reduce-scatter.1

commit v2 on v1

v2 whole, which is shorter than its diff:
```python
import functools

import jax
import jax.numpy as jnp
from jax import lax
from jax.experimental import pallas as pl
from jax.experimental.pallas import tpu as pltpu
from jax.sharding import PartitionSpec as P

D1 = 8
D2 = 2
D3 = 8
RANK = 64
BAG = 2
GROUP = 16


def rows_kernel(ids_ref, first_ref, middle_ref, last_ref, out_ref):
    f32 = jnp.float32
    bf16 = jnp.bfloat16
    own = out_ref.shape[0]
    row16 = lax.broadcasted_iota(jnp.int32, (16, 128), 0)
    lane16 = lax.broadcasted_iota(jnp.int32, (16, 128), 1)
    keep = ((row16 < 8) == (lane16 < 64)).astype(bf16)
    zero = jnp.zeros((16, 128), bf16)
    block = lax.broadcasted_iota(jnp.int32, (8, 128), 1) // 16
    sub = lax.broadcasted_iota(jnp.int32, (8, 128), 0)

    def group(g, carry):
        base = g * GROUP
        prefixes, tails = [], [[], []]
        for k in range(0, GROUP, 2):
            heads, centres = [], []
            for j in range(BAG):
                n0, n1 = base + k, base + k + 1
                pair = [first_ref[ids_ref[j, n0]], first_ref[ids_ref[j, n1]]]
                heads.append(jnp.concatenate(pair, axis=0).astype(bf16) * keep)
                centres += [middle_ref[ids_ref[2 + j, n0]], middle_ref[ids_ref[2 + j, n1]]]
                tails[j] += [last_ref[ids_ref[4 + j, n0]], last_ref[ids_ref[4 + j, n1]]]
            left = jnp.concatenate(
                [
                    jnp.concatenate([heads[0], zero], axis=1),
                    jnp.concatenate([zero, heads[1]], axis=1),
                ],
                axis=0,
            )
            product = jnp.dot(left, jnp.concatenate(centres, axis=0), preferred_element_type=f32)
            prefixes.append(jnp.concatenate([product[:16], product[16:]], axis=1).astype(bf16))
        prefix = jnp.concatenate(prefixes, axis=0)
        tail = jnp.concatenate([jnp.concatenate(t, axis=0) for t in tails], axis=1)
        product = lax.dot_general(prefix, tail, (((1,), (1,)), ((), ())), preferred_element_type=f32)
        finished = []
        for h in range(GROUP // 8):
            part = product[h * 64 : h * 64 + 64, h * 128 : h * 128 + 128]
            mixed = part[:8]
            for n in range(1, 8):
                mixed = jnp.where(block == n, part[n * 8 : n * 8 + 8], mixed)
            for k in (1, 2, 4):
                up = pltpu.roll(pltpu.roll(mixed, 8 - k, 0), 16 * k, 1)
                down = pltpu.roll(pltpu.roll(mixed, k, 0), 128 - 16 * k, 1)
                high = (block & k) != 0
                same = ((sub & k) != 0) == high
                mixed = jnp.where(same, mixed, jnp.where(high, up, down))
            finished.append(mixed)
        row = pl.multiple_of(base, GROUP)
        out_ref[pl.ds(row, GROUP), :] = jnp.concatenate(finished, axis=0).astype(bf16)
        return carry

    lax.fori_loop(0, own // GROUP, group, 0, unroll=True)


def table_rows(got, first, middle, last):
    senders, words, own = got.shape
    ncore = first.shape[0]
    width = D1 * D2 * D3
    head = first.reshape(ncore, D1, RANK).astype(jnp.float32)
    head = jnp.pad(jnp.concatenate([head, head], axis=2), ((0, 8), (0, 0), (0, 0)))
    tail = last.reshape(ncore, RANK, D3).transpose(0, 2, 1)
    blank = jnp.zeros_like(tail)
    tail = jnp.concatenate(
        [jnp.concatenate([tail, blank], axis=2), jnp.concatenate([blank, tail], axis=2)], axis=1
    )

    def whole(x):
        return pl.BlockSpec(x.shape, lambda i: (0,) * x.ndim, pipeline_mode=pl.Buffered(1))

    lookups = senders * own * BAG
    return pl.pallas_call(
        rows_kernel,
        out_shape=jax.ShapeDtypeStruct((senders, own, width), jnp.bfloat16),
        grid=(senders,),
        in_specs=[
            pl.BlockSpec((None, words, own), lambda i: (i, 0, 0), memory_space=pltpu.SMEM),
            whole(head),
            whole(middle),
            whole(tail),
        ],
        out_specs=pl.BlockSpec((None, own, width), lambda i: (i, 0, 0)),
        compiler_params=pltpu.CompilerParams(vmem_limit_bytes=48 << 20),
        cost_estimate=pl.CostEstimate(
            flops=lookups * 4096 * 128, bytes_accessed=8 << 20, transcendentals=0
        ),
    )(got, head, middle, tail)


def product_kernel(rows_ref, grad_ref, out_ref):
    @pl.when(pl.program_id(0) == 0)
    def _():
        out_ref[...] = jnp.zeros_like(out_ref)

    parts, _, columns = out_ref.shape
    rows = rows_ref[...]
    for d in range(parts):
        out_ref[d] += lax.dot_general(
            rows,
            grad_ref[:, d * columns : (d + 1) * columns],
            (((0,), (0,)), ((), ())),
            preferred_element_type=jnp.float32,
        )


def partial_product(rows, grad, parts):
    samples, width = rows.shape
    hidden_units = grad.shape[1]
    step = min(samples, 512)
    shape = (parts, width, hidden_units // parts)
    return pl.pallas_call(
        product_kernel,
        out_shape=jax.ShapeDtypeStruct(shape, jnp.float32),
        grid=(samples // step,),
        in_specs=[
            pl.BlockSpec((step, width), lambda i: (i, 0)),
            pl.BlockSpec((step, hidden_units), lambda i: (i, 0)),
        ],
        out_specs=pl.BlockSpec(shape, lambda i: (0, 0, 0)),
        cost_estimate=pl.CostEstimate(
            flops=2 * samples * width * hidden_units,
            bytes_accessed=2 * samples * (width + hidden_units),
            transcendentals=0,
        ),
    )(rows, grad)


def body(core_ids, bag_lengths, first_core, middle_core, last_core, grad_hidden):
    width = D1 * D2 * D3
    own, tables = bag_lengths.shape
    ncore = first_core.shape[1]
    n_data = lax.axis_size("dp")

    gathered = lax.all_gather(grad_hidden, "table", axis=0, tiled=True)

    ids = jnp.transpose(core_ids, (1, 2, 3, 0))
    lengths = jnp.transpose(bag_lengths)
    live = jnp.arange(BAG, dtype=jnp.int32)[None, :, None] < lengths[:, None, :]
    heads = jnp.where(live, ids[:, 0], ncore)
    sent = jnp.concatenate([heads, ids[:, 1], ids[:, 2]], axis=1)
    got = lax.all_to_all(sent, "table", split_axis=0, concat_axis=0, tiled=True)

    rows = table_rows(got, first_core[0], middle_core[0], last_core[0])

    partial = partial_product(rows.reshape(tables * own, width), gathered, n_data)
    weight_grad = lax.psum_scatter(partial, "dp", scatter_dimension=0, tiled=False)

    returned = lax.all_to_all(rows, "table", split_axis=0, concat_axis=0, tiled=True)
    pooled = jnp.transpose(returned, (1, 0, 2)).reshape(own, tables * width)
    return (pooled, weight_grad)


def solution(mesh):
    placed = (
        P(("dp", "table"), None, None, None),
        P(("dp", "table"), None),
        P("table", None, None),
        P("table", None, None, None),
        P("table", None, None),
        P(("dp", "table"), None),
    )
    return jax.shard_map(
        body,
        mesh=mesh,
        in_specs=placed,
        out_specs=(P(("dp", "table"), None), P("table", "dp")),
        check_vma=False,
    )
```

time: 712 us -> 118 us (0.17)
  local copies, waits for them, and re-layouts: 485 us -> 5.84 us
  matrix products: 170 us -> 0 us
  Pallas kernels: 0 us -> 61 us
    gather x40 -> x0, local copies, waits for them, and re-layouts: 370 us -> none  [the longest x16 197 us: build_rows(): tail = jnp.take(last, wanted[:, 2, :], axis=0).reshape(block, BAG, RANK, D3)]
    dot_general x17 -> x0, matrix products: 170 us -> none  [the longest x8 83.4 us: build_rows(): jnp.einsum('njar,njrs->njas', head, centre, preferred_element_type=jnp.fl...]
    pallas_call x0 -> x2, Pallas kernels: none -> 61 us  [the longest x1 52.9 us: table_rows(): pl.pallas_call(rows_kernel, out_shape=jax.ShapeDtypeStruct((senders, own,...]
    reshape x9 -> x0, local copies, waits for them, and re-layouts: 53.2 us -> none  [the longest x8 53.2 us: build_rows(): prefix = prefix.astype(jnp.bfloat16).reshape(block, BAG, D1 * D2, RANK)]
    convert_element_type x16 -> x1, local copies, waits for them, and re-layouts: 31.1 us -> 0.33 us  [table_rows(): head = first.reshape(ncore, D1, RANK).astype(jnp.float32)]
    dot_general x1 -> x0, local copies, waits for them, and re-layouts: 11.9 us -> none  [body(): lax.dot_general(rows, gathered, (((0,), (0,)), ((), ())), preferred_eleme...]
  transfers between devices with their start and end apart: 3 -> 3, of which waited for: 1 -> 1; matrix products, arithmetic and copies ran while one was open for 90% -> 6% of each run, Pallas kernels for 0% -> 45%
where the time goes in v2:
time: 118 us
  Pallas kernels  61 us (52%)
  blocking collectives  20.6 us (17%)
  between operations  14.1 us (12%)
  starting transfers between devices  8.67 us (7%)
  local copies, waits for them, and re-layouts  5.84 us (5%)
  waiting for transfers between devices  5.82 us (5%)
  other arithmetic  1.97 us (2%)
    pallas_call x1, Pallas kernels, table_rows(): pl.pallas_call(rows_kernel, out_shape=jax.ShapeDtypeStruct((senders, own,...  52.9 us
    all_to_all x1, blocking collectives, body(): lax.all_to_all(rows, 'table', split_axis=0, concat_axis=0, tiled=True)  20.6 us
    all_to_all x1, starting transfers between devices, body(): got = lax.all_to_all(sent, 'table', split_axis=0, concat_axis=0, tiled=True)  8.59 us
    pallas_call x1, Pallas kernels, partial_product(): pl.pallas_call(product_kernel, out_shape=jax.ShapeDtypeStruct(shape, jnp....  8.05 us
    all_to_all x1, waiting for transfers between devices, body(): got = lax.all_to_all(sent, 'table', split_axis=0, concat_axis=0, tiled=True)  5.12 us
    unnamed x10, local copies, waits for them, and re-layouts  4.44 us
  transfers between devices with their start and end apart: 3, of which 1 were waited for; matrix products, arithmetic and copies ran while one was open for 6% of the time, Pallas kernels for 45%

profile of v2, /device:TPU:1, one launch (start us, length us, event | category | flops | bytes accessed | tf_op | source)
XLA Modules:
  0.0 118.0 jit_solution(14238186975125254404)
XLA Ops:
  7.2 0.0 copy-start.2
  7.2 0.0 all-gather.2.cloned.1.call-start
  7.2 0.7 all-gather.2.cloned.1.call-update
  7.9 0.9 copy.18
  8.8 0.7 compare_select_fusion
  9.6 0.7 pad_add_fusion
  10.3 8.6 %all-to-all-start = ((s32[32,6,128]{2,1,0:T(8,128)}), s32[32,6,128]{2,1,0:T(8,128)S(1)}, u32[]{:S(2)}, u32[]{:S(2)}) async-start(s32[32,6,128]{2,1,0:T(8,128)} %pad_add_fusion), calls=%async_computation | async-start | bytes 262144 | tf_op jit(solution)/shard_map/all_to_all | solution.py:157
  18.9 0.0 reduce-scatter.2.cloned.1.call-start
  18.9 1.1 copy.10
  20.0 0.3 copy.11
  20.4 0.0 copy-done.2
  20.4 0.1 copy.13
  20.5 0.4 copy.14
  20.9 0.3 fusion.6.first_ref
  21.2 0.3 fusion.4.last_ref
  21.5 5.1 %all-to-all-done.ids_ref = s32[32,6,128]{2,1,0:T(8,128)S(1)} async-done(((s32[32,6,128]{2,1,0:T(8,128)}), s32[32,6,128]{2,1,0:T(8,128)S(1)}, u32[]{:S(2)}, u32[]{:S(2)}) %all-to-all-start) | async-done | bytes 98336 | tf_op jit(solution)/shard_map/all_to_all | solution.py:157
  26.6 52.9 %shard_map.77 = bf16[32,128,128]{2,1,0:T(8,128)(2,1)S(1)} custom-call(s32[32,6,128]{2,1,0:T(8,128)S(1)} %all-to-all-done.ids_ref, f32[258,8,128]{2,1,0:T(8,128)S(1)} %fusion.6.first_ref, bf16[250,64,128]{2,1,0:T(8,128)(2,1)} %bitcast.29, bf16[250,16,128]{2,1,0:T(8,128)(2,1)S(1)} %fusion.4.last_ref), custom_call_target="tpu_custom_call" | custom-call | flops 4294967296 | bytes 8388608 | tf_op jit(solution)/shard_map/pallas_call | solution.py:88
  79.5 1.0 copy-done
  80.5 8.0 %shard_map.78 = f32[4,128,256]{2,1,0:T(8,128)} custom-call(bf16[4096,128]{1,0:T(8,128)(2,1)} %bitcast.20, bf16[4096,1024]{1,0:T(8,128)(2,1)} %all-gather.2.cloned.1.call-done.grad_ref), custom_call_target="tpu_custom_call" | custom-call | flops 1073741824 | bytes 9437184 | tf_op jit(solution)/shard_map/pallas_call | solution.py:127
  88.5 0.0 reduce-scatter.2.cloned.1.call-update
  88.6 0.0 copy-done.1
  88.6 20.6 %all_to_all.10 = bf16[32,128,128]{2,1,0:T(8,128)(2,1)S(1)} all-to-all(bf16[32,128,128]{2,1,0:T(8,128)(2,1)S(1)} %copy-done.1), channel_id=1, replica_groups=mesh['dp'=4,'table'=32] {'table'}, dimensions={0} | all-to-all | bytes 2097152 | tf_op jit(solution)/shard_map/all_to_all | solution.py:164
  109.2 0.7 copy.15
  109.9 1.3 %copy.16 = bf16[128,4096]{1,0:T(8,128)(2,1)} copy(bf16[128,4096]{0,1:T(8,128)(2,1)S(1)} %bitcast.22) | data formatting | bytes 2097152
  (5 shorter events, 0.0 us)
Async XLA Ops:
  7.2 13.2 %copy-start.2 = (bf16[1,250,512]{2,1,0:T(8,128)(2,1)S(1)}, bf16[1,250,512]{2,1,0:T(8,128)(2,1)}, u32[]{:S(2)}) copy-start(bf16[1,250,512]{2,1,0:T(8,128)(2,1)} %param.10) | copy-start | bytes 768004
  7.2 73.3 %all-gather.2.cloned.1.call-start = ((), (), s32[]{:S(2)}) async-start(), calls=%async_computation.3 | async-start | bytes 8650752 | tf_op jit(solution)/shard_map/all_gather | solution.py:150
  10.3 16.3 %all-to-all-start = ((s32[32,6,128]{2,1,0:T(8,128)}), s32[32,6,128]{2,1,0:T(8,128)S(1)}, u32[]{:S(2)}, u32[]{:S(2)}) async-start(s32[32,6,128]{2,1,0:T(8,128)} %pad_add_fusion), calls=%async_computation | async-start | bytes 262144 | tf_op jit(solution)/shard_map/all_to_all | solution.py:157
  18.9 92.3 %reduce-scatter.2.cloned.1.call-start = ((), (), s32[]{:S(2)}) async-start(), calls=%async_computation.4 | async-start | bytes 655360 | tf_op jit(solution)/shard_map/reduce_scatter | solution.py:162
  79.5 1.0 copy-start
  80.5 8.1 %copy-start.1 = (bf16[32,128,128]{2,1,0:T(8,128)(2,1)S(1)}, bf16[32,128,128]{2,1,0:T(8,128)(2,1)}, u32[]{:S(2)}) copy-start(bf16[32,128,128]{2,1,0:T(8,128)(2,1)} %copy-done) | copy-start | bytes 3145732
Sparse Core Ops, SparseCore 0:
  10.3 56.5 all-gather.1
  88.7 18.5 reduce-scatter.1

commit v3 on v1

v3 whole, which is shorter than its diff:
```python
import functools

import jax
import jax.numpy as jnp
from jax import lax
from jax.experimental import pallas as pl
from jax.experimental.pallas import tpu as pltpu
from jax.sharding import Mesh
from jax.sharding import PartitionSpec as P

D1 = 8
D2 = 2
D3 = 8
RANK = 64
BAG = 2
WIDTH = D1 * D2 * D3
BLOCK = 128
SPLIT = (64, 32, 32)
NX = 4
NY = 4
NCORES = 2
TABLE = ("x", "y", "core")
EVERY = ("dp", "x", "y", "core")


def rows_kernel(ids_ref, first_ref, middle_ref, last_ref, out_ref, prefix_ref, mixed_ref, *, offset):
    f32 = jnp.float32
    bf16 = jnp.bfloat16
    senders, part, _ = out_ref.shape
    per_block = BLOCK // part
    blocks = senders // per_block
    groups = BLOCK // 8
    row16 = lax.broadcasted_iota(jnp.int32, (16, 128), 0)
    lane16 = lax.broadcasted_iota(jnp.int32, (16, 128), 1)
    keep = ((row16 < 8) == (lane16 < 64)).astype(bf16)
    zero = jnp.zeros((16, 128), bf16)
    lane = lax.broadcasted_iota(jnp.int32, (8, 128), 1) // 16

    def index(i, word, sample):
        return ids_ref[i * per_block + sample // part, word, offset + sample % part]

    def prefixes(i, g):
        for n in range(0, 8, 2):
            pair = (n * groups + g, (n + 1) * groups + g)
            heads, centres = [], []
            for j in range(BAG):
                two = [first_ref[index(i, j, a)] for a in pair]
                heads.append(jnp.concatenate(two, axis=0).astype(bf16) * keep)
                centres += [middle_ref[index(i, 2 + j, a)] for a in pair]
            left = jnp.concatenate(
                [
                    jnp.concatenate([heads[0], zero], axis=1),
                    jnp.concatenate([zero, heads[1]], axis=1),
                ],
                axis=0,
            )
            product = jnp.dot(left, jnp.concatenate(centres, axis=0), preferred_element_type=f32)
            product = product.astype(bf16)
            at = g * 64 + n * 8
            prefix_ref[at : at + 16, :128] = product[:16]
            prefix_ref[at : at + 16, 128:] = product[16:]

    def contract(i, g):
        tails = [
            jnp.concatenate(
                [last_ref[index(i, 4 + j, n * groups + e)] for e in (g, g + 1) for n in range(8)],
                axis=0,
            )
            for j in range(BAG)
        ]
        product = lax.dot_general(
            prefix_ref[g * 64 : g * 64 + 128, :],
            jnp.concatenate(tails, axis=1),
            (((1,), (1,)), ((), ())),
            preferred_element_type=f32,
        )
        for e in range(2):
            own = product[e * 64 : e * 64 + 64, e * 128 : e * 128 + 128]
            mixed = own[:8]
            for n in range(1, 8):
                mixed = jnp.where(lane == n, own[n * 8 : n * 8 + 8], mixed)
            mixed_ref[(g + e) * 8 : (g + e) * 8 + 8, :] = mixed

    def arrange(i, h):
        parts = [mixed_ref[pl.ds(h * 8 + a, 8, stride=8), :] for a in range(8)]
        for k in (1, 2, 4):
            low = (lane & k) == 0
            moved = list(parts)
            for a in range(8):
                if a & k == 0:
                    p, q = parts[a], parts[a + k]
                    moved[a] = jnp.where(low, p, pltpu.roll(q, 16 * k, 1))
                    moved[a + k] = jnp.where(low, pltpu.roll(p, 128 - 16 * k, 1), q)
            parts = moved
        for n in range(8):
            at = n * groups + h
            out_ref[i * per_block + at // part, at % part : at % part + 8, :] = parts[n].astype(bf16)

    def step(i, carry):
        now = jnp.minimum(i, blocks - 1)
        before = jnp.clip(i - 1, 0, blocks - 1)
        earlier = jnp.clip(i - 2, 0, blocks - 1)
        for h in range(0, groups, 8):
            arrange(earlier, h)
        for g in range(0, groups, 2):
            contract(before, g)
            prefixes(now, g)
            prefixes(now, g + 1)
        return carry

    lax.fori_loop(0, blocks + 2, step, 0)


def table_rows(got, head, middle, tail, offset, part):
    senders = got.shape[0]
    lookups = senders * part * BAG
    vmem = pl.BlockSpec(memory_space=pltpu.VMEM)
    return pl.pallas_call(
        functools.partial(rows_kernel, offset=offset),
        out_shape=jax.ShapeDtypeStruct((senders, part, WIDTH), jnp.bfloat16),
        in_specs=[pl.BlockSpec(memory_space=pltpu.SMEM), vmem, vmem, vmem],
        out_specs=vmem,
        scratch_shapes=[
            pltpu.VMEM((BLOCK * 8, 256), jnp.bfloat16),
            pltpu.VMEM((BLOCK, 128), jnp.float32),
        ],
        compiler_params=pltpu.CompilerParams(vmem_limit_bytes=32 << 20),
        cost_estimate=pl.CostEstimate(
            flops=lookups * 2000000, bytes_accessed=6 << 20, transcendentals=0
        ),
    )(got, head, middle, tail)


def product_kernel(place_ref, *refs):
    rows_refs = refs[: len(SPLIT)]
    left_refs = refs[len(SPLIT) : len(SPLIT) + NCORES * NY]
    right_refs = refs[len(SPLIT) + NCORES * NY : len(SPLIT) + NCORES * (NX + NY)]
    own_ref, out_refs, total_ref = refs[-5], refs[-4:-1], refs[-1]
    me, x, y, core = place_ref[0], place_ref[1], place_ref[2], place_ref[3]
    half = left_refs[0].shape[2]

    def rows_from(sx, sy, sc):
        sender = (sx * NY + sy) * NCORES + sc
        return [ref[sender] for ref in rows_refs]

    def add(value, first, columns):
        if first:
            total_ref[:, columns] = value
        else:
            total_ref[:, columns] += value

    for c in range(NCORES):
        sc = (core + c) % NCORES
        for m in range(NY):
            for refs_of, columns, turn in (
                (left_refs, slice(0, half), False),
                (right_refs, slice(half, 2 * half), True),
            ):
                rows = []
                for k in range(NX):
                    a, b = (m, k) if turn else (k, m)
                    rows += rows_from((x - a + NX) % NX, (y - b + NY) % NY, sc)
                rows = jnp.concatenate(rows, axis=0)
                grad = refs_of[c * NY + m][...]
                grad = grad.reshape(grad.shape[0] * grad.shape[1], half)
                value = lax.dot_general(
                    rows, grad, (((0,), (0,)), ((), ())), preferred_element_type=jnp.float32
                )
                add(value, c == 0 and m == 0, columns)

    columns = own_ref.shape[1]

    def block(k):
        at = pl.multiple_of(((me + k) % 4) * columns, columns)
        return total_ref[:, pl.ds(at, columns)]

    own_ref[...] = block(0)
    for k in range(3):
        out_refs[k][...] = block(k + 1).astype(jnp.bfloat16)


def partial_product(rows, left, right, place):
    senders = rows[0].shape[0]
    columns = 2 * left[0].shape[2]
    quarter = columns // 4
    samples = senders * sum(SPLIT)
    vmem = pl.BlockSpec(memory_space=pltpu.VMEM)
    operands = [*rows, *left, *right]
    return pl.pallas_call(
        product_kernel,
        out_shape=[jax.ShapeDtypeStruct((WIDTH, quarter), jnp.float32)]
        + [jax.ShapeDtypeStruct((WIDTH, quarter), jnp.bfloat16)] * 3,
        in_specs=[pl.BlockSpec(memory_space=pltpu.SMEM)] + [vmem] * len(operands),
        out_specs=[vmem] * 4,
        scratch_shapes=[pltpu.VMEM((WIDTH, columns), jnp.float32)],
        compiler_params=pltpu.CompilerParams(vmem_limit_bytes=32 << 20),
        cost_estimate=pl.CostEstimate(
            flops=2 * samples * WIDTH * columns,
            bytes_accessed=2 * samples * (WIDTH + columns),
            transcendentals=0,
        ),
    )(place, *operands)


def around(axis, size, value):
    out = [value]
    for k in range(1, size):
        out.append(lax.ppermute(value, axis, [(i, (i + k) % size) for i in range(size)]))
    return out


def body(core_ids, bag_lengths, first_core, middle_core, last_core, grad_hidden):
    own, tables = bag_lengths.shape
    ncore = first_core.shape[1]
    half = grad_hidden.shape[1] // 2
    swap = [(0, 1), (1, 0)]

    left = around("x", NX, grad_hidden[:, :half])
    right = around("y", NY, grad_hidden[:, half:])

    ids = jnp.transpose(core_ids, (1, 2, 3, 0))
    lengths = jnp.transpose(bag_lengths)
    live = jnp.arange(BAG, dtype=jnp.int32)[None, :, None] < lengths[:, None, :]
    heads = jnp.where(live, ids[:, 0], ncore)
    sent = jnp.concatenate([heads, ids[:, 1], ids[:, 2]], axis=1)
    got = lax.all_to_all(sent, TABLE, split_axis=0, concat_axis=0, tiled=True)

    middle = middle_core[0]
    head = first_core[0].reshape(ncore, D1, RANK).astype(jnp.float32)
    head = jnp.pad(jnp.concatenate([head, head], axis=2), ((0, 8), (0, 0), (0, 0)))
    tail = last_core[0].reshape(ncore, RANK, D3).transpose(0, 2, 1)
    blank = jnp.zeros_like(tail)
    tail = jnp.concatenate(
        [jnp.concatenate([tail, blank], axis=2), jnp.concatenate([blank, tail], axis=2)], axis=1
    )

    left, right = jnp.stack(left), jnp.stack(right)
    got, left, right = lax.optimization_barrier((got, left, right))
    left = around("y", NY, left)
    right = around("x", NX, right)

    rows, returned = [], []
    offset = 0
    for number, part in enumerate(SPLIT):
        if number == len(SPLIT) - 1:
            got, left, right = lax.optimization_barrier((got, left, right))
            left = left + [lax.ppermute(v, "core", swap) for v in left]
            right = right + [lax.ppermute(v, "core", swap) for v in right]
        rows.append(table_rows(got, head, middle, tail, offset, part))
        returned.append(lax.all_to_all(rows[-1], TABLE, split_axis=0, concat_axis=0, tiled=True))
        offset += part

    me = lax.axis_index("dp")
    place = jnp.stack([me, lax.axis_index("x"), lax.axis_index("y"), lax.axis_index("core")])
    mine, *others = partial_product(rows, left, right, place.astype(jnp.int32))
    weight_grad = mine
    for k, other in enumerate(others):
        came = lax.ppermute(other, "dp", [(i, (i + k + 1) % 4) for i in range(4)])
        weight_grad = weight_grad + came.astype(jnp.float32)

    pooled = jnp.concatenate(
        [jnp.transpose(r, (1, 0, 2)).reshape(r.shape[1], tables * WIDTH) for r in returned], axis=0
    )
    return (pooled, weight_grad)


def solution(mesh):
    n_data = mesh.devices.shape[0]
    fine = Mesh(mesh.devices.reshape(n_data, NX, NY, NCORES), EVERY)
    placed = (
        P(EVERY, None, None, None),
        P(EVERY, None),
        P(TABLE, None, None),
        P(TABLE, None, None, None),
        P(TABLE, None, None),
        P(EVERY, None),
    )
    return jax.shard_map(
        body,
        mesh=fine,
        in_specs=placed,
        out_specs=(P(EVERY, None), P(TABLE, "dp")),
        check_vma=False,
    )
```

time: 712 us -> 154 us (0.22)
  local copies, waits for them, and re-layouts: 485 us -> 13.7 us
  matrix products: 170 us -> 0 us
  Pallas kernels: 0 us -> 56.5 us
  starting transfers between devices: 8.67 us -> 56.1 us
  blocking collectives: 20.1 us -> 0 us
  between operations: 14.1 us -> 0.89 us
  waiting for transfers between devices: 6.63 us -> 19.8 us
    gather x40 -> x0, local copies, waits for them, and re-layouts: 370 us -> none  [the longest x16 197 us: build_rows(): tail = jnp.take(last, wanted[:, 2, :], axis=0).reshape(block, BAG, RANK, D3)]
    dot_general x17 -> x0, matrix products: 170 us -> none  [the longest x8 83.4 us: build_rows(): jnp.einsum('njar,njrs->njas', head, centre, preferred_element_type=jnp.fl...]
    pallas_call x0 -> x4, Pallas kernels: none -> 56.5 us  [the longest x3 52.3 us: table_rows(): pl.pallas_call(functools.partial(rows_kernel, offset=offset), out_shape=j...]
    reshape x9 -> x3, local copies, waits for them, and re-layouts: 53.2 us -> 2.62 us  [body(): jnp.transpose(r, (1, 0, 2)).reshape(r.shape[1], tables * WIDTH)]
    convert_element_type x16 -> x1, local copies, waits for them, and re-layouts: 31.1 us -> 0.33 us  [body(): head = first_core[0].reshape(ncore, D1, RANK).astype(jnp.float32)]
    ppermute x0 -> x23, starting transfers between devices: none -> 27.5 us  [the longest x12 18 us: around(): lax.ppermute(value, axis, [(i, (i + k) % size) for i in range(size)])]
    all_to_all x1 -> x4, starting transfers between devices: 8.59 us -> 28.7 us  [the longest x3 20.5 us: body(): lax.all_to_all(rows[-1], TABLE, split_axis=0, concat_axis=0, tiled=True)]
    all_to_all x1 -> x0, blocking collectives: 20.1 us -> none  [body(): lax.all_to_all(rows.reshape(group_rows, 1, width), 'table', split_axis=0,...]
  transfers between devices with their start and end apart: 3 -> 27, of which waited for: 1 -> 6; matrix products, arithmetic and copies ran while one was open for 90% -> 7% of each run, Pallas kernels for 0% -> 34%
where the time goes in v3:
time: 154 us; the launch traced here: 153 us
  Pallas kernels  56.5 us (37%)
  starting transfers between devices  56.1 us (36%)
  waiting for transfers between devices  19.8 us (13%)
  local copies, waits for them, and re-layouts  13.7 us (9%)
  other arithmetic  5.92 us (4%)
    pallas_call x3, Pallas kernels, table_rows(): pl.pallas_call(functools.partial(rows_kernel, offset=offset), out_shape=j...  52.3 us
    all_to_all x3, starting transfers between devices, body(): lax.all_to_all(rows[-1], TABLE, split_axis=0, concat_axis=0, tiled=True)  20.5 us
    ppermute x12, starting transfers between devices, around(): lax.ppermute(value, axis, [(i, (i + k) % size) for i in range(size)])  18 us
    ppermute x12, waiting for transfers between devices, around(): lax.ppermute(value, axis, [(i, (i + k) % size) for i in range(size)])  9.35 us
    unnamed x15, local copies, waits for them, and re-layouts  8.63 us
    all_to_all x1, starting transfers between devices, body(): got = lax.all_to_all(sent, TABLE, split_axis=0, concat_axis=0, tiled=True)  8.19 us
    all_to_all x3, waiting for transfers between devices, body(): lax.all_to_all(rows[-1], TABLE, split_axis=0, concat_axis=0, tiled=True)  5.83 us
    ppermute x3, waiting for transfers between devices, body(): came = lax.ppermute(other, 'dp', [(i, (i + k + 1) % 4) for i in range(4)])  4.62 us
  transfers between devices with their start and end apart: 27, of which 6 were waited for; matrix products, arithmetic and copies ran while one was open for 7% of the time, Pallas kernels for 34%

profile of v3, /device:TPU:1, one launch (start us, length us, event | category | flops | bytes accessed | tf_op | source)
XLA Modules:
  0.0 152.9 jit_solution(10589336250555134545)
XLA Ops:
  0.6 1.7 %slice_bitcast_fusion.3 = (bf16[1,128,512]{2,1,0:T(8,128)(2,1)S(1)}, bf16[1,128,512]{2,1,0:T(8,128)(2,1)S(1)}, bf16[128,512]{1,0:T(8,128)(2,1)S(1)}, bf16[128,512]{1,0:T(8,128)(2,1)}) fusion(bf16[128,1024]{1,0:T(8,128)(2,1)} %param.11), kind=kLoop, calls=%fused_computation.24 | loop fusion | bytes 786432 | tf_op jit(solution)/shard_map/stack | solution.py:237
  2.3 3.3 %collective-permute-start.2 = (bf16[128,512]{1,0:T(8,128)(2,1)}, bf16[128,512]{1,0:T(8,128)(2,1)}, u32[]{:S(2)}, u32[]{:S(2)}) collective-permute-start(bf16[128,512]{1,0:T(8,128)(2,1)} %get-tuple-element.37), channel_id=1, source_target_pairs={{0,24},{8,0},{16,8},{24,16},{1,25},{9,1},{17,9},{25,17},{2,26},{10... | collective-permute-start | bytes 393224 | tf_op jit(solution)/shard_map/ppermute | solution.py:208
  6.7 2.7 %collective-permute-start.5 = (bf16[128,512]{1,0:T(8,128)(2,1)S(1)}, bf16[128,512]{1,0:T(8,128)(2,1)}, u32[]{:S(2)}, u32[]{:S(2)}) collective-permute-start(bf16[128,512]{1,0:T(8,128)(2,1)S(1)} %get-tuple-element.36), channel_id=1, source_target_pairs={{0,6},{2,0},{4,2},{6,4},{1,7},{3,1},{5,3},{7,5},{8,14},{10,8},{12,... | collective-permute-start | bytes 393224 | tf_op jit(solution)/shard_map/ppermute | solution.py:208
  12.2 8.2 %all-to-all-start = ((s32[32,6,128]{2,1,0:T(8,128)}), s32[32,6,128]{2,1,0:T(8,128)S(1)}, u32[]{:S(2)}, u32[]{:S(2)}) async-start(s32[32,6,128]{2,1,0:T(8,128)} %pad_add_fusion), calls=%async_computation | async-start | bytes 262144 | tf_op jit(solution)/shard_map/all_to_all | solution.py:226
  25.6 4.4 %collective-permute-done.3 = bf16[128,512]{1,0:T(8,128)(2,1)S(1)} collective-permute-done((bf16[128,512]{1,0:T(8,128)(2,1)S(1)}, bf16[128,512]{1,0:T(8,128)(2,1)S(1)}, u32[]{:S(2)}, u32[]{:S(2)}) %collective-permute-start.3) | collective-permute-done | bytes 131104 | tf_op jit(solution)/shard_map/ppermute | solution.py:208
  31.2 1.7 %collective-permute-start.7 = (bf16[4,128,512]{2,1,0:T(8,128)(2,1)S(1)}, bf16[4,128,512]{2,1,0:T(8,128)(2,1)}, u32[]{:S(2)}, u32[]{:S(2)}) collective-permute-start(bf16[4,128,512]{2,1,0:T(8,128)(2,1)S(1)} %pad_maximum_fusion.1.refs_3_), channel_id=1, source_target_pairs={{0,4},{2,6},{4,0},{6,2},{1,5},{3,7},{5,1},{7,3},{8,12},{10,14},{12... | collective-permute-start | bytes 1572872 | tf_op jit(solution)/shard_map/ppermute | solution.py:208
  35.0 2.5 %collective-permute-start.10 = (bf16[4,128,512]{2,1,0:T(8,128)(2,1)S(1)}, bf16[4,128,512]{2,1,0:T(8,128)(2,1)}, u32[]{:S(2)}, u32[]{:S(2)}) collective-permute-start(bf16[4,128,512]{2,1,0:T(8,128)(2,1)S(1)} %pad_maximum_fusion.2.refs_11_), channel_id=1, source_target_pairs={{0,16},{8,24},{16,0},{24,8},{1,17},{9,25},{17,1},{25,9},{2,18},{10... | collective-permute-start | bytes 1572872 | tf_op jit(solution)/shard_map/ppermute | solution.py:208
  37.5 2.2 %copy-done = bf16[1,250,64,128]{3,2,1,0:T(8,128)(2,1)S(1)} copy-done((bf16[1,250,64,128]{3,2,1,0:T(8,128)(2,1)S(1)}, bf16[1,250,64,128]{3,2,1,0:T(8,128)(2,1)}, u32[]{:S(2)}) %copy-start) | copy-done | bytes 4096024
  39.6 14.5 %shard_map.78.refs_1_ = bf16[32,32,128]{2,1,0:T(8,128)(2,1)} custom-call(s32[32,6,128]{2,1,0:T(8,128)S(1)} %all-to-all-done.ids_ref, f32[258,8,128]{2,1,0:T(8,128)S(1)} %fusion.6.first_ref, bf16[250,64,128]{2,1,0:T(8,128)(2,1)S(1)} %bitcast.48, bf16[250,16,128]{2,1,0:T(8,128)(2,1)S(1)} %fusion.4.last_ref), custom_call_target="tpu_custom_call" | custom-call | flops 4096000000 | bytes 6291456 | tf_op jit(solution)/shard_map/pallas_call | solution.py:118
  54.2 6.6 %all-to-all-start.2 = ((bf16[32,32,128]{2,1,0:T(8,128)(2,1)}), bf16[32,32,128]{2,1,0:T(8,128)(2,1)S(1)}, u32[]{:S(2)}, u32[]{:S(2)}) async-start(bf16[32,32,128]{2,1,0:T(8,128)(2,1)} %shard_map.78.refs_1_), calls=%async_computation.2 | async-start | bytes 524288 | tf_op jit(solution)/shard_map/all_to_all | solution.py:250
  60.8 2.2 %copy-done.1 = bf16[1,250,64,128]{3,2,1,0:T(8,128)(2,1)S(1)} copy-done((bf16[1,250,64,128]{3,2,1,0:T(8,128)(2,1)S(1)}, bf16[1,250,64,128]{3,2,1,0:T(8,128)(2,1)}, u32[]{:S(2)}) %copy-start.1) | copy-done | bytes 4096024
  63.0 23.3 %shard_map.77.refs_0_ = bf16[32,64,128]{2,1,0:T(8,128)(2,1)} custom-call(s32[32,6,128]{2,1,0:T(8,128)S(1)} %all-to-all-done.ids_ref, f32[258,8,128]{2,1,0:T(8,128)S(1)} %fusion.6.first_ref, bf16[250,64,128]{2,1,0:T(8,128)(2,1)S(1)} %bitcast.49, bf16[250,16,128]{2,1,0:T(8,128)(2,1)S(1)} %fusion.4.last_ref), custom_call_target="tpu_custom_call" | custom-call | flops 8192000000 | bytes 6291456 | tf_op jit(solution)/shard_map/pallas_call | solution.py:118
  86.3 2.6 %collective-permute-start.11 = (bf16[4,128,512]{2,1,0:T(8,128)(2,1)S(1)}, bf16[4,128,512]{2,1,0:T(8,128)(2,1)}, u32[]{:S(2)}, u32[]{:S(2)}) collective-permute-start(bf16[4,128,512]{2,1,0:T(8,128)(2,1)S(1)} %pad_maximum_fusion.2.refs_11_), channel_id=1, source_target_pairs={{0,24},{8,0},{16,8},{24,16},{1,25},{9,1},{17,9},{25,17},{2,26},{10... | collective-permute-start | bytes 1572872 | tf_op jit(solution)/shard_map/ppermute | solution.py:208
  88.9 5.3 %all-to-all-start.1 = ((bf16[32,64,128]{2,1,0:T(8,128)(2,1)}), bf16[32,64,128]{2,1,0:T(8,128)(2,1)}, u32[]{:S(2)}, u32[]{:S(2)}) async-start(bf16[32,64,128]{2,1,0:T(8,128)(2,1)} %shard_map.77.refs_0_), calls=%async_computation.1 | async-start | bytes 1048576 | tf_op jit(solution)/shard_map/all_to_all | solution.py:250
  95.0 4.9 %collective-permute-done.11.refs_14_ = bf16[4,128,512]{2,1,0:T(8,128)(2,1)} collective-permute-done((bf16[4,128,512]{2,1,0:T(8,128)(2,1)S(1)}, bf16[4,128,512]{2,1,0:T(8,128)(2,1)}, u32[]{:S(2)}, u32[]{:S(2)}) %collective-permute-start.11) | collective-permute-done | bytes 524320 | tf_op jit(solution)/shard_map/ppermute | solution.py:208
  99.9 3.2 %collective-permute-start.12 = (bf16[4,128,512]{2,1,0:T(8,128)(2,1)S(1)}, bf16[4,128,512]{2,1,0:T(8,128)(2,1)}, u32[]{:S(2)}, u32[]{:S(2)}) collective-permute-start(bf16[4,128,512]{2,1,0:T(8,128)(2,1)S(1)} %pad_maximum_fusion.1.refs_3_), channel_id=1, source_target_pairs={{0,1},{1,0},{2,3},{3,2},{4,5},{5,4},{6,7},{7,6},{8,9},{9,8},{10,11... | collective-permute-start | bytes 1572872 | tf_op jit(solution)/shard_map/ppermute | solution.py:247
  103.6 2.2 %copy-done.2 = bf16[1,250,64,128]{3,2,1,0:T(8,128)(2,1)S(1)} copy-done((bf16[1,250,64,128]{3,2,1,0:T(8,128)(2,1)S(1)}, bf16[1,250,64,128]{3,2,1,0:T(8,128)(2,1)}, u32[]{:S(2)}) %copy-start.2) | copy-done | bytes 4096024
  105.8 14.5 %shard_map.79.refs_2_ = bf16[32,32,128]{2,1,0:T(8,128)(2,1)} custom-call(s32[32,6,128]{2,1,0:T(8,128)S(1)} %all-to-all-done.ids_ref, f32[258,8,128]{2,1,0:T(8,128)S(1)} %fusion.6.first_ref, bf16[250,64,128]{2,1,0:T(8,128)(2,1)S(1)} %bitcast.50, bf16[250,16,128]{2,1,0:T(8,128)(2,1)S(1)} %fusion.4.last_ref), custom_call_target="tpu_custom_call" | custom-call | flops 4096000000 | bytes 6291456 | tf_op jit(solution)/shard_map/pallas_call | solution.py:118
  120.3 8.5 %all-to-all-start.3 = ((bf16[32,32,128]{2,1,0:T(8,128)(2,1)}), bf16[32,32,128]{2,1,0:T(8,128)(2,1)S(1)}, u32[]{:S(2)}, u32[]{:S(2)}) async-start(bf16[32,32,128]{2,1,0:T(8,128)(2,1)} %shard_map.79.refs_2_), calls=%async_computation.3 | async-start | bytes 524288 | tf_op jit(solution)/shard_map/all_to_all | solution.py:250
  128.8 1.9 %copy_bitcast_fusion = bf16[64,4096]{1,0:T(8,128)(2,1)} fusion(bf16[32,64,128]{2,1,0:T(8,128)(2,1)} %all-to-all-done.1), kind=kLoop, calls=%fused_computation.11 | loop fusion | bytes 1048576 | tf_op jit(solution)/shard_map/reshape | solution.py:262
  132.0 5.8 %all-to-all-done.3 = bf16[32,32,128]{2,1,0:T(8,128)(2,1)S(1)} async-done(((bf16[32,32,128]{2,1,0:T(8,128)(2,1)}), bf16[32,32,128]{2,1,0:T(8,128)(2,1)S(1)}, u32[]{:S(2)}, u32[]{:S(2)}) %all-to-all-start.3) | async-done | bytes 262176 | tf_op jit(solution)/shard_map/all_to_all | solution.py:250
  137.9 4.2 %shard_map.80 = (f32[128,256]{1,0:T(8,128)S(1)}, bf16[128,256]{1,0:T(8,128)(2,1)S(1)}, bf16[128,256]{1,0:T(8,128)(2,1)S(1)}, bf16[128,256]{1,0:T(8,128)(2,1)S(1)}) custom-call(s32[4]{0:T(128)S(1)} %pad_add_fusion.1.place_ref, bf16[32,64,128]{2,1,0:T(8,128)(2,1)} %shard_map.77.refs_0_, bf16[32,32,128]{2,1,0:T(8,128)(2,1)} %shard_map.78.refs_1_, ...), custom_call_target="tpu_custom_call" | custom-call | flops 1073741824 | bytes 9437184 | tf_op jit(solution)/shard_map/pallas_call | solution.py:189
  142.1 3.8 %collective-permute-start.22 = (bf16[128,256]{1,0:T(8,128)(2,1)S(1)}, bf16[128,256]{1,0:T(8,128)(2,1)S(1)}, u32[]{:S(2)}, u32[]{:S(2)}) collective-permute-start(bf16[128,256]{1,0:T(8,128)(2,1)S(1)} %get-tuple-element.33), channel_id=1, source_target_pairs={{0,96},{32,0},{64,32},{96,64},{1,97},{33,1},{65,33},{97,65},{2,98}... | collective-permute-start | bytes 196616 | tf_op jit(solution)/shard_map/ppermute | solution.py:258
  148.6 2.0 %collective-permute-done.21 = bf16[128,256]{1,0:T(8,128)(2,1)S(1)} collective-permute-done((bf16[128,256]{1,0:T(8,128)(2,1)S(1)}, bf16[128,256]{1,0:T(8,128)(2,1)S(1)}, u32[]{:S(2)}, u32[]{:S(2)}) %collective-permute-start.21) | collective-permute-done | bytes 65568 | tf_op jit(solution)/shard_map/ppermute | solution.py:258
  (65 shorter events, 19.8 us)
Async XLA Ops:
  2.3 20.7 %collective-permute-start.2 = (bf16[128,512]{1,0:T(8,128)(2,1)}, bf16[128,512]{1,0:T(8,128)(2,1)}, u32[]{:S(2)}, u32[]{:S(2)}) collective-permute-start(bf16[128,512]{1,0:T(8,128)(2,1)} %get-tuple-element.37), channel_id=1, source_target_pairs={{0,24},{8,0},{16,8},{24,16},{1,25},{9,1},{17,9},{25,17},{2,26},{10... | collective-permute-start | bytes 393224 | tf_op jit(solution)/shard_map/ppermute | solution.py:208
  5.6 18.9 %collective-permute-start.1 = (bf16[128,512]{1,0:T(8,128)(2,1)}, bf16[128,512]{1,0:T(8,128)(2,1)}, u32[]{:S(2)}, u32[]{:S(2)}) collective-permute-start(bf16[128,512]{1,0:T(8,128)(2,1)} %get-tuple-element.37), channel_id=1, source_target_pairs={{0,16},{8,24},{16,0},{24,8},{1,17},{9,25},{17,1},{25,9},{2,18},{10... | collective-permute-start | bytes 393224 | tf_op jit(solution)/shard_map/ppermute | solution.py:208
  6.1 18.4 %collective-permute-start = (bf16[128,512]{1,0:T(8,128)(2,1)}, bf16[128,512]{1,0:T(8,128)(2,1)}, u32[]{:S(2)}, u32[]{:S(2)}) collective-permute-start(bf16[128,512]{1,0:T(8,128)(2,1)} %get-tuple-element.37), channel_id=1, source_target_pairs={{0,8},{8,16},{16,24},{24,0},{1,9},{9,17},{17,25},{25,1},{2,10},{10... | collective-permute-start | bytes 393224 | tf_op jit(solution)/shard_map/ppermute | solution.py:208
  6.7 18.9 %collective-permute-start.5 = (bf16[128,512]{1,0:T(8,128)(2,1)S(1)}, bf16[128,512]{1,0:T(8,128)(2,1)}, u32[]{:S(2)}, u32[]{:S(2)}) collective-permute-start(bf16[128,512]{1,0:T(8,128)(2,1)S(1)} %get-tuple-element.36), channel_id=1, source_target_pairs={{0,6},{2,0},{4,2},{6,4},{1,7},{3,1},{5,3},{7,5},{8,14},{10,8},{12,... | collective-permute-start | bytes 393224 | tf_op jit(solution)/shard_map/ppermute | solution.py:208
  9.5 16.1 %collective-permute-start.4 = (bf16[128,512]{1,0:T(8,128)(2,1)S(1)}, bf16[128,512]{1,0:T(8,128)(2,1)}, u32[]{:S(2)}, u32[]{:S(2)}) collective-permute-start(bf16[128,512]{1,0:T(8,128)(2,1)S(1)} %get-tuple-element.36), channel_id=1, source_target_pairs={{0,4},{2,6},{4,0},{6,2},{1,5},{3,7},{5,1},{7,3},{8,12},{10,14},{12... | collective-permute-start | bytes 393224 | tf_op jit(solution)/shard_map/ppermute | solution.py:208
  12.2 18.9 %all-to-all-start = ((s32[32,6,128]{2,1,0:T(8,128)}), s32[32,6,128]{2,1,0:T(8,128)S(1)}, u32[]{:S(2)}, u32[]{:S(2)}) async-start(s32[32,6,128]{2,1,0:T(8,128)} %pad_add_fusion), calls=%async_computation | async-start | bytes 262144 | tf_op jit(solution)/shard_map/all_to_all | solution.py:226
  23.0 7.1 %collective-permute-start.3 = (bf16[128,512]{1,0:T(8,128)(2,1)S(1)}, bf16[128,512]{1,0:T(8,128)(2,1)S(1)}, u32[]{:S(2)}, u32[]{:S(2)}) collective-permute-start(bf16[128,512]{1,0:T(8,128)(2,1)S(1)} %get-tuple-element.36), channel_id=1, source_target_pairs={{0,2},{2,4},{4,6},{6,0},{1,3},{3,5},{5,7},{7,1},{8,10},{10,12},{12... | collective-permute-start | bytes 393224 | tf_op jit(solution)/shard_map/ppermute | solution.py:208
  31.1 55.2 %collective-permute-start.6 = (bf16[4,128,512]{2,1,0:T(8,128)(2,1)S(1)}, bf16[4,128,512]{2,1,0:T(8,128)(2,1)}, u32[]{:S(2)}, u32[]{:S(2)}) collective-permute-start(bf16[4,128,512]{2,1,0:T(8,128)(2,1)S(1)} %pad_maximum_fusion.1.refs_3_), channel_id=1, source_target_pairs={{0,2},{2,4},{4,6},{6,0},{1,3},{3,5},{5,7},{7,1},{8,10},{10,12},{12... | collective-permute-start | bytes 1572872 | tf_op jit(solution)/shard_map/ppermute | solution.py:208
  31.2 63.8 %collective-permute-start.7 = (bf16[4,128,512]{2,1,0:T(8,128)(2,1)S(1)}, bf16[4,128,512]{2,1,0:T(8,128)(2,1)}, u32[]{:S(2)}, u32[]{:S(2)}) collective-permute-start(bf16[4,128,512]{2,1,0:T(8,128)(2,1)S(1)} %pad_maximum_fusion.1.refs_3_), channel_id=1, source_target_pairs={{0,4},{2,6},{4,0},{6,2},{1,5},{3,7},{5,1},{7,3},{8,12},{10,14},{12... | collective-permute-start | bytes 1572872 | tf_op jit(solution)/shard_map/ppermute | solution.py:208
  32.9 62.1 %collective-permute-start.8 = (bf16[4,128,512]{2,1,0:T(8,128)(2,1)S(1)}, bf16[4,128,512]{2,1,0:T(8,128)(2,1)}, u32[]{:S(2)}, u32[]{:S(2)}) collective-permute-start(bf16[4,128,512]{2,1,0:T(8,128)(2,1)S(1)} %pad_maximum_fusion.1.refs_3_), channel_id=1, source_target_pairs={{0,6},{2,0},{4,2},{6,4},{1,7},{3,1},{5,3},{7,5},{8,14},{10,8},{12,... | collective-permute-start | bytes 1572872 | tf_op jit(solution)/shard_map/ppermute | solution.py:208
  33.9 61.1 %collective-permute-start.9 = (bf16[4,128,512]{2,1,0:T(8,128)(2,1)S(1)}, bf16[4,128,512]{2,1,0:T(8,128)(2,1)}, u32[]{:S(2)}, u32[]{:S(2)}) collective-permute-start(bf16[4,128,512]{2,1,0:T(8,128)(2,1)S(1)} %pad_maximum_fusion.2.refs_11_), channel_id=1, source_target_pairs={{0,8},{8,16},{16,24},{24,0},{1,9},{9,17},{17,25},{25,1},{2,10},{10... | collective-permute-start | bytes 1572872 | tf_op jit(solution)/shard_map/ppermute | solution.py:208
  35.0 60.0 %collective-permute-start.10 = (bf16[4,128,512]{2,1,0:T(8,128)(2,1)S(1)}, bf16[4,128,512]{2,1,0:T(8,128)(2,1)}, u32[]{:S(2)}, u32[]{:S(2)}) collective-permute-start(bf16[4,128,512]{2,1,0:T(8,128)(2,1)S(1)} %pad_maximum_fusion.2.refs_11_), channel_id=1, source_target_pairs={{0,16},{8,24},{16,0},{24,8},{1,17},{9,25},{17,1},{25,9},{2,18},{10... | collective-permute-start | bytes 1572872 | tf_op jit(solution)/shard_map/ppermute | solution.py:208
  54.2 34.7 %all-to-all-start.2 = ((bf16[32,32,128]{2,1,0:T(8,128)(2,1)}), bf16[32,32,128]{2,1,0:T(8,128)(2,1)S(1)}, u32[]{:S(2)}, u32[]{:S(2)}) async-start(bf16[32,32,128]{2,1,0:T(8,128)(2,1)} %shard_map.78.refs_1_), calls=%async_computation.2 | async-start | bytes 524288 | tf_op jit(solution)/shard_map/all_to_all | solution.py:250
  86.3 13.6 %collective-permute-start.11 = (bf16[4,128,512]{2,1,0:T(8,128)(2,1)S(1)}, bf16[4,128,512]{2,1,0:T(8,128)(2,1)}, u32[]{:S(2)}, u32[]{:S(2)}) collective-permute-start(bf16[4,128,512]{2,1,0:T(8,128)(2,1)S(1)} %pad_maximum_fusion.2.refs_11_), channel_id=1, source_target_pairs={{0,24},{8,0},{16,8},{24,16},{1,25},{9,1},{17,9},{25,17},{2,26},{10... | collective-permute-start | bytes 1572872 | tf_op jit(solution)/shard_map/ppermute | solution.py:208
  88.9 31.4 %all-to-all-start.1 = ((bf16[32,64,128]{2,1,0:T(8,128)(2,1)}), bf16[32,64,128]{2,1,0:T(8,128)(2,1)}, u32[]{:S(2)}, u32[]{:S(2)}) async-start(bf16[32,64,128]{2,1,0:T(8,128)(2,1)} %shard_map.77.refs_0_), calls=%async_computation.1 | async-start | bytes 1048576 | tf_op jit(solution)/shard_map/all_to_all | solution.py:250
  99.9 31.3 %collective-permute-start.12 = (bf16[4,128,512]{2,1,0:T(8,128)(2,1)S(1)}, bf16[4,128,512]{2,1,0:T(8,128)(2,1)}, u32[]{:S(2)}, u32[]{:S(2)}) collective-permute-start(bf16[4,128,512]{2,1,0:T(8,128)(2,1)S(1)} %pad_maximum_fusion.1.refs_3_), channel_id=1, source_target_pairs={{0,1},{1,0},{2,3},{3,2},{4,5},{5,4},{6,7},{7,6},{8,9},{9,8},{10,11... | collective-permute-start | bytes 1572872 | tf_op jit(solution)/shard_map/ppermute | solution.py:247
  103.1 28.4 %collective-permute-start.13 = (bf16[4,128,512]{2,1,0:T(8,128)(2,1)}, bf16[4,128,512]{2,1,0:T(8,128)(2,1)}, u32[]{:S(2)}, u32[]{:S(2)}) collective-permute-start(bf16[4,128,512]{2,1,0:T(8,128)(2,1)} %collective-permute-done.6.refs_4_), channel_id=1, source_target_pairs={{0,1},{1,0},{2,3},{3,2},{4,5},{5,4},{6,7},{7,6},{8,9},{9,8},{10,11... | collective-permute-start | bytes 1572872 | tf_op jit(solution)/shard_map/ppermute | solution.py:247
  103.1 28.6 %collective-permute-start.14 = (bf16[4,128,512]{2,1,0:T(8,128)(2,1)}, bf16[4,128,512]{2,1,0:T(8,128)(2,1)}, u32[]{:S(2)}, u32[]{:S(2)}) collective-permute-start(bf16[4,128,512]{2,1,0:T(8,128)(2,1)} %collective-permute-done.7.refs_5_), channel_id=1, source_target_pairs={{0,1},{1,0},{2,3},{3,2},{4,5},{5,4},{6,7},{7,6},{8,9},{9,8},{10,11... | collective-permute-start | bytes 1572872 | tf_op jit(solution)/shard_map/ppermute | solution.py:247
  120.3 17.5 %all-to-all-start.3 = ((bf16[32,32,128]{2,1,0:T(8,128)(2,1)}), bf16[32,32,128]{2,1,0:T(8,128)(2,1)S(1)}, u32[]{:S(2)}, u32[]{:S(2)}) async-start(bf16[32,32,128]{2,1,0:T(8,128)(2,1)} %shard_map.79.refs_2_), calls=%async_computation.3 | async-start | bytes 524288 | tf_op jit(solution)/shard_map/all_to_all | solution.py:250
  130.7 7.1 %collective-permute-start.15 = (bf16[4,128,512]{2,1,0:T(8,128)(2,1)}, bf16[4,128,512]{2,1,0:T(8,128)(2,1)S(1)}, u32[]{:S(2)}, u32[]{:S(2)}) collective-permute-start(bf16[4,128,512]{2,1,0:T(8,128)(2,1)} %collective-permute-done.8.refs_6_), channel_id=1, source_target_pairs={{0,1},{1,0},{2,3},{3,2},{4,5},{5,4},{6,7},{7,6},{8,9},{9,8},{10,11... | collective-permute-start | bytes 1572872 | tf_op jit(solution)/shard_map/ppermute | solution.py:247
  130.9 6.9 %collective-permute-start.16 = (bf16[4,128,512]{2,1,0:T(8,128)(2,1)S(1)}, bf16[4,128,512]{2,1,0:T(8,128)(2,1)S(1)}, u32[]{:S(2)}, u32[]{:S(2)}) collective-permute-start(bf16[4,128,512]{2,1,0:T(8,128)(2,1)S(1)} %pad_maximum_fusion.2.refs_11_), channel_id=1, source_target_pairs={{0,1},{1,0},{2,3},{3,2},{4,5},{5,4},{6,7},{7,6},{8,9},{9,8},{10,11... | collective-permute-start | bytes 1572872 | tf_op jit(solution)/shard_map/ppermute | solution.py:248
  131.2 6.6 %collective-permute-start.17 = (bf16[4,128,512]{2,1,0:T(8,128)(2,1)}, bf16[4,128,512]{2,1,0:T(8,128)(2,1)S(1)}, u32[]{:S(2)}, u32[]{:S(2)}) collective-permute-start(bf16[4,128,512]{2,1,0:T(8,128)(2,1)} %collective-permute-done.9.refs_12_), channel_id=1, source_target_pairs={{0,1},{1,0},{2,3},{3,2},{4,5},{5,4},{6,7},{7,6},{8,9},{9,8},{10,11... | collective-permute-start | bytes 1572872 | tf_op jit(solution)/shard_map/ppermute | solution.py:248
  131.5 6.4 %collective-permute-start.18 = (bf16[4,128,512]{2,1,0:T(8,128)(2,1)}, bf16[4,128,512]{2,1,0:T(8,128)(2,1)S(1)}, u32[]{:S(2)}, u32[]{:S(2)}) collective-permute-start(bf16[4,128,512]{2,1,0:T(8,128)(2,1)} %collective-permute-done.10.refs_13_), channel_id=1, source_target_pairs={{0,1},{1,0},{2,3},{3,2},{4,5},{5,4},{6,7},{7,6},{8,9},{9,8},{10,11... | collective-permute-start | bytes 1572872 | tf_op jit(solution)/shard_map/ppermute | solution.py:248
  142.1 6.6 %collective-permute-start.22 = (bf16[128,256]{1,0:T(8,128)(2,1)S(1)}, bf16[128,256]{1,0:T(8,128)(2,1)S(1)}, u32[]{:S(2)}, u32[]{:S(2)}) collective-permute-start(bf16[128,256]{1,0:T(8,128)(2,1)S(1)} %get-tuple-element.33), channel_id=1, source_target_pairs={{0,96},{32,0},{64,32},{96,64},{1,97},{33,1},{65,33},{97,65},{2,98}... | collective-permute-start | bytes 196616 | tf_op jit(solution)/shard_map/ppermute | solution.py:258
  (9 other events, 61.0 us)

commit v4 on v3

v4 whole, which is shorter than its diff:
```python
import jax
import jax.numpy as jnp
from jax import lax
from jax.experimental import pallas as pl
from jax.experimental.pallas import tpu as pltpu
from jax.sharding import PartitionSpec as P

D1 = 8
D2 = 2
D3 = 8
RANK = 64
BAG = 2
WIDTH = D1 * D2 * D3
BLOCK = 128


def rows_kernel(ids_ref, first_ref, middle_ref, last_ref, out_ref, prefix_ref, mixed_ref):
    f32 = jnp.float32
    bf16 = jnp.bfloat16
    senders, part, _ = out_ref.shape
    per_block = BLOCK // part
    blocks = senders // per_block
    groups = BLOCK // 8
    row16 = lax.broadcasted_iota(jnp.int32, (16, 128), 0)
    lane16 = lax.broadcasted_iota(jnp.int32, (16, 128), 1)
    keep = ((row16 < 8) == (lane16 < 64)).astype(bf16)
    zero = jnp.zeros((16, 128), bf16)
    lane = lax.broadcasted_iota(jnp.int32, (8, 128), 1) // 16

    def index(i, word, sample):
        return ids_ref[i * per_block + sample // part, word, sample % part]

    def prefixes(i, g):
        for n in range(0, 8, 2):
            pair = (n * groups + g, (n + 1) * groups + g)
            heads, centres = [], []
            for j in range(BAG):
                two = [first_ref[index(i, j, a)] for a in pair]
                heads.append(jnp.concatenate(two, axis=0).astype(bf16) * keep)
                centres += [middle_ref[index(i, 2 + j, a)] for a in pair]
            left = jnp.concatenate(
                [
                    jnp.concatenate([heads[0], zero], axis=1),
                    jnp.concatenate([zero, heads[1]], axis=1),
                ],
                axis=0,
            )
            product = jnp.dot(left, jnp.concatenate(centres, axis=0), preferred_element_type=f32)
            product = product.astype(bf16)
            at = g * 64 + n * 8
            prefix_ref[at : at + 16, :128] = product[:16]
            prefix_ref[at : at + 16, 128:] = product[16:]

    def contract(i, g):
        tails = [
            jnp.concatenate(
                [last_ref[index(i, 4 + j, n * groups + e)] for e in (g, g + 1) for n in range(8)],
                axis=0,
            )
            for j in range(BAG)
        ]
        product = lax.dot_general(
            prefix_ref[g * 64 : g * 64 + 128, :],
            jnp.concatenate(tails, axis=1),
            (((1,), (1,)), ((), ())),
            preferred_element_type=f32,
        )
        for e in range(2):
            own = product[e * 64 : e * 64 + 64, e * 128 : e * 128 + 128]
            mixed = own[:8]
            for n in range(1, 8):
                mixed = jnp.where(lane == n, own[n * 8 : n * 8 + 8], mixed)
            mixed_ref[(g + e) * 8 : (g + e) * 8 + 8, :] = mixed

    def arrange(i, h):
        parts = [mixed_ref[pl.ds(h * 8 + a, 8, stride=8), :] for a in range(8)]
        for k in (1, 2, 4):
            low = (lane & k) == 0
            moved = list(parts)
            for a in range(8):
                if a & k == 0:
                    p, q = parts[a], parts[a + k]
                    moved[a] = jnp.where(low, p, pltpu.roll(q, 16 * k, 1))
                    moved[a + k] = jnp.where(low, pltpu.roll(p, 128 - 16 * k, 1), q)
            parts = moved
        for n in range(8):
            at = n * groups + h
            out_ref[i * per_block + at // part, at % part : at % part + 8, :] = parts[n].astype(bf16)

    def step(i, carry):
        now = jnp.minimum(i, blocks - 1)
        before = jnp.clip(i - 1, 0, blocks - 1)
        earlier = jnp.clip(i - 2, 0, blocks - 1)
        for h in range(0, groups, 8):
            arrange(earlier, h)
        for g in range(0, groups, 2):
            contract(before, g)
            prefixes(now, g)
            prefixes(now, g + 1)
        return carry

    lax.fori_loop(0, blocks + 2, step, 0)


def table_rows(got, head, middle, tail):
    senders, _, own = got.shape
    lookups = senders * own * BAG
    vmem = pl.BlockSpec(memory_space=pltpu.VMEM)
    return pl.pallas_call(
        rows_kernel,
        out_shape=jax.ShapeDtypeStruct((senders, own, WIDTH), jnp.bfloat16),
        in_specs=[pl.BlockSpec(memory_space=pltpu.SMEM), vmem, vmem, vmem],
        out_specs=vmem,
        scratch_shapes=[
            pltpu.VMEM((BLOCK * 8, 256), jnp.bfloat16),
            pltpu.VMEM((BLOCK, 128), jnp.float32),
        ],
        compiler_params=pltpu.CompilerParams(vmem_limit_bytes=32 << 20),
        cost_estimate=pl.CostEstimate(
            flops=lookups * 2000000, bytes_accessed=6 << 20, transcendentals=0
        ),
    )(got, head, middle, tail)


def product_kernel(rows_ref, grad_ref, out_ref, total_ref):
    step = pl.program_id(0)
    value = lax.dot_general(
        rows_ref[...], grad_ref[...], (((0,), (0,)), ((), ())), preferred_element_type=jnp.float32
    )

    @pl.when(step == 0)
    def _():
        total_ref[...] = value

    @pl.when(step > 0)
    def _():
        total_ref[...] += value

    @pl.when(step == pl.num_programs(0) - 1)
    def _():
        parts, _, columns = out_ref.shape
        for d in range(parts):
            out_ref[d] = total_ref[:, d * columns : (d + 1) * columns]


def partial_product(rows, grad, parts):
    samples, width = rows.shape
    hidden_units = grad.shape[1]
    step = min(samples, 512)
    shape = (parts, width, hidden_units // parts)
    return pl.pallas_call(
        product_kernel,
        out_shape=jax.ShapeDtypeStruct(shape, jnp.float32),
        grid=(samples // step,),
        in_specs=[
            pl.BlockSpec((step, width), lambda i: (i, 0)),
            pl.BlockSpec((step, hidden_units), lambda i: (i, 0)),
        ],
        out_specs=pl.BlockSpec(shape, lambda i: (0, 0, 0)),
        scratch_shapes=[pltpu.VMEM((width, hidden_units), jnp.float32)],
        cost_estimate=pl.CostEstimate(
            flops=2 * samples * width * hidden_units,
            bytes_accessed=2 * samples * (width + hidden_units),
            transcendentals=0,
        ),
    )(rows, grad)


def body(core_ids, bag_lengths, first_core, middle_core, last_core, grad_hidden):
    own, tables = bag_lengths.shape
    ncore = first_core.shape[1]
    n_data = lax.axis_size("dp")

    gathered = lax.all_gather(grad_hidden, "table", axis=0, tiled=True)

    ids = jnp.transpose(core_ids, (1, 2, 3, 0))
    lengths = jnp.transpose(bag_lengths)
    live = jnp.arange(BAG, dtype=jnp.int32)[None, :, None] < lengths[:, None, :]
    heads = jnp.where(live, ids[:, 0], ncore)
    sent = jnp.concatenate([heads, ids[:, 1], ids[:, 2]], axis=1)
    got = lax.all_to_all(sent, "table", split_axis=0, concat_axis=0, tiled=True)

    head = first_core[0].reshape(ncore, D1, RANK).astype(jnp.float32)
    head = jnp.pad(jnp.concatenate([head, head], axis=2), ((0, 8), (0, 0), (0, 0)))
    tail = last_core[0].reshape(ncore, RANK, D3).transpose(0, 2, 1)
    blank = jnp.zeros_like(tail)
    tail = jnp.concatenate(
        [jnp.concatenate([tail, blank], axis=2), jnp.concatenate([blank, tail], axis=2)], axis=1
    )
    rows = table_rows(got, head, middle_core[0], tail)

    partial = partial_product(rows.reshape(tables * own, WIDTH), gathered, n_data)
    weight_grad = lax.psum_scatter(partial, "dp", scatter_dimension=0, tiled=False)

    returned = lax.all_to_all(rows, "table", split_axis=0, concat_axis=0, tiled=True)
    pooled = jnp.transpose(returned, (1, 0, 2)).reshape(own, tables * WIDTH)
    return (pooled, weight_grad)


def solution(mesh):
    placed = (
        P(("dp", "table"), None, None, None),
        P(("dp", "table"), None),
        P("table", None, None),
        P("table", None, None, None),
        P("table", None, None),
        P(("dp", "table"), None),
    )
    return jax.shard_map(
        body,
        mesh=mesh,
        in_specs=placed,
        out_specs=(P(("dp", "table"), None), P("table", "dp")),
        check_vma=False,
    )
```

time: 154 us -> 108 us (0.70)
  starting transfers between devices: 56.1 us -> 8.67 us
  blocking collectives: 0 us -> 20.6 us
  waiting for transfers between devices: 19.8 us -> 5.82 us
  between operations: 0.89 us -> 14.2 us
  Pallas kernels: 56.5 us -> 48.7 us
  local copies, waits for them, and re-layouts: 13.7 us -> 7.99 us
  other arithmetic: 5.92 us -> 1.97 us
    ppermute x23 -> x0, starting transfers between devices: 27.5 us -> none  [the longest x12 18 us: around(): lax.ppermute(value, axis, [(i, (i + k) % size) for i in range(size)])]
    all_to_all x0 -> x1, blocking collectives: none -> 20.6 us  [body(): lax.all_to_all(rows, 'table', split_axis=0, concat_axis=0, tiled=True)]
    all_to_all x4 -> x1, starting transfers between devices: 28.7 us -> 8.59 us  [body(): got = lax.all_to_all(sent, 'table', split_axis=0, concat_axis=0, tiled=True)]
    ppermute x23 -> x0, waiting for transfers between devices: 14 us -> none  [the longest x12 9.35 us: around(): lax.ppermute(value, axis, [(i, (i + k) % size) for i in range(size)])]
    pallas_call x4 -> x2, Pallas kernels: 56.5 us -> 48.7 us  [the longest x1 40.5 us: table_rows(): pl.pallas_call(rows_kernel, out_shape=jax.ShapeDtypeStruct((senders, own,...]
    reshape x3 -> x0, local copies, waits for them, and re-layouts: 2.62 us -> none  [body(): jnp.transpose(r, (1, 0, 2)).reshape(r.shape[1], tables * WIDTH)]
    another operation x3 -> x0, other arithmetic: 2.21 us -> none  [the longest x2 2.14 us: body(): left, right = (jnp.stack(left), jnp.stack(right))]
    unnamed x15 -> x12, local copies, waits for them, and re-layouts: 8.63 us -> 6.59 us
  transfers between devices with their start and end apart: 27 -> 3, of which waited for: 6 -> 1; matrix products, arithmetic and copies ran while one was open for 7% -> 6% of each run, Pallas kernels for 34% -> 38%
where the time goes in v4:
time: 108 us
  Pallas kernels  48.7 us (45%)
  blocking collectives  20.6 us (19%)
  between operations  14.2 us (13%)
  starting transfers between devices  8.67 us (8%)
  local copies, waits for them, and re-layouts  7.99 us (7%)
  waiting for transfers between devices  5.82 us (5%)
  other arithmetic  1.97 us (2%)
    pallas_call x1, Pallas kernels, table_rows(): pl.pallas_call(rows_kernel, out_shape=jax.ShapeDtypeStruct((senders, own,...  40.5 us
    all_to_all x1, blocking collectives, body(): lax.all_to_all(rows, 'table', split_axis=0, concat_axis=0, tiled=True)  20.6 us
    all_to_all x1, starting transfers between devices, body(): got = lax.all_to_all(sent, 'table', split_axis=0, concat_axis=0, tiled=True)  8.59 us
    pallas_call x1, Pallas kernels, partial_product(): pl.pallas_call(product_kernel, out_shape=jax.ShapeDtypeStruct(shape, jnp....  8.27 us
    unnamed x12, local copies, waits for them, and re-layouts  6.59 us
    all_to_all x1, waiting for transfers between devices, body(): got = lax.all_to_all(sent, 'table', split_axis=0, concat_axis=0, tiled=True)  5.12 us
  transfers between devices with their start and end apart: 3, of which 1 were waited for; matrix products, arithmetic and copies ran while one was open for 6% of the time, Pallas kernels for 38%

profile of v4, /device:TPU:1, one launch (start us, length us, event | category | flops | bytes accessed | tf_op | source)
XLA Modules:
  0.0 107.9 jit_solution(6443177289344295977)
XLA Ops:
  7.2 0.0 all-gather.2.cloned.1.call-start
  7.2 0.7 all-gather.2.cloned.1.call-update
  7.9 0.9 copy.18
  8.8 0.7 compare_select_fusion
  9.6 0.7 pad_add_fusion
  10.3 8.6 %all-to-all-start = ((s32[32,6,128]{2,1,0:T(8,128)}), s32[32,6,128]{2,1,0:T(8,128)S(1)}, u32[]{:S(2)}, u32[]{:S(2)}) async-start(s32[32,6,128]{2,1,0:T(8,128)} %pad_add_fusion), calls=%async_computation | async-start | bytes 262144 | tf_op jit(solution)/shard_map/all_to_all | solution.py:181
  18.9 0.0 reduce-scatter.2.cloned.1.call-start
  18.9 1.1 %copy.10 = bf16[1,250,512]{1,2,0:T(8,128)(2,1)S(1)} copy(bf16[1,250,512]{2,1,0:T(8,128)(2,1)} %param.8) | data formatting | bytes 512000 | tf_op args[2]
  20.0 0.3 copy.11
  20.4 0.1 copy.13
  20.5 0.4 copy.14
  20.9 0.3 fusion.6.first_ref
  21.2 0.3 fusion.4.last_ref
  21.5 5.1 %all-to-all-done.ids_ref = s32[32,6,128]{2,1,0:T(8,128)S(1)} async-done(((s32[32,6,128]{2,1,0:T(8,128)}), s32[32,6,128]{2,1,0:T(8,128)S(1)}, u32[]{:S(2)}, u32[]{:S(2)}) %all-to-all-start) | async-done | bytes 98336 | tf_op jit(solution)/shard_map/all_to_all | solution.py:181
  26.6 2.2 %copy-done.2 = bf16[1,250,64,128]{3,2,1,0:T(8,128)(2,1)S(1)} copy-done((bf16[1,250,64,128]{3,2,1,0:T(8,128)(2,1)S(1)}, bf16[1,250,64,128]{3,2,1,0:T(8,128)(2,1)}, u32[]{:S(2)}) %copy-start.2) | copy-done | bytes 4096024
  28.8 40.5 %shard_map.77 = bf16[32,128,128]{2,1,0:T(8,128)(2,1)S(1)} custom-call(s32[32,6,128]{2,1,0:T(8,128)S(1)} %all-to-all-done.ids_ref, f32[258,8,128]{2,1,0:T(8,128)S(1)} %fusion.6.first_ref, bf16[250,64,128]{2,1,0:T(8,128)(2,1)S(1)} %bitcast.21, bf16[250,16,128]{2,1,0:T(8,128)(2,1)S(1)} %fusion.4.last_ref), custom_call_target="tpu_custom_call" | custom-call | flops 16384000000 | bytes 6291456 | tf_op jit(solution)/shard_map/pallas_call | solution.py:109
  69.2 0.0 copy-start
  69.3 1.0 copy-done
  70.2 8.3 %shard_map.78 = f32[4,128,256]{2,1,0:T(8,128)} custom-call(bf16[4096,128]{1,0:T(8,128)(2,1)} %bitcast.20, bf16[4096,1024]{1,0:T(8,128)(2,1)} %all-gather.2.cloned.1.call-done.grad_ref), custom_call_target="tpu_custom_call" | custom-call | flops 1073741824 | bytes 9437184 | tf_op jit(solution)/shard_map/pallas_call | solution.py:151
  78.5 0.0 reduce-scatter.2.cloned.1.call-update
  78.5 0.0 copy-done.1
  78.5 20.6 %all_to_all.10 = bf16[32,128,128]{2,1,0:T(8,128)(2,1)S(1)} all-to-all(bf16[32,128,128]{2,1,0:T(8,128)(2,1)S(1)} %copy-done.1), channel_id=1, replica_groups=mesh['dp'=4,'table'=32] {'table'}, dimensions={0} | all-to-all | bytes 2097152 | tf_op jit(solution)/shard_map/all_to_all | solution.py:195
  99.1 0.7 copy.15
  99.8 1.3 %copy.16 = bf16[128,4096]{1,0:T(8,128)(2,1)} copy(bf16[128,4096]{0,1:T(8,128)(2,1)S(1)} %bitcast.23) | data formatting | bytes 2097152
  (7 shorter events, 0.0 us)
Async XLA Ops:
  7.2 13.2 %copy-start.3 = (bf16[1,250,512]{2,1,0:T(8,128)(2,1)S(1)}, bf16[1,250,512]{2,1,0:T(8,128)(2,1)}, u32[]{:S(2)}) copy-start(bf16[1,250,512]{2,1,0:T(8,128)(2,1)} %param.10) | copy-start | bytes 768004
  7.2 63.0 %all-gather.2.cloned.1.call-start = ((), (), s32[]{:S(2)}) async-start(), calls=%async_computation.3 | async-start | bytes 8650752 | tf_op jit(solution)/shard_map/all_gather | solution.py:174
  10.3 16.3 %all-to-all-start = ((s32[32,6,128]{2,1,0:T(8,128)}), s32[32,6,128]{2,1,0:T(8,128)S(1)}, u32[]{:S(2)}, u32[]{:S(2)}) async-start(s32[32,6,128]{2,1,0:T(8,128)} %pad_add_fusion), calls=%async_computation | async-start | bytes 262144 | tf_op jit(solution)/shard_map/all_to_all | solution.py:181
  18.9 82.2 %reduce-scatter.2.cloned.1.call-start = ((), (), s32[]{:S(2)}) async-start(), calls=%async_computation.4 | async-start | bytes 655360 | tf_op jit(solution)/shard_map/reduce_scatter | solution.py:193
  26.6 2.2 %copy-start.2 = (bf16[1,250,64,128]{3,2,1,0:T(8,128)(2,1)S(1)}, bf16[1,250,64,128]{3,2,1,0:T(8,128)(2,1)}, u32[]{:S(2)}) copy-start(bf16[1,250,64,128]{3,2,1,0:T(8,128)(2,1)} %param.9) | copy-start | bytes 12288004
  69.2 1.0 copy-start
  70.2 8.3 %copy-start.1 = (bf16[32,128,128]{2,1,0:T(8,128)(2,1)S(1)}, bf16[32,128,128]{2,1,0:T(8,128)(2,1)}, u32[]{:S(2)}) copy-start(bf16[32,128,128]{2,1,0:T(8,128)(2,1)} %copy-done) | copy-start | bytes 3145732
Sparse Core Ops, SparseCore 0:
  10.3 56.3 all-gather.1
  78.6 18.5 reduce-scatter.1

commit v5 on v4

--- a/solution.py
+++ b/solution.py
@@ -28,7 +28,7 @@
     lane = lax.broadcasted_iota(jnp.int32, (8, 128), 1) // 16
 
     def index(i, word, sample):
-        return ids_ref[i * per_block + sample // part, word, sample % part]
+        return ids_ref[i * per_block + sample // part, word // BAG, word % BAG, sample % part]
 
     def prefixes(i, g):
         for n in range(0, 8, 2):
@@ -103,7 +103,7 @@
 
 
 def table_rows(got, head, middle, tail):
-    senders, _, own = got.shape
+    senders, own = got.shape[0], got.shape[-1]
     lookups = senders * own * BAG
     vmem = pl.BlockSpec(memory_space=pltpu.VMEM)
     return pl.pallas_call(
@@ -122,42 +122,48 @@
     )(got, head, middle, tail)
 
 
-def product_kernel(rows_ref, grad_ref, out_ref, total_ref):
-    step = pl.program_id(0)
-    value = lax.dot_general(
-        rows_ref[...], grad_ref[...], (((0,), (0,)), ((), ())), preferred_element_type=jnp.float32
-    )
-
-    @pl.when(step == 0)
-    def _():
-        total_ref[...] = value
-
-    @pl.when(step > 0)
-    def _():
-        total_ref[...] += value
-
-    @pl.when(step == pl.num_programs(0) - 1)
-    def _():
-        parts, _, columns = out_ref.shape
-        for d in range(parts):
-            out_ref[d] = total_ref[:, d * columns : (d + 1) * columns]
+def product_kernel(rows_ref, grad_ref, out_ref, held_ref, total_ref, sems):
+    chunks, size, _ = held_ref.shape
+    copies = []
+    for i in range(chunks):
+        source = grad_ref.at[pl.ds(i * size, size)]
+        copies.append(pltpu.make_async_copy(source, held_ref.at[i], sems.at[i]))
+        copies[-1].start()
+    for i in range(chunks):
+        copies[i].wait()
+        value = lax.dot_general(
+            rows_ref[i * size : (i + 1) * size, :],
+            held_ref[i],
+            (((0,), (0,)), ((), ())),
+            preferred_element_type=jnp.float32,
+        )
+        if i == 0:
+            total_ref[...] = value
+        elif i < chunks - 1:
+            total_ref[...] += value
+        else:
+            value += total_ref[...]
+            parts, _, columns = out_ref.shape
+            for d in range(parts):
+                out_ref[d] = value[:, d * columns : (d + 1) * columns]
 
 
 def partial_product(rows, grad, parts):
     samples, width = rows.shape
     hidden_units = grad.shape[1]
-    step = min(samples, 512)
-    shape = (parts, width, hidden_units // parts)
+    size = min(samples, 512)
+    vmem = pl.BlockSpec(memory_space=pltpu.VMEM)
     return pl.pallas_call(
         product_kernel,
-        out_shape=jax.ShapeDtypeStruct(shape, jnp.float32),
-        grid=(samples // step,),
-        in_specs=[
-            pl.BlockSpec((step, width), lambda i: (i, 0)),
-            pl.BlockSpec((step, hidden_units), lambda i: (i, 0)),
+        out_shape=jax.ShapeDtypeStruct((parts, width, hidden_units // parts), jnp.float32),
+        in_specs=[vmem, pl.BlockSpec(memory_space=pltpu.HBM)],
+        out_specs=vmem,
+        scratch_shapes=[
+            pltpu.VMEM((samples // size, size, hidden_units), grad.dtype),
+            pltpu.VMEM((width, hidden_units), jnp.float32),
+            pltpu.SemaphoreType.DMA((samples // size,)),
         ],
-        out_specs=pl.BlockSpec(shape, lambda i: (0, 0, 0)),
-        scratch_shapes=[pltpu.VMEM((width, hidden_units), jnp.float32)],
+        compiler_params=pltpu.CompilerParams(vmem_limit_bytes=54 << 20),
         cost_estimate=pl.CostEstimate(
             flops=2 * samples * width * hidden_units,
             bytes_accessed=2 * samples * (width + hidden_units),
@@ -166,6 +172,24 @@
     )(rows, grad)
 
 
+def beside_kernel(blocks_ref, out_ref):
+    tables, _, width = blocks_ref.shape
+    for t in range(tables):
+        out_ref[:, t * width : (t + 1) * width] = blocks_ref[t]
+
+
+def side_by_side(blocks):
+    tables, own, width = blocks.shape
+    step = min(own, 32)
+    return pl.pallas_call(
+        beside_kernel,
+        out_shape=jax.ShapeDtypeStruct((own, tables * width), blocks.dtype),
+        grid=(own // step,),
+        in_specs=[pl.BlockSpec((tables, step, width), lambda i: (0, i, 0))],
+        out_specs=pl.BlockSpec((step, tables * width), lambda i: (i, 0)),
+    )(blocks)
+
+
 def body(core_ids, bag_lengths, first_core, middle_core, last_core, grad_hidden):
     own, tables = bag_lengths.shape
     ncore = first_core.shape[1]
@@ -174,10 +198,10 @@
     gathered = lax.all_gather(grad_hidden, "table", axis=0, tiled=True)
 
     ids = jnp.transpose(core_ids, (1, 2, 3, 0))
-    lengths = jnp.transpose(bag_lengths)
-    live = jnp.arange(BAG, dtype=jnp.int32)[None, :, None] < lengths[:, None, :]
-    heads = jnp.where(live, ids[:, 0], ncore)
-    sent = jnp.concatenate([heads, ids[:, 1], ids[:, 2]], axis=1)
+    lengths = jnp.transpose(bag_lengths)[:, None, None, :]
+    core = lax.broadcasted_iota(jnp.int32, ids.shape, 1)
+    slot = lax.broadcasted_iota(jnp.int32, ids.shape, 2)
+    sent = jnp.where((core == 0) & (slot >= lengths), ncore, ids)
     got = lax.all_to_all(sent, "table", split_axis=0, concat_axis=0, tiled=True)
 
     head = first_core[0].reshape(ncore, D1, RANK).astype(jnp.float32)
@@ -193,7 +217,7 @@
     weight_grad = lax.psum_scatter(partial, "dp", scatter_dimension=0, tiled=False)
 
     returned = lax.all_to_all(rows, "table", split_axis=0, concat_axis=0, tiled=True)
-    pooled = jnp.transpose(returned, (1, 0, 2)).reshape(own, tables * WIDTH)
+    pooled = side_by_side(returned)
     return (pooled, weight_grad)
 
 

time: 108 us -> 106 us (0.981)
  local copies, waits for them, and re-layouts: 7.99 us -> 5.09 us
    unnamed x12 -> x10, local copies, waits for them, and re-layouts: 6.59 us -> 4.35 us
    pallas_call x1 -> x2, Pallas kernels: 8.27 us -> 9.38 us  [the longest x1 5.96 us: partial_product(): pl.pallas_call(product_kernel, out_shape=jax.ShapeDtypeStruct((parts, wid...]
  transfers between devices with their start and end apart: 3 -> 3, of which waited for: 1 -> 1; matrix products, arithmetic and copies ran while one was open for 6% -> 4% of each run, Pallas kernels for 38% -> 41%
where the time goes in v5:
time: 106 us
  Pallas kernels  49.3 us (47%)
  blocking collectives  20.7 us (20%)
  between operations  14.1 us (13%)
  starting transfers between devices  8.67 us (8%)
  waiting for transfers between devices  5.57 us (5%)
  local copies, waits for them, and re-layouts  5.09 us (5%)
  other arithmetic  2.19 us (2%)
    pallas_call x1, Pallas kernels, table_rows(): pl.pallas_call(rows_kernel, out_shape=jax.ShapeDtypeStruct((senders, own,...  39.9 us
    all_to_all x1, blocking collectives, body(): lax.all_to_all(rows, 'table', split_axis=0, concat_axis=0, tiled=True)  20.7 us
    all_to_all x1, starting transfers between devices, body(): got = lax.all_to_all(sent, 'table', split_axis=0, concat_axis=0, tiled=True)  8.59 us
    pallas_call x1, Pallas kernels, partial_product(): pl.pallas_call(product_kernel, out_shape=jax.ShapeDtypeStruct((parts, wid...  5.96 us
    all_to_all x1, waiting for transfers between devices, body(): got = lax.all_to_all(sent, 'table', split_axis=0, concat_axis=0, tiled=True)  4.87 us
    unnamed x10, local copies, waits for them, and re-layouts  4.35 us
    pallas_call x1, Pallas kernels, side_by_side(): pl.pallas_call(beside_kernel, out_shape=jax.ShapeDtypeStruct((own, tables...  3.42 us
  transfers between devices with their start and end apart: 3, of which 1 were waited for; matrix products, arithmetic and copies ran while one was open for 4% of the time, Pallas kernels for 41%

profile of v5, /device:TPU:1, one launch (start us, length us, event | category | flops | bytes accessed | tf_op | source)
XLA Modules:
  0.0 105.7 jit_solution(2468891648932384073)
XLA Ops:
  7.2 0.0 copy-start.3
  7.2 0.0 all-gather.2.cloned.1.call-start
  7.2 0.7 all-gather.2.cloned.1.call-update
  7.9 1.7 %and_select_fusion = s32[32,3,2,128]{3,2,1,0:T(2,128)} fusion(s32[128,32,3,2]{0,3,2,1:T(2,128)} %param.6, pred[3]{0:T(512)(128)(4,1)S(1)} %iota_compare_fusion.3, s32[32,128]{1,0:T(8,128)} %bitcast.14), kind=kLoop, calls=%fused_computation.10 | loop fusion | flops 73728 | bytes 212995 | tf_op jit(solution)/shard_map/jit(_where)/select_n | solution.py:204
  9.6 8.6 %all-to-all-start = ((s32[32,3,2,128]{3,2,1,0:T(2,128)}), s32[32,3,2,128]{3,2,1,0:T(2,128)S(1)}, u32[]{:S(2)}, u32[]{:S(2)}) async-start(s32[32,3,2,128]{3,2,1,0:T(2,128)} %and_select_fusion), calls=%async_computation | async-start | bytes 196608 | tf_op jit(solution)/shard_map/all_to_all | solution.py:205
  18.2 0.0 reduce-scatter.2.cloned.1.call-start
  18.2 1.1 %copy.8 = bf16[1,250,512]{1,2,0:T(8,128)(2,1)S(1)} copy(bf16[1,250,512]{2,1,0:T(8,128)(2,1)} %param.8) | data formatting | bytes 512000 | tf_op args[2]
  19.3 0.3 copy.9
  19.6 0.0 copy-done.3
  19.7 0.1 copy.11
  19.8 0.4 copy.12
  20.2 0.3 fusion.6.first_ref
  20.5 0.3 fusion.4.last_ref
  20.8 4.9 %all-to-all-done.ids_ref = s32[32,3,2,128]{3,2,1,0:T(2,128)S(1)} async-done(((s32[32,3,2,128]{3,2,1,0:T(2,128)}), s32[32,3,2,128]{3,2,1,0:T(2,128)S(1)}, u32[]{:S(2)}, u32[]{:S(2)}) %all-to-all-start) | async-done | bytes 98336 | tf_op jit(solution)/shard_map/all_to_all | solution.py:205
  25.6 0.0 copy-start.2
  25.6 2.2 %copy-done.2 = bf16[1,250,64,128]{3,2,1,0:T(8,128)(2,1)S(1)} copy-done((bf16[1,250,64,128]{3,2,1,0:T(8,128)(2,1)S(1)}, bf16[1,250,64,128]{3,2,1,0:T(8,128)(2,1)}, u32[]{:S(2)}) %copy-start.2) | copy-done | bytes 4096024
  27.8 39.9 %shard_map.77 = bf16[32,128,128]{2,1,0:T(8,128)(2,1)S(1)} custom-call(s32[32,3,2,128]{3,2,1,0:T(2,128)S(1)} %all-to-all-done.ids_ref, f32[258,8,128]{2,1,0:T(8,128)S(1)} %fusion.6.first_ref, bf16[250,64,128]{2,1,0:T(8,128)(2,1)S(1)} %bitcast.10, bf16[250,16,128]{2,1,0:T(8,128)(2,1)S(1)} %fusion.4.last_ref), custom_call_target="tpu_custom_call" | custom-call | flops 16384000000 | bytes 6291456 | tf_op jit(solution)/shard_map/pallas_call | solution.py:109
  67.7 0.0 copy-start
  67.7 1.0 copy-done
  68.7 6.0 %shard_map.79 = f32[4,128,256]{2,1,0:T(8,128)} custom-call(bf16[4096,128]{1,0:T(8,128)(2,1)} %bitcast.9, bf16[4096,1024]{1,0:T(8,128)(2,1)} %all-gather.2.cloned.1.call-done.grad_ref), custom_call_target="tpu_custom_call" | custom-call | flops 1073741824 | bytes 9437184 | tf_op jit(solution)/shard_map/pallas_call | solution.py:156
  74.7 0.0 reduce-scatter.2.cloned.1.call-update
  74.7 0.0 copy-done.1
  74.7 20.7 %all_to_all.10.blocks_ref = bf16[32,128,128]{2,1,0:T(8,128)(2,1)} all-to-all(bf16[32,128,128]{2,1,0:T(8,128)(2,1)S(1)} %copy-done.1), channel_id=1, replica_groups=mesh['dp'=4,'table'=32] {'table'}, dimensions={0} | all-to-all | bytes 2097152 | tf_op jit(solution)/shard_map/all_to_all | solution.py:219
  95.4 3.4 %shard_map.78 = bf16[128,4096]{1,0:T(8,128)(2,1)} custom-call(bf16[32,128,128]{2,1,0:T(8,128)(2,1)} %all_to_all.10.blocks_ref), custom_call_target="tpu_custom_call" | custom-call | tf_op jit(solution)/shard_map/pallas_call | solution.py:184
  (4 shorter events, 0.0 us)
Async XLA Ops:
  7.2 12.5 %copy-start.3 = (bf16[1,250,512]{2,1,0:T(8,128)(2,1)S(1)}, bf16[1,250,512]{2,1,0:T(8,128)(2,1)}, u32[]{:S(2)}) copy-start(bf16[1,250,512]{2,1,0:T(8,128)(2,1)} %param.10) | copy-start | bytes 768004
  7.2 61.5 %all-gather.2.cloned.1.call-start = ((), (), s32[]{:S(2)}) async-start(), calls=%async_computation.3 | async-start | bytes 8650752 | tf_op jit(solution)/shard_map/all_gather | solution.py:198
  9.6 16.1 %all-to-all-start = ((s32[32,3,2,128]{3,2,1,0:T(2,128)}), s32[32,3,2,128]{3,2,1,0:T(2,128)S(1)}, u32[]{:S(2)}, u32[]{:S(2)}) async-start(s32[32,3,2,128]{3,2,1,0:T(2,128)} %and_select_fusion), calls=%async_computation | async-start | bytes 196608 | tf_op jit(solution)/shard_map/all_to_all | solution.py:205
  18.2 80.7 %reduce-scatter.2.cloned.1.call-start = ((), (), s32[]{:S(2)}) async-start(), calls=%async_computation.4 | async-start | bytes 655360 | tf_op jit(solution)/shard_map/reduce_scatter | solution.py:217
  25.6 2.2 %copy-start.2 = (bf16[1,250,64,128]{3,2,1,0:T(8,128)(2,1)S(1)}, bf16[1,250,64,128]{3,2,1,0:T(8,128)(2,1)}, u32[]{:S(2)}) copy-start(bf16[1,250,64,128]{3,2,1,0:T(8,128)(2,1)} %param.9) | copy-start | bytes 12288004
  67.7 1.0 copy-start
  68.7 6.0 %copy-start.1 = (bf16[32,128,128]{2,1,0:T(8,128)(2,1)S(1)}, bf16[32,128,128]{2,1,0:T(8,128)(2,1)}, u32[]{:S(2)}) copy-start(bf16[32,128,128]{2,1,0:T(8,128)(2,1)} %copy-done) | copy-start | bytes 3145732
Sparse Core Ops, SparseCore 0:
  10.3 56.4 all-gather.1
  74.8 18.7 reduce-scatter.1

commit v6 on v5

--- a/solution.py
+++ b/solution.py
@@ -122,7 +122,8 @@
     )(got, head, middle, tail)
 
 
-def product_kernel(rows_ref, grad_ref, out_ref, held_ref, total_ref, sems):
+def product_kernel(place_ref, rows_ref, grad_ref, own_ref, *refs):
+    others, (held_ref, total_ref, sems) = refs[:-3], refs[-3:]
     chunks, size, _ = held_ref.shape
     copies = []
     for i in range(chunks):
@@ -139,55 +140,46 @@
         )
         if i == 0:
             total_ref[...] = value
-        elif i < chunks - 1:
+        else:
             total_ref[...] += value
+    columns = own_ref.shape[1]
+    parts = len(others) + 1
+    for k in range(parts):
+        at = pl.multiple_of(lax.rem(place_ref[0] + k, parts) * columns, columns)
+        block = total_ref[:, pl.ds(at, columns)]
+        if k == 0:
+            own_ref[...] = block
         else:
-            value += total_ref[...]
-            parts, _, columns = out_ref.shape
-            for d in range(parts):
-                out_ref[d] = value[:, d * columns : (d + 1) * columns]
-
-
-def partial_product(rows, grad, parts):
+            others[k - 1][...] = block.astype(jnp.bfloat16)
+
+
+def partial_product(rows, grad, place, parts):
     samples, width = rows.shape
     hidden_units = grad.shape[1]
     size = min(samples, 512)
     vmem = pl.BlockSpec(memory_space=pltpu.VMEM)
     return pl.pallas_call(
         product_kernel,
-        out_shape=jax.ShapeDtypeStruct((parts, width, hidden_units // parts), jnp.float32),
-        in_specs=[vmem, pl.BlockSpec(memory_space=pltpu.HBM)],
-        out_specs=vmem,
+        out_shape=[jax.ShapeDtypeStruct((width, hidden_units // parts), jnp.float32)]
+        + [jax.ShapeDtypeStruct((width, hidden_units // parts), jnp.bfloat16)] * (parts - 1),
+        in_specs=[
+            pl.BlockSpec(memory_space=pltpu.SMEM),
+            vmem,
+            pl.BlockSpec(memory_space=pltpu.HBM),
+        ],
+        out_specs=[vmem] * parts,
         scratch_shapes=[
             pltpu.VMEM((samples // size, size, hidden_units), grad.dtype),
             pltpu.VMEM((width, hidden_units), jnp.float32),
             pltpu.SemaphoreType.DMA((samples // size,)),
         ],
-        compiler_params=pltpu.CompilerParams(vmem_limit_bytes=54 << 20),
+        compiler_params=pltpu.CompilerParams(vmem_limit_bytes=50 << 20),
         cost_estimate=pl.CostEstimate(
             flops=2 * samples * width * hidden_units,
             bytes_accessed=2 * samples * (width + hidden_units),
             transcendentals=0,
         ),
-    )(rows, grad)
-
-
-def beside_kernel(blocks_ref, out_ref):
-    tables, _, width = blocks_ref.shape
-    for t in range(tables):
-        out_ref[:, t * width : (t + 1) * width] = blocks_ref[t]
-
-
-def side_by_side(blocks):
-    tables, own, width = blocks.shape
-    step = min(own, 32)
-    return pl.pallas_call(
-        beside_kernel,
-        out_shape=jax.ShapeDtypeStruct((own, tables * width), blocks.dtype),
-        grid=(own // step,),
-        in_specs=[pl.BlockSpec((tables, step, width), lambda i: (0, i, 0))],
-        out_specs=pl.BlockSpec((step, tables * width), lambda i: (i, 0)),
-    )(blocks)
+    )(place, rows, grad)
 
 
 def body(core_ids, bag_lengths, first_core, middle_core, last_core, grad_hidden):
@@ -213,11 +205,15 @@
     )
     rows = table_rows(got, head, middle_core[0], tail)
 
-    partial = partial_product(rows.reshape(tables * own, WIDTH), gathered, n_data)
-    weight_grad = lax.psum_scatter(partial, "dp", scatter_dimension=0, tiled=False)
-
     returned = lax.all_to_all(rows, "table", split_axis=0, concat_axis=0, tiled=True)
-    pooled = side_by_side(returned)
+
+    place = lax.axis_index("dp").astype(jnp.int32).reshape(1)
+    weight_grad, *others = partial_product(rows.reshape(tables * own, WIDTH), gathered, place, n_data)
+    for k, other in enumerate(others, 1):
+        came = lax.ppermute(other, "dp", [(i, (i + k) % n_data) for i in range(n_data)])
+        weight_grad = weight_grad + came.astype(jnp.float32)
+
+    pooled = jnp.transpose(returned, (1, 0, 2)).reshape(own, tables * WIDTH)
     return (pooled, weight_grad)
 
 

time: 106 us -> 99.5 us (0.939)
  blocking collectives: 20.7 us -> 0 us
  starting transfers between devices: 8.67 us -> 18.3 us
  waiting for transfers between devices: 5.57 us -> 11.7 us
  Pallas kernels: 49.3 us -> 45.9 us
    all_to_all x1 -> x0, blocking collectives: 20.7 us -> none  [body(): lax.all_to_all(rows, 'table', split_axis=0, concat_axis=0, tiled=True)]
    all_to_all x0 -> x1, waiting for transfers between devices: none -> 6.12 us  [body(): lax.all_to_all(rows, 'table', split_axis=0, concat_axis=0, tiled=True)]
    ppermute x0 -> x3, starting transfers between devices: none -> 5.72 us  [body(): lax.ppermute(other, 'dp', [(i, (i + k) % n_data) for i in range(n_data)])]
    pallas_call x2 -> x1, Pallas kernels: 9.38 us -> 5.12 us  [partial_product(): pl.pallas_call(product_kernel, out_shape=[jax.ShapeDtypeStruct((width, hi...]
    all_to_all x0 -> x1, starting transfers between devices: none -> 3.99 us  [body(): lax.all_to_all(rows, 'table', split_axis=0, concat_axis=0, tiled=True)]
    unnamed x10 -> x7, local copies, waits for them, and re-layouts: 4.35 us -> 4.69 us
  transfers between devices with their start and end apart: 3 -> 6, of which waited for: 1 -> 2; matrix products, arithmetic and copies ran while one was open for 4% -> 6% of each run, Pallas kernels for 41% -> 46%
where the time goes in v6:
time: 99.5 us; the launch traced here: 99.1 us
  Pallas kernels  45.9 us (46%)
  starting transfers between devices  18.3 us (18%)
  between operations  14.1 us (14%)
  waiting for transfers between devices  11.7 us (12%)
  local copies, waits for them, and re-layouts  6.09 us (6%)
  other arithmetic  2.87 us (3%)
    pallas_call x1, Pallas kernels, table_rows(): pl.pallas_call(rows_kernel, out_shape=jax.ShapeDtypeStruct((senders, own,...  40.8 us
    all_to_all x1, starting transfers between devices, body(): got = lax.all_to_all(sent, 'table', split_axis=0, concat_axis=0, tiled=True)  8.59 us
    all_to_all x1, waiting for transfers between devices, body(): lax.all_to_all(rows, 'table', split_axis=0, concat_axis=0, tiled=True)  6.12 us
    ppermute x3, starting transfers between devices, body(): lax.ppermute(other, 'dp', [(i, (i + k) % n_data) for i in range(n_data)])  5.72 us
    pallas_call x1, Pallas kernels, partial_product(): pl.pallas_call(product_kernel, out_shape=[jax.ShapeDtypeStruct((width, hi...  5.12 us
    all_to_all x1, waiting for transfers between devices, body(): got = lax.all_to_all(sent, 'table', split_axis=0, concat_axis=0, tiled=True)  4.92 us
    unnamed x7, local copies, waits for them, and re-layouts  4.69 us
    all_to_all x1, starting transfers between devices, body(): lax.all_to_all(rows, 'table', split_axis=0, concat_axis=0, tiled=True)  3.99 us
  transfers between devices with their start and end apart: 6, of which 2 were waited for; matrix products, arithmetic and copies ran while one was open for 6% of the time, Pallas kernels for 46%

profile of v6, /device:TPU:1, one launch (start us, length us, event | category | flops | bytes accessed | tf_op | source)
XLA Modules:
  0.0 99.1 jit_solution(17367599557533671283)
XLA Ops:
  7.2 0.0 all-gather.2.cloned.1.call-start
  7.2 0.7 all-gather.2.cloned.1.call-update
  7.9 1.7 %and_select_fusion = s32[32,3,2,128]{3,2,1,0:T(2,128)} fusion(s32[128,32,3,2]{0,3,2,1:T(2,128)} %param.6, pred[3]{0:T(512)(128)(4,1)S(1)} %iota_compare_fusion.3, s32[32,128]{1,0:T(8,128)} %bitcast.17), kind=kLoop, calls=%fused_computation.10 | loop fusion | flops 73728 | bytes 212995 | tf_op jit(solution)/shard_map/jit(_where)/select_n | solution.py:196
  9.6 8.6 %all-to-all-start = ((s32[32,3,2,128]{3,2,1,0:T(2,128)}), s32[32,3,2,128]{3,2,1,0:T(2,128)S(1)}, u32[]{:S(2)}, u32[]{:S(2)}) async-start(s32[32,3,2,128]{3,2,1,0:T(2,128)} %and_select_fusion), calls=%async_computation | async-start | bytes 196608 | tf_op jit(solution)/shard_map/all_to_all | solution.py:197
  18.2 1.1 %copy.8 = bf16[1,250,512]{1,2,0:T(8,128)(2,1)S(1)} copy(bf16[1,250,512]{2,1,0:T(8,128)(2,1)} %param.8) | data formatting | bytes 512000 | tf_op args[2]
  19.3 0.3 copy.9
  19.6 0.1 copy.11
  19.7 0.4 copy.12
  20.2 0.3 fusion.6.first_ref
  20.4 0.3 fusion.4.last_ref
  20.7 4.9 %all-to-all-done.ids_ref = s32[32,3,2,128]{3,2,1,0:T(2,128)S(1)} async-done(((s32[32,3,2,128]{3,2,1,0:T(2,128)}), s32[32,3,2,128]{3,2,1,0:T(2,128)S(1)}, u32[]{:S(2)}, u32[]{:S(2)}) %all-to-all-start) | async-done | bytes 98336 | tf_op jit(solution)/shard_map/all_to_all | solution.py:197
  25.6 2.2 %copy-done = bf16[1,250,64,128]{3,2,1,0:T(8,128)(2,1)S(1)} copy-done((bf16[1,250,64,128]{3,2,1,0:T(8,128)(2,1)S(1)}, bf16[1,250,64,128]{3,2,1,0:T(8,128)(2,1)}, u32[]{:S(2)}) %copy-start) | copy-done | bytes 4096024
  27.8 40.8 %shard_map.77 = bf16[32,128,128]{2,1,0:T(8,128)(2,1)} custom-call(s32[32,3,2,128]{3,2,1,0:T(2,128)S(1)} %all-to-all-done.ids_ref, f32[258,8,128]{2,1,0:T(8,128)S(1)} %fusion.6.first_ref, bf16[250,64,128]{2,1,0:T(8,128)(2,1)S(1)} %bitcast.11, bf16[250,16,128]{2,1,0:T(8,128)(2,1)S(1)} %fusion.4.last_ref), custom_call_target="tpu_custom_call" | custom-call | flops 16384000000 | bytes 6291456 | tf_op jit(solution)/shard_map/pallas_call | solution.py:109
  68.6 4.0 %all-to-all-start.1 = ((bf16[32,128,128]{2,1,0:T(8,128)(2,1)}), bf16[32,128,128]{2,1,0:T(8,128)(2,1)S(1)}, u32[]{:S(2)}, u32[]{:S(2)}) async-start(bf16[32,128,128]{2,1,0:T(8,128)(2,1)} %shard_map.77), calls=%async_computation.1 | async-start | bytes 2097152 | tf_op jit(solution)/shard_map/all_to_all | solution.py:208
  72.6 0.0 all-gather.2.cloned.1.call-done.grad_ref
  72.6 5.1 %shard_map.78 = (f32[128,256]{1,0:T(8,128)S(1)}, bf16[128,256]{1,0:T(8,128)(2,1)S(1)}, bf16[128,256]{1,0:T(8,128)(2,1)S(1)}, bf16[128,256]{1,0:T(8,128)(2,1)S(1)}) custom-call(s32[1]{0:T(128)} %bitcast.8.place_ref, bf16[4096,128]{1,0:T(8,128)(2,1)} %bitcast.9.rows_ref, bf16[4096,1024]{1,0:T(8,128)(2,1)} %all-gather.2.cloned.1.call-done.grad_ref), custom_call_target="tpu_custom_call" | custom-call | flops 1073741824 | bytes 9437184 | tf_op jit(solution)/shard_map/pallas_call | solution.py:161
  77.7 1.7 %collective-permute-start = (bf16[128,256]{1,0:T(8,128)(2,1)S(1)}, bf16[128,256]{1,0:T(8,128)(2,1)S(1)}, u32[]{:S(2)}, u32[]{:S(2)}) collective-permute-start(bf16[128,256]{1,0:T(8,128)(2,1)S(1)} %get-tuple-element.7), channel_id=1, source_target_pairs={{0,32},{32,64},{64,96},{96,0},{1,33},{33,65},{65,97},{97,1},{2,34}... | collective-permute-start | bytes 196616 | tf_op jit(solution)/shard_map/ppermute | solution.py:213
  79.4 3.3 %collective-permute-start.1 = (bf16[128,256]{1,0:T(8,128)(2,1)S(1)}, bf16[128,256]{1,0:T(8,128)(2,1)S(1)}, u32[]{:S(2)}, u32[]{:S(2)}) collective-permute-start(bf16[128,256]{1,0:T(8,128)(2,1)S(1)} %get-tuple-element.8), channel_id=1, source_target_pairs={{0,64},{32,96},{64,0},{96,32},{1,65},{33,97},{65,1},{97,33},{2,66}... | collective-permute-start | bytes 196616 | tf_op jit(solution)/shard_map/ppermute | solution.py:213
  82.7 0.7 collective-permute-start.2
  83.4 6.1 %all-to-all-done.1 = bf16[32,128,128]{2,1,0:T(8,128)(2,1)S(1)} async-done(((bf16[32,128,128]{2,1,0:T(8,128)(2,1)}), bf16[32,128,128]{2,1,0:T(8,128)(2,1)S(1)}, u32[]{:S(2)}, u32[]{:S(2)}) %all-to-all-start.1) | async-done | bytes 1048608 | tf_op jit(solution)/shard_map/all_to_all | solution.py:208
  89.6 0.7 copy.13
  90.2 1.3 %copy.14 = bf16[128,4096]{1,0:T(8,128)(2,1)} copy(bf16[128,4096]{0,1:T(8,128)(2,1)S(1)} %bitcast.13) | data formatting | bytes 2097152
  91.5 0.0 collective-permute-done
  91.5 0.7 convert_add_fusion
  (6 shorter events, 0.0 us)
Async XLA Ops:
  7.2 12.4 %copy-start.1 = (bf16[1,250,512]{2,1,0:T(8,128)(2,1)S(1)}, bf16[1,250,512]{2,1,0:T(8,128)(2,1)}, u32[]{:S(2)}) copy-start(bf16[1,250,512]{2,1,0:T(8,128)(2,1)} %param.10) | copy-start | bytes 768004
  7.2 65.4 %all-gather.2.cloned.1.call-start = ((), (), s32[]{:S(2)}) async-start(), calls=%async_computation.2 | async-start | bytes 8650752 | tf_op jit(solution)/shard_map/all_gather | solution.py:190
  9.6 16.1 %all-to-all-start = ((s32[32,3,2,128]{3,2,1,0:T(2,128)}), s32[32,3,2,128]{3,2,1,0:T(2,128)S(1)}, u32[]{:S(2)}, u32[]{:S(2)}) async-start(s32[32,3,2,128]{3,2,1,0:T(2,128)} %and_select_fusion), calls=%async_computation | async-start | bytes 196608 | tf_op jit(solution)/shard_map/all_to_all | solution.py:197
  25.6 2.2 %copy-start = (bf16[1,250,64,128]{3,2,1,0:T(8,128)(2,1)S(1)}, bf16[1,250,64,128]{3,2,1,0:T(8,128)(2,1)}, u32[]{:S(2)}) copy-start(bf16[1,250,64,128]{3,2,1,0:T(8,128)(2,1)} %param.9) | copy-start | bytes 12288004
  68.6 21.0 %all-to-all-start.1 = ((bf16[32,128,128]{2,1,0:T(8,128)(2,1)}), bf16[32,128,128]{2,1,0:T(8,128)(2,1)S(1)}, u32[]{:S(2)}, u32[]{:S(2)}) async-start(bf16[32,128,128]{2,1,0:T(8,128)(2,1)} %shard_map.77), calls=%async_computation.1 | async-start | bytes 2097152 | tf_op jit(solution)/shard_map/all_to_all | solution.py:208
  77.7 13.8 %collective-permute-start = (bf16[128,256]{1,0:T(8,128)(2,1)S(1)}, bf16[128,256]{1,0:T(8,128)(2,1)S(1)}, u32[]{:S(2)}, u32[]{:S(2)}) collective-permute-start(bf16[128,256]{1,0:T(8,128)(2,1)S(1)} %get-tuple-element.7), channel_id=1, source_target_pairs={{0,32},{32,64},{64,96},{96,0},{1,33},{33,65},{65,97},{97,1},{2,34}... | collective-permute-start | bytes 196616 | tf_op jit(solution)/shard_map/ppermute | solution.py:213
  79.4 12.2 %collective-permute-start.1 = (bf16[128,256]{1,0:T(8,128)(2,1)S(1)}, bf16[128,256]{1,0:T(8,128)(2,1)S(1)}, u32[]{:S(2)}, u32[]{:S(2)}) collective-permute-start(bf16[128,256]{1,0:T(8,128)(2,1)S(1)} %get-tuple-element.8), channel_id=1, source_target_pairs={{0,64},{32,96},{64,0},{96,32},{1,65},{33,97},{65,1},{97,33},{2,66}... | collective-permute-start | bytes 196616 | tf_op jit(solution)/shard_map/ppermute | solution.py:213
  82.7 8.8 %collective-permute-start.2 = (bf16[128,256]{1,0:T(8,128)(2,1)S(1)}, bf16[128,256]{1,0:T(8,128)(2,1)S(1)}, u32[]{:S(2)}, u32[]{:S(2)}) collective-permute-start(bf16[128,256]{1,0:T(8,128)(2,1)S(1)} %get-tuple-element.9), channel_id=1, source_target_pairs={{0,96},{32,0},{64,32},{96,64},{1,97},{33,1},{65,33},{97,65},{2,98}... | collective-permute-start | bytes 196616 | tf_op jit(solution)/shard_map/ppermute | solution.py:213
Sparse Core Ops, SparseCore 0:
  10.3 56.3 all-gather.1

commit v7 on v6

--- a/solution.py
+++ b/solution.py
@@ -1,3 +1,5 @@
+import functools
+
 import jax
 import jax.numpy as jnp
 from jax import lax
@@ -24,32 +26,29 @@
     row16 = lax.broadcasted_iota(jnp.int32, (16, 128), 0)
     lane16 = lax.broadcasted_iota(jnp.int32, (16, 128), 1)
     keep = ((row16 < 8) == (lane16 < 64)).astype(bf16)
-    zero = jnp.zeros((16, 128), bf16)
     lane = lax.broadcasted_iota(jnp.int32, (8, 128), 1) // 16
 
     def index(i, word, sample):
         return ids_ref[i * per_block + sample // part, word // BAG, word % BAG, sample % part]
 
     def prefixes(i, g):
-        for n in range(0, 8, 2):
-            pair = (n * groups + g, (n + 1) * groups + g)
-            heads, centres = [], []
+        for n in range(0, 8, 4):
+            at = g * 64 + n * 8
             for j in range(BAG):
-                two = [first_ref[index(i, j, a)] for a in pair]
-                heads.append(jnp.concatenate(two, axis=0).astype(bf16) * keep)
-                centres += [middle_ref[index(i, 2 + j, a)] for a in pair]
-            left = jnp.concatenate(
-                [
-                    jnp.concatenate([heads[0], zero], axis=1),
-                    jnp.concatenate([zero, heads[1]], axis=1),
-                ],
-                axis=0,
-            )
-            product = jnp.dot(left, jnp.concatenate(centres, axis=0), preferred_element_type=f32)
-            product = product.astype(bf16)
-            at = g * 64 + n * 8
-            prefix_ref[at : at + 16, :128] = product[:16]
-            prefix_ref[at : at + 16, 128:] = product[16:]
+                left, right = [], []
+                for m in (n, n + 2):
+                    pair = (m * groups + g, (m + 1) * groups + g)
+                    two = [first_ref[index(i, j, a)] for a in pair]
+                    left.append(jnp.concatenate(two, axis=0).astype(bf16) * keep)
+                    two = [middle_ref[index(i, 2 + j, a)] for a in pair]
+                    right.append(jnp.concatenate(two, axis=0))
+                product = jnp.dot(
+                    jnp.concatenate(left, axis=0),
+                    jnp.concatenate(right, axis=1),
+                    preferred_element_type=f32,
+                ).astype(bf16)
+                prefix_ref[at : at + 16, j * 128 : j * 128 + 128] = product[:16, :128]
+                prefix_ref[at + 16 : at + 32, j * 128 : j * 128 + 128] = product[16:, 128:]
 
     def contract(i, g):
         tails = [
@@ -87,19 +86,26 @@
             at = n * groups + h
             out_ref[i * per_block + at // part, at % part : at % part + 8, :] = parts[n].astype(bf16)
 
-    def step(i, carry):
-        now = jnp.minimum(i, blocks - 1)
-        before = jnp.clip(i - 1, 0, blocks - 1)
-        earlier = jnp.clip(i - 2, 0, blocks - 1)
-        for h in range(0, groups, 8):
-            arrange(earlier, h)
+    def step(now, before, earlier):
+        if earlier is not None:
+            for h in range(0, groups, 8):
+                arrange(earlier, h)
         for g in range(0, groups, 2):
-            contract(before, g)
-            prefixes(now, g)
-            prefixes(now, g + 1)
+            if before is not None:
+                contract(before, g)
+            if now is not None:
+                prefixes(now, g)
+                prefixes(now, g + 1)
+
+    def steady(i, carry):
+        step(i, i - 1, i - 2)
         return carry
 
-    lax.fori_loop(0, blocks + 2, step, 0)
+    step(0, None, None)
+    step(1, 0, None)
+    lax.fori_loop(2, blocks, steady, 0, unroll=2)
+    step(None, blocks - 1, blocks - 2)
+    step(None, None, blocks - 1)
 
 
 def table_rows(got, head, middle, tail):
@@ -182,6 +188,44 @@
     )(place, rows, grad)
 
 
+def mask_kernel(ids_ref, lengths_ref, out_ref, *, unused):
+    slot = lax.broadcasted_iota(jnp.int32, ids_ref.shape[:1] + ids_ref.shape[2:], 1)
+    out_ref[:, 1:] = ids_ref[:, 1:]
+    out_ref[:, 0] = jnp.where(slot < lengths_ref[...][:, None, :], ids_ref[:, 0], unused)
+
+
+def masked(ids, lengths, unused):
+    vmem = pl.BlockSpec(memory_space=pltpu.VMEM)
+    return pl.pallas_call(
+        functools.partial(mask_kernel, unused=unused),
+        out_shape=jax.ShapeDtypeStruct(ids.shape, ids.dtype),
+        in_specs=[vmem, vmem],
+        out_specs=vmem,
+    )(ids, lengths)
+
+
+def beside_kernel(blocks_ref, out_ref, sems):
+    tables, _, width = blocks_ref.shape
+    copies = []
+    for t in range(tables):
+        target = out_ref.at[:, pl.ds(t * width, width)]
+        copies.append(pltpu.make_async_copy(blocks_ref.at[t], target, sems.at[t]))
+        copies[-1].start()
+    for copy in copies:
+        copy.wait()
+
+
+def side_by_side(blocks):
+    tables, own, width = blocks.shape
+    return pl.pallas_call(
+        beside_kernel,
+        out_shape=jax.ShapeDtypeStruct((own, tables * width), blocks.dtype),
+        in_specs=[pl.BlockSpec(memory_space=pl.ANY)],
+        out_specs=pl.BlockSpec(memory_space=pl.ANY),
+        scratch_shapes=[pltpu.SemaphoreType.DMA((tables,))],
+    )(blocks)
+
+
 def body(core_ids, bag_lengths, first_core, middle_core, last_core, grad_hidden):
     own, tables = bag_lengths.shape
     ncore = first_core.shape[1]
@@ -189,11 +233,7 @@
 
     gathered = lax.all_gather(grad_hidden, "table", axis=0, tiled=True)
 
-    ids = jnp.transpose(core_ids, (1, 2, 3, 0))
-    lengths = jnp.transpose(bag_lengths)[:, None, None, :]
-    core = lax.broadcasted_iota(jnp.int32, ids.shape, 1)
-    slot = lax.broadcasted_iota(jnp.int32, ids.shape, 2)
-    sent = jnp.where((core == 0) & (slot >= lengths), ncore, ids)
+    sent = masked(jnp.transpose(core_ids, (1, 2, 3, 0)), jnp.transpose(bag_lengths), ncore)
     got = lax.all_to_all(sent, "table", split_axis=0, concat_axis=0, tiled=True)
 
     head = first_core[0].reshape(ncore, D1, RANK).astype(jnp.float32)
@@ -213,7 +253,8 @@
         came = lax.ppermute(other, "dp", [(i, (i + k) % n_data) for i in range(n_data)])
         weight_grad = weight_grad + came.astype(jnp.float32)
 
-    pooled = jnp.transpose(returned, (1, 0, 2)).reshape(own, tables * WIDTH)
+    returned, weight_grad = lax.optimization_barrier((returned, weight_grad))
+    pooled = side_by_side(returned)
     return (pooled, weight_grad)
 
 

time: 99.5 us -> 127 us (1.28)
  Pallas kernels: 45.9 us -> 76.9 us
  other arithmetic: 2.87 us -> 1.21 us
    pallas_call x0 -> x2, Pallas kernels: none -> 34.7 us  [the longest x1 33.1 us: side_by_side(): pl.pallas_call(beside_kernel, out_shape=jax.ShapeDtypeStruct((own, tables...]
    pallas_call x1, Pallas kernels: 40.8 us -> 37 us  [table_rows(): pl.pallas_call(rows_kernel, out_shape=jax.ShapeDtypeStruct((senders, own,...]
    all_to_all x1, waiting for transfers between devices: 6.12 us -> 2.76 us  [body(): lax.all_to_all(rows, 'table', split_axis=0, concat_axis=0, tiled=True)]
    ppermute x3, waiting for transfers between devices: 0.01 us -> 2.68 us  [body(): lax.ppermute(other, 'dp', [(i, (i + k) % n_data) for i in range(n_data)])]
    select_n x1 -> x0, other arithmetic: 1.66 us -> none  [body(): sent = jnp.where((core == 0) & (slot >= lengths), ncore, ids)]
    unnamed x7 -> x8, local copies, waits for them, and re-layouts: 4.69 us -> 4.35 us
  transfers between devices with their start and end apart: 6 -> 6, of which waited for: 2 -> 5; matrix products, arithmetic and copies ran while one was open for 6% -> 2% of each run, Pallas kernels for 46% -> 35%
where the time goes in v7:
time: 127 us
  Pallas kernels  76.9 us (61%)
  starting transfers between devices  18.3 us (14%)
  between operations  14.1 us (11%)
  waiting for transfers between devices  11.1 us (9%)
  local copies, waits for them, and re-layouts  5.09 us (4%)
    pallas_call x1, Pallas kernels, table_rows(): pl.pallas_call(rows_kernel, out_shape=jax.ShapeDtypeStruct((senders, own,...  37 us
    pallas_call x1, Pallas kernels, side_by_side(): pl.pallas_call(beside_kernel, out_shape=jax.ShapeDtypeStruct((own, tables...  33.1 us
    all_to_all x1, starting transfers between devices, body(): got = lax.all_to_all(sent, 'table', split_axis=0, concat_axis=0, tiled=True)  8.59 us
    ppermute x3, starting transfers between devices, body(): lax.ppermute(other, 'dp', [(i, (i + k) % n_data) for i in range(n_data)])  5.71 us
    pallas_call x1, Pallas kernels, partial_product(): pl.pallas_call(product_kernel, out_shape=[jax.ShapeDtypeStruct((width, hi...  5.12 us
    all_to_all x1, waiting for transfers between devices, body(): got = lax.all_to_all(sent, 'table', split_axis=0, concat_axis=0, tiled=True)  4.92 us
    unnamed x8, local copies, waits for them, and re-layouts  4.35 us
    all_to_all x1, starting transfers between devices, body(): lax.all_to_all(rows, 'table', split_axis=0, concat_axis=0, tiled=True)  4 us
  transfers between devices with their start and end apart: 6, of which 5 were waited for; matrix products, arithmetic and copies ran while one was open for 2% of the time, Pallas kernels for 35%

profile of v7, /device:TPU:1, one launch (start us, length us, event | category | flops | bytes accessed | tf_op | source)
XLA Modules:
  0.0 126.7 jit_solution(10038684678964364755)
XLA Ops:
  7.2 0.7 all-gather.2.cloned.1.call-update
  7.9 1.6 %shard_map.77 = s32[32,3,2,128]{3,2,1,0:T(2,128)} custom-call(s32[32,3,2,128]{3,2,1,0:T(2,128)} %bitcast.12, s32[32,128]{1,0:T(8,128)} %bitcast.13), custom_call_target="tpu_custom_call" | custom-call | tf_op jit(solution)/shard_map/pallas_call | solution.py:199
  9.5 8.6 %all-to-all-start = ((s32[32,3,2,128]{3,2,1,0:T(2,128)}), s32[32,3,2,128]{3,2,1,0:T(2,128)S(1)}, u32[]{:S(2)}, u32[]{:S(2)}) async-start(s32[32,3,2,128]{3,2,1,0:T(2,128)} %shard_map.77), calls=%async_computation | async-start | bytes 196608 | tf_op jit(solution)/shard_map/all_to_all | solution.py:237
  18.1 1.1 copy.8
  19.2 0.3 copy.9
  19.5 0.1 copy.11
  19.6 0.4 copy.12
  20.1 0.3 fusion.6.first_ref
  20.3 0.3 fusion.4.last_ref
  20.6 4.9 %all-to-all-done.ids_ref = s32[32,3,2,128]{3,2,1,0:T(2,128)S(1)} async-done(((s32[32,3,2,128]{3,2,1,0:T(2,128)}), s32[32,3,2,128]{3,2,1,0:T(2,128)S(1)}, u32[]{:S(2)}, u32[]{:S(2)}) %all-to-all-start) | async-done | bytes 98336 | tf_op jit(solution)/shard_map/all_to_all | solution.py:237
  25.5 2.2 %copy-done = bf16[1,250,64,128]{3,2,1,0:T(8,128)(2,1)S(1)} copy-done((bf16[1,250,64,128]{3,2,1,0:T(8,128)(2,1)S(1)}, bf16[1,250,64,128]{3,2,1,0:T(8,128)(2,1)}, u32[]{:S(2)}) %copy-start) | copy-done | bytes 4096024
  27.7 37.0 %shard_map.78 = bf16[32,128,128]{2,1,0:T(8,128)(2,1)} custom-call(s32[32,3,2,128]{3,2,1,0:T(2,128)S(1)} %all-to-all-done.ids_ref, f32[258,8,128]{2,1,0:T(8,128)S(1)} %fusion.6.first_ref, bf16[250,64,128]{2,1,0:T(8,128)(2,1)S(1)} %bitcast.8, bf16[250,16,128]{2,1,0:T(8,128)(2,1)S(1)} %fusion.4.last_ref), custom_call_target="tpu_custom_call" | custom-call | flops 16384000000 | bytes 6291456 | tf_op jit(solution)/shard_map/pallas_call | solution.py:115
  64.7 4.0 %all-to-all-start.1 = ((bf16[32,128,128]{2,1,0:T(8,128)(2,1)}), bf16[32,128,128]{2,1,0:T(8,128)(2,1)S(1)}, u32[]{:S(2)}, u32[]{:S(2)}) async-start(bf16[32,128,128]{2,1,0:T(8,128)(2,1)} %shard_map.78), calls=%async_computation.1 | async-start | bytes 2097152 | tf_op jit(solution)/shard_map/all_to_all | solution.py:248
  68.8 5.1 %shard_map.79 = (f32[128,256]{1,0:T(8,128)S(1)}, bf16[128,256]{1,0:T(8,128)(2,1)S(1)}, bf16[128,256]{1,0:T(8,128)(2,1)S(1)}, bf16[128,256]{1,0:T(8,128)(2,1)S(1)}) custom-call(s32[1]{0:T(128)} %bitcast.6.place_ref, bf16[4096,128]{1,0:T(8,128)(2,1)} %bitcast.7.rows_ref, bf16[4096,1024]{1,0:T(8,128)(2,1)} %all-gather.2.cloned.1.call-done.grad_ref), custom_call_target="tpu_custom_call" | custom-call | flops 1073741824 | bytes 9437184 | tf_op jit(solution)/shard_map/pallas_call | solution.py:167
  73.9 1.7 %collective-permute-start = (bf16[128,256]{1,0:T(8,128)(2,1)S(1)}, bf16[128,256]{1,0:T(8,128)(2,1)S(1)}, u32[]{:S(2)}, u32[]{:S(2)}) collective-permute-start(bf16[128,256]{1,0:T(8,128)(2,1)S(1)} %get-tuple-element.9), channel_id=1, source_target_pairs={{0,32},{32,64},{64,96},{96,0},{1,33},{33,65},{65,97},{97,1},{2,34}... | collective-permute-start | bytes 196616 | tf_op jit(solution)/shard_map/ppermute | solution.py:253
  75.6 3.3 %collective-permute-start.1 = (bf16[128,256]{1,0:T(8,128)(2,1)S(1)}, bf16[128,256]{1,0:T(8,128)(2,1)S(1)}, u32[]{:S(2)}, u32[]{:S(2)}) collective-permute-start(bf16[128,256]{1,0:T(8,128)(2,1)S(1)} %get-tuple-element.10), channel_id=1, source_target_pairs={{0,64},{32,96},{64,0},{96,32},{1,65},{33,97},{65,1},{97,33},{2,66}... | collective-permute-start | bytes 196616 | tf_op jit(solution)/shard_map/ppermute | solution.py:253
  78.9 0.7 collective-permute-start.2
  79.6 0.3 collective-permute-done
  79.9 2.3 %collective-permute-done.1 = bf16[128,256]{1,0:T(8,128)(2,1)S(1)} collective-permute-done((bf16[128,256]{1,0:T(8,128)(2,1)S(1)}, bf16[128,256]{1,0:T(8,128)(2,1)S(1)}, u32[]{:S(2)}, u32[]{:S(2)}) %collective-permute-start.1) | collective-permute-done | bytes 65568 | tf_op jit(solution)/shard_map/ppermute | solution.py:253
  82.1 0.1 collective-permute-done.2
  82.3 0.7 convert_add_fusion
  83.0 2.8 %all-to-all-done.1.blocks_ref = bf16[32,128,128]{2,1,0:T(8,128)(2,1)S(1)} async-done(((bf16[32,128,128]{2,1,0:T(8,128)(2,1)}), bf16[32,128,128]{2,1,0:T(8,128)(2,1)S(1)}, u32[]{:S(2)}, u32[]{:S(2)}) %all-to-all-start.1) | async-done | bytes 1048608 | tf_op jit(solution)/shard_map/all_to_all | solution.py:248
  85.7 1.0 copy-done.1
  86.7 33.1 %shard_map.80 = bf16[128,4096]{1,0:T(8,128)(2,1)} custom-call(bf16[32,128,128]{2,1,0:T(8,128)(2,1)} %copy-done.1), custom_call_target="tpu_custom_call" | custom-call | tf_op jit(solution)/shard_map/pallas_call | solution.py:220
  (6 shorter events, 0.1 us)
Async XLA Ops:
  7.2 12.3 %copy-start.2 = (bf16[1,250,512]{2,1,0:T(8,128)(2,1)S(1)}, bf16[1,250,512]{2,1,0:T(8,128)(2,1)}, u32[]{:S(2)}) copy-start(bf16[1,250,512]{2,1,0:T(8,128)(2,1)} %param.10) | copy-start | bytes 768004
  7.2 61.6 %all-gather.2.cloned.1.call-start = ((), (), s32[]{:S(2)}) async-start(), calls=%async_computation.2 | async-start | bytes 8650752 | tf_op jit(solution)/shard_map/all_gather | solution.py:234
  9.5 16.1 %all-to-all-start = ((s32[32,3,2,128]{3,2,1,0:T(2,128)}), s32[32,3,2,128]{3,2,1,0:T(2,128)S(1)}, u32[]{:S(2)}, u32[]{:S(2)}) async-start(s32[32,3,2,128]{3,2,1,0:T(2,128)} %shard_map.77), calls=%async_computation | async-start | bytes 196608 | tf_op jit(solution)/shard_map/all_to_all | solution.py:237
  25.5 2.2 %copy-start = (bf16[1,250,64,128]{3,2,1,0:T(8,128)(2,1)S(1)}, bf16[1,250,64,128]{3,2,1,0:T(8,128)(2,1)}, u32[]{:S(2)}) copy-start(bf16[1,250,64,128]{3,2,1,0:T(8,128)(2,1)} %param.9) | copy-start | bytes 12288004
  64.7 21.0 %all-to-all-start.1 = ((bf16[32,128,128]{2,1,0:T(8,128)(2,1)}), bf16[32,128,128]{2,1,0:T(8,128)(2,1)S(1)}, u32[]{:S(2)}, u32[]{:S(2)}) async-start(bf16[32,128,128]{2,1,0:T(8,128)(2,1)} %shard_map.78), calls=%async_computation.1 | async-start | bytes 2097152 | tf_op jit(solution)/shard_map/all_to_all | solution.py:248
  73.9 6.0 %collective-permute-start = (bf16[128,256]{1,0:T(8,128)(2,1)S(1)}, bf16[128,256]{1,0:T(8,128)(2,1)S(1)}, u32[]{:S(2)}, u32[]{:S(2)}) collective-permute-start(bf16[128,256]{1,0:T(8,128)(2,1)S(1)} %get-tuple-element.9), channel_id=1, source_target_pairs={{0,32},{32,64},{64,96},{96,0},{1,33},{33,65},{65,97},{97,1},{2,34}... | collective-permute-start | bytes 196616 | tf_op jit(solution)/shard_map/ppermute | solution.py:253
  75.6 6.6 %collective-permute-start.1 = (bf16[128,256]{1,0:T(8,128)(2,1)S(1)}, bf16[128,256]{1,0:T(8,128)(2,1)S(1)}, u32[]{:S(2)}, u32[]{:S(2)}) collective-permute-start(bf16[128,256]{1,0:T(8,128)(2,1)S(1)} %get-tuple-element.10), channel_id=1, source_target_pairs={{0,64},{32,96},{64,0},{96,32},{1,65},{33,97},{65,1},{97,33},{2,66}... | collective-permute-start | bytes 196616 | tf_op jit(solution)/shard_map/ppermute | solution.py:253
  78.9 3.4 %collective-permute-start.2 = (bf16[128,256]{1,0:T(8,128)(2,1)S(1)}, bf16[128,256]{1,0:T(8,128)(2,1)S(1)}, u32[]{:S(2)}, u32[]{:S(2)}) collective-permute-start(bf16[128,256]{1,0:T(8,128)(2,1)S(1)} %get-tuple-element.11), channel_id=1, source_target_pairs={{0,96},{32,0},{64,32},{96,64},{1,97},{33,1},{65,33},{97,65},{2,98}... | collective-permute-start | bytes 196616 | tf_op jit(solution)/shard_map/ppermute | solution.py:253
  85.7 1.0 copy-start.1
Sparse Core Ops, SparseCore 0:
  10.3 56.3 all-gather.1

commit v8 on v7

--- a/solution.py
+++ b/solution.py
@@ -201,15 +201,19 @@
         out_shape=jax.ShapeDtypeStruct(ids.shape, ids.dtype),
         in_specs=[vmem, vmem],
         out_specs=vmem,
+        compiler_params=pltpu.CompilerParams(vmem_limit_bytes=2 << 20),
     )(ids, lengths)
 
 
-def beside_kernel(blocks_ref, out_ref, sems):
+def beside_kernel(blocks_ref, out_ref, rows_ref, sems):
     tables, _, width = blocks_ref.shape
+    pieces, size, _ = rows_ref.shape
     copies = []
-    for t in range(tables):
-        target = out_ref.at[:, pl.ds(t * width, width)]
-        copies.append(pltpu.make_async_copy(blocks_ref.at[t], target, sems.at[t]))
+    for p in range(pieces):
+        for t in range(tables):
+            rows_ref[p, :, t * width : (t + 1) * width] = blocks_ref[t, p * size : (p + 1) * size]
+        target = out_ref.at[pl.ds(p * size, size)]
+        copies.append(pltpu.make_async_copy(rows_ref.at[p], target, sems.at[p]))
         copies[-1].start()
     for copy in copies:
         copy.wait()
@@ -217,12 +221,17 @@
 
 def side_by_side(blocks):
     tables, own, width = blocks.shape
+    pieces = own // 16
     return pl.pallas_call(
         beside_kernel,
         out_shape=jax.ShapeDtypeStruct((own, tables * width), blocks.dtype),
-        in_specs=[pl.BlockSpec(memory_space=pl.ANY)],
+        in_specs=[pl.BlockSpec(memory_space=pltpu.VMEM)],
         out_specs=pl.BlockSpec(memory_space=pl.ANY),
-        scratch_shapes=[pltpu.SemaphoreType.DMA((tables,))],
+        scratch_shapes=[
+            pltpu.VMEM((pieces, own // pieces, tables * width), blocks.dtype),
+            pltpu.SemaphoreType.DMA((pieces,)),
+        ],
+        compiler_params=pltpu.CompilerParams(vmem_limit_bytes=4 << 20),
     )(blocks)
 
 

time: 127 us -> 94.8 us (0.75)
  Pallas kernels: 76.9 us -> 43.9 us
    pallas_call x1, Pallas kernels: 33.1 us -> 1.05 us  [side_by_side(): pl.pallas_call(beside_kernel, out_shape=jax.ShapeDtypeStruct((own, tables...]
    unnamed x8 -> x10, local copies, waits for them, and re-layouts: 4.35 us -> 4.98 us
  transfers between devices with their start and end apart: 6 -> 6, of which waited for: 5 -> 5; matrix products, arithmetic and copies ran while one was open for 2% -> 3% of each run, Pallas kernels for 35% -> 45%
where the time goes in v8:
time: 94.8 us; the launch traced here: 94.4 us
  Pallas kernels  43.9 us (46%)
  starting transfers between devices  18.3 us (19%)
  between operations  14.2 us (15%)
  waiting for transfers between devices  11 us (12%)
  local copies, waits for them, and re-layouts  5.72 us (6%)
  other arithmetic  1.21 us (1%)
    pallas_call x1, Pallas kernels, table_rows(): pl.pallas_call(rows_kernel, out_shape=jax.ShapeDtypeStruct((senders, own,...  37.1 us
    all_to_all x1, starting transfers between devices, body(): got = lax.all_to_all(sent, 'table', split_axis=0, concat_axis=0, tiled=True)  8.59 us
    ppermute x3, starting transfers between devices, body(): lax.ppermute(other, 'dp', [(i, (i + k) % n_data) for i in range(n_data)])  5.72 us
    pallas_call x1, Pallas kernels, partial_product(): pl.pallas_call(product_kernel, out_shape=[jax.ShapeDtypeStruct((width, hi...  5.12 us
    unnamed x10, local copies, waits for them, and re-layouts  4.98 us
    all_to_all x1, waiting for transfers between devices, body(): got = lax.all_to_all(sent, 'table', split_axis=0, concat_axis=0, tiled=True)  4.92 us
    all_to_all x1, starting transfers between devices, body(): lax.all_to_all(rows, 'table', split_axis=0, concat_axis=0, tiled=True)  3.98 us
    all_to_all x1, waiting for transfers between devices, body(): lax.all_to_all(rows, 'table', split_axis=0, concat_axis=0, tiled=True)  2.74 us
  transfers between devices with their start and end apart: 6, of which 5 were waited for; matrix products, arithmetic and copies ran while one was open for 3% of the time, Pallas kernels for 45%

profile of v8, /device:TPU:1, one launch (start us, length us, event | category | flops | bytes accessed | tf_op | source)
XLA Modules:
  0.0 94.4 jit_solution(8957780995505327617)
XLA Ops:
  7.2 0.7 all-gather.2.cloned.1.call-update
  7.9 0.9 copy-done
  8.8 0.7 copy-done.1
  9.5 0.7 shard_map.77
  10.2 8.6 %all-to-all-start = ((s32[32,3,2,128]{3,2,1,0:T(2,128)}), s32[32,3,2,128]{3,2,1,0:T(2,128)S(1)}, u32[]{:S(2)}, u32[]{:S(2)}) async-start(s32[32,3,2,128]{3,2,1,0:T(2,128)} %shard_map.77), calls=%async_computation | async-start | bytes 196608 | tf_op jit(solution)/shard_map/all_to_all | solution.py:246
  18.8 1.1 %copy.8 = bf16[1,250,512]{1,2,0:T(8,128)(2,1)S(1)} copy(bf16[1,250,512]{2,1,0:T(8,128)(2,1)} %param.8) | data formatting | bytes 512000 | tf_op args[2]
  19.9 0.3 copy.9
  20.4 0.4 copy.12
  20.8 0.3 fusion.6.first_ref
  21.1 0.3 fusion.4.last_ref
  21.3 4.9 %all-to-all-done.ids_ref = s32[32,3,2,128]{3,2,1,0:T(2,128)S(1)} async-done(((s32[32,3,2,128]{3,2,1,0:T(2,128)}), s32[32,3,2,128]{3,2,1,0:T(2,128)S(1)}, u32[]{:S(2)}, u32[]{:S(2)}) %all-to-all-start) | async-done | bytes 98336 | tf_op jit(solution)/shard_map/all_to_all | solution.py:246
  26.2 2.2 %copy-done.2 = bf16[1,250,64,128]{3,2,1,0:T(8,128)(2,1)S(1)} copy-done((bf16[1,250,64,128]{3,2,1,0:T(8,128)(2,1)S(1)}, bf16[1,250,64,128]{3,2,1,0:T(8,128)(2,1)}, u32[]{:S(2)}) %copy-start.2) | copy-done | bytes 4096024
  28.4 37.1 %shard_map.78 = bf16[32,128,128]{2,1,0:T(8,128)(2,1)} custom-call(s32[32,3,2,128]{3,2,1,0:T(2,128)S(1)} %all-to-all-done.ids_ref, f32[258,8,128]{2,1,0:T(8,128)S(1)} %fusion.6.first_ref, bf16[250,64,128]{2,1,0:T(8,128)(2,1)S(1)} %bitcast.10, bf16[250,16,128]{2,1,0:T(8,128)(2,1)S(1)} %fusion.4.last_ref), custom_call_target="tpu_custom_call" | custom-call | flops 16384000000 | bytes 6291456 | tf_op jit(solution)/shard_map/pallas_call | solution.py:115
  65.5 4.0 %all-to-all-start.1 = ((bf16[32,128,128]{2,1,0:T(8,128)(2,1)}), bf16[32,128,128]{2,1,0:T(8,128)(2,1)S(1)}, u32[]{:S(2)}, u32[]{:S(2)}) async-start(bf16[32,128,128]{2,1,0:T(8,128)(2,1)} %shard_map.78), calls=%async_computation.1 | async-start | bytes 2097152 | tf_op jit(solution)/shard_map/all_to_all | solution.py:257
  69.5 5.1 %shard_map.79 = (f32[128,256]{1,0:T(8,128)S(1)}, bf16[128,256]{1,0:T(8,128)(2,1)S(1)}, bf16[128,256]{1,0:T(8,128)(2,1)S(1)}, bf16[128,256]{1,0:T(8,128)(2,1)S(1)}) custom-call(s32[1]{0:T(128)} %bitcast.6.place_ref, bf16[4096,128]{1,0:T(8,128)(2,1)} %bitcast.7.rows_ref, bf16[4096,1024]{1,0:T(8,128)(2,1)} %all-gather.2.cloned.1.call-done.grad_ref), custom_call_target="tpu_custom_call" | custom-call | flops 1073741824 | bytes 9437184 | tf_op jit(solution)/shard_map/pallas_call | solution.py:167
  74.6 1.7 %collective-permute-start = (bf16[128,256]{1,0:T(8,128)(2,1)S(1)}, bf16[128,256]{1,0:T(8,128)(2,1)S(1)}, u32[]{:S(2)}, u32[]{:S(2)}) collective-permute-start(bf16[128,256]{1,0:T(8,128)(2,1)S(1)} %get-tuple-element.9), channel_id=1, source_target_pairs={{0,32},{32,64},{64,96},{96,0},{1,33},{33,65},{65,97},{97,1},{2,34}... | collective-permute-start | bytes 196616 | tf_op jit(solution)/shard_map/ppermute | solution.py:262
  76.3 3.3 %collective-permute-start.1 = (bf16[128,256]{1,0:T(8,128)(2,1)S(1)}, bf16[128,256]{1,0:T(8,128)(2,1)S(1)}, u32[]{:S(2)}, u32[]{:S(2)}) collective-permute-start(bf16[128,256]{1,0:T(8,128)(2,1)S(1)} %get-tuple-element.10), channel_id=1, source_target_pairs={{0,64},{32,96},{64,0},{96,32},{1,65},{33,97},{65,1},{97,33},{2,66}... | collective-permute-start | bytes 196616 | tf_op jit(solution)/shard_map/ppermute | solution.py:262
  79.6 0.7 collective-permute-start.2
  80.3 0.3 collective-permute-done
  80.6 2.3 %collective-permute-done.1 = bf16[128,256]{1,0:T(8,128)(2,1)S(1)} collective-permute-done((bf16[128,256]{1,0:T(8,128)(2,1)S(1)}, bf16[128,256]{1,0:T(8,128)(2,1)S(1)}, u32[]{:S(2)}, u32[]{:S(2)}) %collective-permute-start.1) | collective-permute-done | bytes 65568 | tf_op jit(solution)/shard_map/ppermute | solution.py:262
  82.9 0.1 collective-permute-done.2
  83.0 0.7 convert_add_fusion
  83.7 2.7 %all-to-all-done.1.blocks_ref = bf16[32,128,128]{2,1,0:T(8,128)(2,1)S(1)} async-done(((bf16[32,128,128]{2,1,0:T(8,128)(2,1)}), bf16[32,128,128]{2,1,0:T(8,128)(2,1)S(1)}, u32[]{:S(2)}, u32[]{:S(2)}) %all-to-all-start.1) | async-done | bytes 1048608 | tf_op jit(solution)/shard_map/all_to_all | solution.py:257
  86.5 1.0 %shard_map.80 = bf16[128,4096]{1,0:T(8,128)(2,1)} custom-call(bf16[32,128,128]{2,1,0:T(8,128)(2,1)S(1)} %all-to-all-done.1.blocks_ref), custom_call_target="tpu_custom_call" | custom-call | tf_op jit(solution)/shard_map/pallas_call | solution.py:225
  (8 shorter events, 0.2 us)
Async XLA Ops:
  7.2 13.1 %copy-start.3 = (bf16[1,250,512]{2,1,0:T(8,128)(2,1)S(1)}, bf16[1,250,512]{2,1,0:T(8,128)(2,1)}, u32[]{:S(2)}) copy-start(bf16[1,250,512]{2,1,0:T(8,128)(2,1)} %param.10) | copy-start | bytes 768004
  7.2 62.3 %all-gather.2.cloned.1.call-start = ((), (), s32[]{:S(2)}) async-start(), calls=%async_computation.2 | async-start | bytes 8650752 | tf_op jit(solution)/shard_map/all_gather | solution.py:243
  7.9 0.9 copy-start
  8.8 0.7 copy-start.1
  10.2 16.0 %all-to-all-start = ((s32[32,3,2,128]{3,2,1,0:T(2,128)}), s32[32,3,2,128]{3,2,1,0:T(2,128)S(1)}, u32[]{:S(2)}, u32[]{:S(2)}) async-start(s32[32,3,2,128]{3,2,1,0:T(2,128)} %shard_map.77), calls=%async_computation | async-start | bytes 196608 | tf_op jit(solution)/shard_map/all_to_all | solution.py:246
  26.2 2.2 %copy-start.2 = (bf16[1,250,64,128]{3,2,1,0:T(8,128)(2,1)S(1)}, bf16[1,250,64,128]{3,2,1,0:T(8,128)(2,1)}, u32[]{:S(2)}) copy-start(bf16[1,250,64,128]{3,2,1,0:T(8,128)(2,1)} %param.9) | copy-start | bytes 12288004
  65.5 21.0 %all-to-all-start.1 = ((bf16[32,128,128]{2,1,0:T(8,128)(2,1)}), bf16[32,128,128]{2,1,0:T(8,128)(2,1)S(1)}, u32[]{:S(2)}, u32[]{:S(2)}) async-start(bf16[32,128,128]{2,1,0:T(8,128)(2,1)} %shard_map.78), calls=%async_computation.1 | async-start | bytes 2097152 | tf_op jit(solution)/shard_map/all_to_all | solution.py:257
  74.6 6.0 %collective-permute-start = (bf16[128,256]{1,0:T(8,128)(2,1)S(1)}, bf16[128,256]{1,0:T(8,128)(2,1)S(1)}, u32[]{:S(2)}, u32[]{:S(2)}) collective-permute-start(bf16[128,256]{1,0:T(8,128)(2,1)S(1)} %get-tuple-element.9), channel_id=1, source_target_pairs={{0,32},{32,64},{64,96},{96,0},{1,33},{33,65},{65,97},{97,1},{2,34}... | collective-permute-start | bytes 196616 | tf_op jit(solution)/shard_map/ppermute | solution.py:262
  76.3 6.6 %collective-permute-start.1 = (bf16[128,256]{1,0:T(8,128)(2,1)S(1)}, bf16[128,256]{1,0:T(8,128)(2,1)S(1)}, u32[]{:S(2)}, u32[]{:S(2)}) collective-permute-start(bf16[128,256]{1,0:T(8,128)(2,1)S(1)} %get-tuple-element.10), channel_id=1, source_target_pairs={{0,64},{32,96},{64,0},{96,32},{1,65},{33,97},{65,1},{97,33},{2,66}... | collective-permute-start | bytes 196616 | tf_op jit(solution)/shard_map/ppermute | solution.py:262
  79.6 3.4 %collective-permute-start.2 = (bf16[128,256]{1,0:T(8,128)(2,1)S(1)}, bf16[128,256]{1,0:T(8,128)(2,1)S(1)}, u32[]{:S(2)}, u32[]{:S(2)}) collective-permute-start(bf16[128,256]{1,0:T(8,128)(2,1)S(1)} %get-tuple-element.11), channel_id=1, source_target_pairs={{0,96},{32,0},{64,32},{96,64},{1,97},{33,1},{65,33},{97,65},{2,98}... | collective-permute-start | bytes 196616 | tf_op jit(solution)/shard_map/ppermute | solution.py:262
Sparse Core Ops, SparseCore 0:
  10.3 56.3 all-gather.1

commit v9 on v8

--- a/solution.py
+++ b/solution.py
@@ -14,9 +14,12 @@
 BAG = 2
 WIDTH = D1 * D2 * D3
 BLOCK = 128
-
-
-def rows_kernel(ids_ref, first_ref, middle_ref, last_ref, out_ref, prefix_ref, mixed_ref):
+FETCHES = 5
+
+
+def rows_kernel(
+    got_ref, first_ref, core_ref, last_ref, out_ref, prefix_ref, mixed_ref, middle_ref, ids_ref, sems
+):
     f32 = jnp.float32
     bf16 = jnp.bfloat16
     senders, part, _ = out_ref.shape
@@ -27,6 +30,18 @@
     lane16 = lax.broadcasted_iota(jnp.int32, (16, 128), 1)
     keep = ((row16 < 8) == (lane16 < 64)).astype(bf16)
     lane = lax.broadcasted_iota(jnp.int32, (8, 128), 1) // 16
+
+    size = core_ref.shape[0] // FETCHES
+    copies = [pltpu.make_async_copy(got_ref, ids_ref, sems.at[FETCHES])]
+    for f in range(FETCHES):
+        part_of = pl.ds(f * size, size)
+        copies.append(
+            pltpu.make_async_copy(core_ref.at[part_of], middle_ref.at[part_of], sems.at[f])
+        )
+    for copy in copies:
+        copy.start()
+    for copy in copies:
+        copy.wait()
 
     def index(i, word, sample):
         return ids_ref[i * per_block + sample // part, word // BAG, word % BAG, sample % part]
@@ -115,13 +130,16 @@
     return pl.pallas_call(
         rows_kernel,
         out_shape=jax.ShapeDtypeStruct((senders, own, WIDTH), jnp.bfloat16),
-        in_specs=[pl.BlockSpec(memory_space=pltpu.SMEM), vmem, vmem, vmem],
+        in_specs=[pl.BlockSpec(memory_space=pl.ANY), vmem, pl.BlockSpec(memory_space=pl.ANY), vmem],
         out_specs=vmem,
         scratch_shapes=[
             pltpu.VMEM((BLOCK * 8, 256), jnp.bfloat16),
             pltpu.VMEM((BLOCK, 128), jnp.float32),
+            pltpu.VMEM(middle.shape, middle.dtype),
+            pltpu.SMEM(got.shape, got.dtype),
+            pltpu.SemaphoreType.DMA((FETCHES + 1,)),
         ],
-        compiler_params=pltpu.CompilerParams(vmem_limit_bytes=32 << 20),
+        compiler_params=pltpu.CompilerParams(vmem_limit_bytes=50 << 20),
         cost_estimate=pl.CostEstimate(
             flops=lookups * 2000000, bytes_accessed=6 << 20, transcendentals=0
         ),
@@ -201,7 +219,6 @@
         out_shape=jax.ShapeDtypeStruct(ids.shape, ids.dtype),
         in_specs=[vmem, vmem],
         out_specs=vmem,
-        compiler_params=pltpu.CompilerParams(vmem_limit_bytes=2 << 20),
     )(ids, lengths)
 
 

time: 94.8 us -> 92.5 us (0.976)
  local copies, waits for them, and re-layouts: 5.72 us -> 1.96 us
  Pallas kernels: 43.9 us -> 45.4 us
    unnamed x10 -> x4, local copies, waits for them, and re-layouts: 4.98 us -> 1.22 us
  transfers between devices with their start and end apart: 6 -> 6, of which waited for: 5 -> 5; matrix products, arithmetic and copies ran while one was open for 3% -> 3% of each run, Pallas kernels for 45% -> 48%
where the time goes in v9:
time: 92.5 us; the launch traced here: 92.1 us
  Pallas kernels  45.4 us (49%)
  starting transfers between devices  18.3 us (20%)
  between operations  14.2 us (15%)
  waiting for transfers between devices  11 us (12%)
  local copies, waits for them, and re-layouts  1.96 us (2%)
  other arithmetic  1.21 us (1%)
    pallas_call x1, Pallas kernels, table_rows(): pl.pallas_call(rows_kernel, out_shape=jax.ShapeDtypeStruct((senders, own,...  37.7 us
    all_to_all x1, starting transfers between devices, body(): got = lax.all_to_all(sent, 'table', split_axis=0, concat_axis=0, tiled=True)  8.59 us
    ppermute x3, starting transfers between devices, body(): lax.ppermute(other, 'dp', [(i, (i + k) % n_data) for i in range(n_data)])  5.76 us
    pallas_call x1, Pallas kernels, partial_product(): pl.pallas_call(product_kernel, out_shape=[jax.ShapeDtypeStruct((width, hi...  5.12 us
    all_to_all x1, waiting for transfers between devices, body(): got = lax.all_to_all(sent, 'table', split_axis=0, concat_axis=0, tiled=True)  4.92 us
    all_to_all x1, starting transfers between devices, body(): lax.all_to_all(rows, 'table', split_axis=0, concat_axis=0, tiled=True)  3.95 us
    ppermute x3, waiting for transfers between devices, body(): lax.ppermute(other, 'dp', [(i, (i + k) % n_data) for i in range(n_data)])  2.71 us
    all_to_all x1, waiting for transfers between devices, body(): lax.all_to_all(rows, 'table', split_axis=0, concat_axis=0, tiled=True)  2.67 us
  transfers between devices with their start and end apart: 6, of which 5 were waited for; matrix products, arithmetic and copies ran while one was open for 3% of the time, Pallas kernels for 48%

profile of v9, /device:TPU:1, one launch (start us, length us, event | category | flops | bytes accessed | tf_op | source)
XLA Modules:
  0.0 92.1 jit_solution(15505974169739925357)
XLA Ops:
  7.2 0.0 all-gather.2.cloned.1.call-start
  7.2 0.7 all-gather.2.cloned.1.call-update
  7.9 1.6 %shard_map.77 = s32[32,3,2,128]{3,2,1,0:T(2,128)} custom-call(s32[32,3,2,128]{3,2,1,0:T(2,128)} %bitcast.11, s32[32,128]{1,0:T(8,128)} %bitcast.12), custom_call_target="tpu_custom_call" | custom-call | tf_op jit(solution)/shard_map/pallas_call | solution.py:217
  9.5 8.6 %all-to-all-start = ((s32[32,3,2,128]{3,2,1,0:T(2,128)}), s32[32,3,2,128]{3,2,1,0:T(2,128)S(1)}, u32[]{:S(2)}, u32[]{:S(2)}) async-start(s32[32,3,2,128]{3,2,1,0:T(2,128)} %shard_map.77), calls=%async_computation | async-start | bytes 196608 | tf_op jit(solution)/shard_map/all_to_all | solution.py:263
  18.1 1.1 %copy.8 = bf16[1,250,512]{1,2,0:T(8,128)(2,1)S(1)} copy(bf16[1,250,512]{2,1,0:T(8,128)(2,1)} %param.8) | data formatting | bytes 512000 | tf_op args[2]
  19.2 0.3 copy.9
  19.5 0.1 copy.11
  19.6 0.4 copy.12
  20.1 0.3 fusion.6.first_ref
  20.3 0.3 fusion.4.last_ref
  20.6 4.9 %all-to-all-done.got_ref = s32[32,3,2,128]{3,2,1,0:T(2,128)S(1)} async-done(((s32[32,3,2,128]{3,2,1,0:T(2,128)}), s32[32,3,2,128]{3,2,1,0:T(2,128)S(1)}, u32[]{:S(2)}, u32[]{:S(2)}) %all-to-all-start) | async-done | bytes 98336 | tf_op jit(solution)/shard_map/all_to_all | solution.py:263
  25.5 37.7 %shard_map.78 = bf16[32,128,128]{2,1,0:T(8,128)(2,1)} custom-call(s32[32,3,2,128]{3,2,1,0:T(2,128)S(1)} %all-to-all-done.got_ref, f32[258,8,128]{2,1,0:T(8,128)S(1)} %fusion.6.first_ref, bf16[250,64,128]{2,1,0:T(8,128)(2,1)} %bitcast.13, bf16[250,16,128]{2,1,0:T(8,128)(2,1)S(1)} %fusion.4.last_ref), custom_call_target="tpu_custom_call" | custom-call | flops 16384000000 | bytes 6291456 | tf_op jit(solution)/shard_map/pallas_call | solution.py:130
  63.2 4.0 %all-to-all-start.1 = ((bf16[32,128,128]{2,1,0:T(8,128)(2,1)}), bf16[32,128,128]{2,1,0:T(8,128)(2,1)S(1)}, u32[]{:S(2)}, u32[]{:S(2)}) async-start(bf16[32,128,128]{2,1,0:T(8,128)(2,1)} %shard_map.78), calls=%async_computation.1 | async-start | bytes 2097152 | tf_op jit(solution)/shard_map/all_to_all | solution.py:274
  67.2 0.0 all-gather.2.cloned.1.call-done.grad_ref
  67.2 5.1 %shard_map.79 = (f32[128,256]{1,0:T(8,128)S(1)}, bf16[128,256]{1,0:T(8,128)(2,1)S(1)}, bf16[128,256]{1,0:T(8,128)(2,1)S(1)}, bf16[128,256]{1,0:T(8,128)(2,1)S(1)}) custom-call(s32[1]{0:T(128)} %bitcast.6.place_ref, bf16[4096,128]{1,0:T(8,128)(2,1)} %bitcast.7.rows_ref, bf16[4096,1024]{1,0:T(8,128)(2,1)} %all-gather.2.cloned.1.call-done.grad_ref), custom_call_target="tpu_custom_call" | custom-call | flops 1073741824 | bytes 9437184 | tf_op jit(solution)/shard_map/pallas_call | solution.py:185
  72.4 1.7 %collective-permute-start = (bf16[128,256]{1,0:T(8,128)(2,1)S(1)}, bf16[128,256]{1,0:T(8,128)(2,1)S(1)}, u32[]{:S(2)}, u32[]{:S(2)}) collective-permute-start(bf16[128,256]{1,0:T(8,128)(2,1)S(1)} %get-tuple-element.9), channel_id=1, source_target_pairs={{0,32},{32,64},{64,96},{96,0},{1,33},{33,65},{65,97},{97,1},{2,34}... | collective-permute-start | bytes 196616 | tf_op jit(solution)/shard_map/ppermute | solution.py:279
  74.1 3.3 %collective-permute-start.1 = (bf16[128,256]{1,0:T(8,128)(2,1)S(1)}, bf16[128,256]{1,0:T(8,128)(2,1)S(1)}, u32[]{:S(2)}, u32[]{:S(2)}) collective-permute-start(bf16[128,256]{1,0:T(8,128)(2,1)S(1)} %get-tuple-element.10), channel_id=1, source_target_pairs={{0,64},{32,96},{64,0},{96,32},{1,65},{33,97},{65,1},{97,33},{2,66}... | collective-permute-start | bytes 196616 | tf_op jit(solution)/shard_map/ppermute | solution.py:279
  77.4 0.7 collective-permute-start.2
  78.1 0.3 collective-permute-done
  78.4 2.3 %collective-permute-done.1 = bf16[128,256]{1,0:T(8,128)(2,1)S(1)} collective-permute-done((bf16[128,256]{1,0:T(8,128)(2,1)S(1)}, bf16[128,256]{1,0:T(8,128)(2,1)S(1)}, u32[]{:S(2)}, u32[]{:S(2)}) %collective-permute-start.1) | collective-permute-done | bytes 65568 | tf_op jit(solution)/shard_map/ppermute | solution.py:279
  80.7 0.1 collective-permute-done.2
  80.8 0.7 convert_add_fusion
  81.5 2.7 %all-to-all-done.1.blocks_ref = bf16[32,128,128]{2,1,0:T(8,128)(2,1)S(1)} async-done(((bf16[32,128,128]{2,1,0:T(8,128)(2,1)}), bf16[32,128,128]{2,1,0:T(8,128)(2,1)S(1)}, u32[]{:S(2)}, u32[]{:S(2)}) %all-to-all-start.1) | async-done | bytes 1048608 | tf_op jit(solution)/shard_map/all_to_all | solution.py:274
  84.2 1.0 %shard_map.80 = bf16[128,4096]{1,0:T(8,128)(2,1)} custom-call(bf16[32,128,128]{2,1,0:T(8,128)(2,1)S(1)} %all-to-all-done.1.blocks_ref), custom_call_target="tpu_custom_call" | custom-call | tf_op jit(solution)/shard_map/pallas_call | solution.py:242
  (2 shorter events, 0.0 us)
Async XLA Ops:
  7.2 12.3 %copy-start = (bf16[1,250,512]{2,1,0:T(8,128)(2,1)S(1)}, bf16[1,250,512]{2,1,0:T(8,128)(2,1)}, u32[]{:S(2)}) copy-start(bf16[1,250,512]{2,1,0:T(8,128)(2,1)} %param.10) | copy-start | bytes 768004
  7.2 60.0 %all-gather.2.cloned.1.call-start = ((), (), s32[]{:S(2)}) async-start(), calls=%async_computation.2 | async-start | bytes 8650752 | tf_op jit(solution)/shard_map/all_gather | solution.py:260
  9.5 16.1 %all-to-all-start = ((s32[32,3,2,128]{3,2,1,0:T(2,128)}), s32[32,3,2,128]{3,2,1,0:T(2,128)S(1)}, u32[]{:S(2)}, u32[]{:S(2)}) async-start(s32[32,3,2,128]{3,2,1,0:T(2,128)} %shard_map.77), calls=%async_computation | async-start | bytes 196608 | tf_op jit(solution)/shard_map/all_to_all | solution.py:263
  63.2 21.0 %all-to-all-start.1 = ((bf16[32,128,128]{2,1,0:T(8,128)(2,1)}), bf16[32,128,128]{2,1,0:T(8,128)(2,1)S(1)}, u32[]{:S(2)}, u32[]{:S(2)}) async-start(bf16[32,128,128]{2,1,0:T(8,128)(2,1)} %shard_map.78), calls=%async_computation.1 | async-start | bytes 2097152 | tf_op jit(solution)/shard_map/all_to_all | solution.py:274
  72.4 6.1 %collective-permute-start = (bf16[128,256]{1,0:T(8,128)(2,1)S(1)}, bf16[128,256]{1,0:T(8,128)(2,1)S(1)}, u32[]{:S(2)}, u32[]{:S(2)}) collective-permute-start(bf16[128,256]{1,0:T(8,128)(2,1)S(1)} %get-tuple-element.9), channel_id=1, source_target_pairs={{0,32},{32,64},{64,96},{96,0},{1,33},{33,65},{65,97},{97,1},{2,34}... | collective-permute-start | bytes 196616 | tf_op jit(solution)/shard_map/ppermute | solution.py:279
  74.1 6.6 %collective-permute-start.1 = (bf16[128,256]{1,0:T(8,128)(2,1)S(1)}, bf16[128,256]{1,0:T(8,128)(2,1)S(1)}, u32[]{:S(2)}, u32[]{:S(2)}) collective-permute-start(bf16[128,256]{1,0:T(8,128)(2,1)S(1)} %get-tuple-element.10), channel_id=1, source_target_pairs={{0,64},{32,96},{64,0},{96,32},{1,65},{33,97},{65,1},{97,33},{2,66}... | collective-permute-start | bytes 196616 | tf_op jit(solution)/shard_map/ppermute | solution.py:279
  77.4 3.4 %collective-permute-start.2 = (bf16[128,256]{1,0:T(8,128)(2,1)S(1)}, bf16[128,256]{1,0:T(8,128)(2,1)S(1)}, u32[]{:S(2)}, u32[]{:S(2)}) collective-permute-start(bf16[128,256]{1,0:T(8,128)(2,1)S(1)} %get-tuple-element.11), channel_id=1, source_target_pairs={{0,96},{32,0},{64,32},{96,64},{1,97},{33,1},{65,33},{97,65},{2,98}... | collective-permute-start | bytes 196616 | tf_op jit(solution)/shard_map/ppermute | solution.py:279
Sparse Core Ops, SparseCore 0:
  10.3 56.3 all-gather.1

commit v10 on v9

--- a/solution.py
+++ b/solution.py
@@ -118,7 +118,7 @@
 
     step(0, None, None)
     step(1, 0, None)
-    lax.fori_loop(2, blocks, steady, 0, unroll=2)
+    lax.fori_loop(2, blocks, steady, 0, unroll=5)
     step(None, blocks - 1, blocks - 2)
     step(None, None, blocks - 1)
 

time: 92.5 us -> 91.8 us (level)
  transfers between devices with their start and end apart: 6 -> 6, of which waited for: 5 -> 6; matrix products, arithmetic and copies ran while one was open for 3% -> 3% of each run, Pallas kernels for 48% -> 48%
where the time goes in v10:
time: 91.8 us; the launch traced here: 91.5 us
  Pallas kernels  44.7 us (49%)
  starting transfers between devices  18.3 us (20%)
  between operations  14.1 us (15%)
  waiting for transfers between devices  11.2 us (12%)
  local copies, waits for them, and re-layouts  1.96 us (2%)
  other arithmetic  1.21 us (1%)
    pallas_call x1, Pallas kernels, table_rows(): pl.pallas_call(rows_kernel, out_shape=jax.ShapeDtypeStruct((senders, own,...  37 us
    all_to_all x1, starting transfers between devices, body(): got = lax.all_to_all(sent, 'table', split_axis=0, concat_axis=0, tiled=True)  8.59 us
    ppermute x3, starting transfers between devices, body(): lax.ppermute(other, 'dp', [(i, (i + k) % n_data) for i in range(n_data)])  5.64 us
    pallas_call x1, Pallas kernels, partial_product(): pl.pallas_call(product_kernel, out_shape=[jax.ShapeDtypeStruct((width, hi...  5.09 us
    all_to_all x1, waiting for transfers between devices, body(): got = lax.all_to_all(sent, 'table', split_axis=0, concat_axis=0, tiled=True)  4.92 us
    all_to_all x1, starting transfers between devices, body(): lax.all_to_all(rows, 'table', split_axis=0, concat_axis=0, tiled=True)  4.01 us
    all_to_all x1, waiting for transfers between devices, body(): lax.all_to_all(rows, 'table', split_axis=0, concat_axis=0, tiled=True)  2.76 us
    ppermute x3, waiting for transfers between devices, body(): lax.ppermute(other, 'dp', [(i, (i + k) % n_data) for i in range(n_data)])  2.66 us
  transfers between devices with their start and end apart: 6, of which 6 were waited for; matrix products, arithmetic and copies ran while one was open for 3% of the time, Pallas kernels for 48%

profile of v10, /device:TPU:1, one launch (start us, length us, event | category | flops | bytes accessed | tf_op | source)
XLA Modules:
  0.0 91.5 jit_solution(6218023418094553530)
XLA Ops:
  7.2 0.0 all-gather.2.cloned.1.call-start
  7.2 0.7 all-gather.2.cloned.1.call-update
  7.9 1.6 %shard_map.77 = s32[32,3,2,128]{3,2,1,0:T(2,128)} custom-call(s32[32,3,2,128]{3,2,1,0:T(2,128)} %bitcast.11, s32[32,128]{1,0:T(8,128)} %bitcast.12), custom_call_target="tpu_custom_call" | custom-call | tf_op jit(solution)/shard_map/pallas_call | solution.py:217
  9.5 8.6 %all-to-all-start = ((s32[32,3,2,128]{3,2,1,0:T(2,128)}), s32[32,3,2,128]{3,2,1,0:T(2,128)S(1)}, u32[]{:S(2)}, u32[]{:S(2)}) async-start(s32[32,3,2,128]{3,2,1,0:T(2,128)} %shard_map.77), calls=%async_computation | async-start | bytes 196608 | tf_op jit(solution)/shard_map/all_to_all | solution.py:263
  18.1 1.1 %copy.8 = bf16[1,250,512]{1,2,0:T(8,128)(2,1)S(1)} copy(bf16[1,250,512]{2,1,0:T(8,128)(2,1)} %param.8) | data formatting | bytes 512000 | tf_op args[2]
  19.2 0.3 copy.9
  19.5 0.1 copy.11
  19.6 0.4 copy.12
  20.1 0.3 fusion.6.first_ref
  20.3 0.3 fusion.4.last_ref
  20.6 4.9 %all-to-all-done.got_ref = s32[32,3,2,128]{3,2,1,0:T(2,128)S(1)} async-done(((s32[32,3,2,128]{3,2,1,0:T(2,128)}), s32[32,3,2,128]{3,2,1,0:T(2,128)S(1)}, u32[]{:S(2)}, u32[]{:S(2)}) %all-to-all-start) | async-done | bytes 98336 | tf_op jit(solution)/shard_map/all_to_all | solution.py:263
  25.5 37.0 %shard_map.78 = bf16[32,128,128]{2,1,0:T(8,128)(2,1)} custom-call(s32[32,3,2,128]{3,2,1,0:T(2,128)S(1)} %all-to-all-done.got_ref, f32[258,8,128]{2,1,0:T(8,128)S(1)} %fusion.6.first_ref, bf16[250,64,128]{2,1,0:T(8,128)(2,1)} %bitcast.13, bf16[250,16,128]{2,1,0:T(8,128)(2,1)S(1)} %fusion.4.last_ref), custom_call_target="tpu_custom_call" | custom-call | flops 16384000000 | bytes 6291456 | tf_op jit(solution)/shard_map/pallas_call | solution.py:130
  62.5 4.0 %all-to-all-start.1 = ((bf16[32,128,128]{2,1,0:T(8,128)(2,1)}), bf16[32,128,128]{2,1,0:T(8,128)(2,1)S(1)}, u32[]{:S(2)}, u32[]{:S(2)}) async-start(bf16[32,128,128]{2,1,0:T(8,128)(2,1)} %shard_map.78), calls=%async_computation.1 | async-start | bytes 2097152 | tf_op jit(solution)/shard_map/all_to_all | solution.py:274
  66.6 0.1 all-gather.2.cloned.1.call-done.grad_ref
  66.7 5.1 %shard_map.79 = (f32[128,256]{1,0:T(8,128)S(1)}, bf16[128,256]{1,0:T(8,128)(2,1)S(1)}, bf16[128,256]{1,0:T(8,128)(2,1)S(1)}, bf16[128,256]{1,0:T(8,128)(2,1)S(1)}) custom-call(s32[1]{0:T(128)} %bitcast.6.place_ref, bf16[4096,128]{1,0:T(8,128)(2,1)} %bitcast.7.rows_ref, bf16[4096,1024]{1,0:T(8,128)(2,1)} %all-gather.2.cloned.1.call-done.grad_ref), custom_call_target="tpu_custom_call" | custom-call | flops 1073741824 | bytes 9437184 | tf_op jit(solution)/shard_map/pallas_call | solution.py:185
  71.8 1.6 %collective-permute-start = (bf16[128,256]{1,0:T(8,128)(2,1)S(1)}, bf16[128,256]{1,0:T(8,128)(2,1)S(1)}, u32[]{:S(2)}, u32[]{:S(2)}) collective-permute-start(bf16[128,256]{1,0:T(8,128)(2,1)S(1)} %get-tuple-element.9), channel_id=1, source_target_pairs={{0,32},{32,64},{64,96},{96,0},{1,33},{33,65},{65,97},{97,1},{2,34}... | collective-permute-start | bytes 196616 | tf_op jit(solution)/shard_map/ppermute | solution.py:279
  73.4 3.3 %collective-permute-start.1 = (bf16[128,256]{1,0:T(8,128)(2,1)S(1)}, bf16[128,256]{1,0:T(8,128)(2,1)S(1)}, u32[]{:S(2)}, u32[]{:S(2)}) collective-permute-start(bf16[128,256]{1,0:T(8,128)(2,1)S(1)} %get-tuple-element.10), channel_id=1, source_target_pairs={{0,64},{32,96},{64,0},{96,32},{1,65},{33,97},{65,1},{97,33},{2,66}... | collective-permute-start | bytes 196616 | tf_op jit(solution)/shard_map/ppermute | solution.py:279
  76.7 0.7 collective-permute-start.2
  77.4 0.3 collective-permute-done
  77.7 2.3 %collective-permute-done.1 = bf16[128,256]{1,0:T(8,128)(2,1)S(1)} collective-permute-done((bf16[128,256]{1,0:T(8,128)(2,1)S(1)}, bf16[128,256]{1,0:T(8,128)(2,1)S(1)}, u32[]{:S(2)}, u32[]{:S(2)}) %collective-permute-start.1) | collective-permute-done | bytes 65568 | tf_op jit(solution)/shard_map/ppermute | solution.py:279
  80.0 0.1 collective-permute-done.2
  80.1 0.7 convert_add_fusion
  80.8 2.8 %all-to-all-done.1.blocks_ref = bf16[32,128,128]{2,1,0:T(8,128)(2,1)S(1)} async-done(((bf16[32,128,128]{2,1,0:T(8,128)(2,1)}), bf16[32,128,128]{2,1,0:T(8,128)(2,1)S(1)}, u32[]{:S(2)}, u32[]{:S(2)}) %all-to-all-start.1) | async-done | bytes 1048608 | tf_op jit(solution)/shard_map/all_to_all | solution.py:274
  83.6 1.0 %shard_map.80 = bf16[128,4096]{1,0:T(8,128)(2,1)} custom-call(bf16[32,128,128]{2,1,0:T(8,128)(2,1)S(1)} %all-to-all-done.1.blocks_ref), custom_call_target="tpu_custom_call" | custom-call | tf_op jit(solution)/shard_map/pallas_call | solution.py:242
  (2 shorter events, 0.0 us)
Async XLA Ops:
  7.2 12.3 %copy-start = (bf16[1,250,512]{2,1,0:T(8,128)(2,1)S(1)}, bf16[1,250,512]{2,1,0:T(8,128)(2,1)}, u32[]{:S(2)}) copy-start(bf16[1,250,512]{2,1,0:T(8,128)(2,1)} %param.10) | copy-start | bytes 768004
  7.2 59.5 %all-gather.2.cloned.1.call-start = ((), (), s32[]{:S(2)}) async-start(), calls=%async_computation.2 | async-start | bytes 8650752 | tf_op jit(solution)/shard_map/all_gather | solution.py:260
  9.5 16.1 %all-to-all-start = ((s32[32,3,2,128]{3,2,1,0:T(2,128)}), s32[32,3,2,128]{3,2,1,0:T(2,128)S(1)}, u32[]{:S(2)}, u32[]{:S(2)}) async-start(s32[32,3,2,128]{3,2,1,0:T(2,128)} %shard_map.77), calls=%async_computation | async-start | bytes 196608 | tf_op jit(solution)/shard_map/all_to_all | solution.py:263
  62.5 21.0 %all-to-all-start.1 = ((bf16[32,128,128]{2,1,0:T(8,128)(2,1)}), bf16[32,128,128]{2,1,0:T(8,128)(2,1)S(1)}, u32[]{:S(2)}, u32[]{:S(2)}) async-start(bf16[32,128,128]{2,1,0:T(8,128)(2,1)} %shard_map.78), calls=%async_computation.1 | async-start | bytes 2097152 | tf_op jit(solution)/shard_map/all_to_all | solution.py:274
  71.8 5.9 %collective-permute-start = (bf16[128,256]{1,0:T(8,128)(2,1)S(1)}, bf16[128,256]{1,0:T(8,128)(2,1)S(1)}, u32[]{:S(2)}, u32[]{:S(2)}) collective-permute-start(bf16[128,256]{1,0:T(8,128)(2,1)S(1)} %get-tuple-element.9), channel_id=1, source_target_pairs={{0,32},{32,64},{64,96},{96,0},{1,33},{33,65},{65,97},{97,1},{2,34}... | collective-permute-start | bytes 196616 | tf_op jit(solution)/shard_map/ppermute | solution.py:279
  73.4 6.6 %collective-permute-start.1 = (bf16[128,256]{1,0:T(8,128)(2,1)S(1)}, bf16[128,256]{1,0:T(8,128)(2,1)S(1)}, u32[]{:S(2)}, u32[]{:S(2)}) collective-permute-start(bf16[128,256]{1,0:T(8,128)(2,1)S(1)} %get-tuple-element.10), channel_id=1, source_target_pairs={{0,64},{32,96},{64,0},{96,32},{1,65},{33,97},{65,1},{97,33},{2,66}... | collective-permute-start | bytes 196616 | tf_op jit(solution)/shard_map/ppermute | solution.py:279
  76.7 3.4 %collective-permute-start.2 = (bf16[128,256]{1,0:T(8,128)(2,1)S(1)}, bf16[128,256]{1,0:T(8,128)(2,1)S(1)}, u32[]{:S(2)}, u32[]{:S(2)}) collective-permute-start(bf16[128,256]{1,0:T(8,128)(2,1)S(1)} %get-tuple-element.11), channel_id=1, source_target_pairs={{0,96},{32,0},{64,32},{96,64},{1,97},{33,1},{65,33},{97,65},{2,98}... | collective-permute-start | bytes 196616 | tf_op jit(solution)/shard_map/ppermute | solution.py:279
Sparse Core Ops, SparseCore 0:
  10.3 56.3 all-gather.1

commit v11 on v10

--- a/solution.py
+++ b/solution.py
@@ -18,7 +18,8 @@
 
 
 def rows_kernel(
-    got_ref, first_ref, core_ref, last_ref, out_ref, prefix_ref, mixed_ref, middle_ref, ids_ref, sems
+    got_ref, first_ref, core_ref, last_ref, rows_ref,
+    prefix_ref, mixed_ref, middle_ref, ids_ref, out_ref, sems, out_sems,
 ):
     f32 = jnp.float32
     bf16 = jnp.bfloat16
@@ -112,15 +113,23 @@
                 prefixes(now, g)
                 prefixes(now, g + 1)
 
-    def steady(i, carry):
+    def turn(i, carry):
         step(i, i - 1, i - 2)
         return carry
 
+    def leave(number, first, count):
+        blocks_of = pl.ds(first, count)
+        return pltpu.make_async_copy(out_ref.at[blocks_of], rows_ref.at[blocks_of], out_sems.at[number])
+
     step(0, None, None)
     step(1, 0, None)
-    lax.fori_loop(2, blocks, steady, 0, unroll=5)
+    lax.fori_loop(2, blocks, turn, 0, unroll=5)
+    leave(0, 0, blocks - 2).start()
     step(None, blocks - 1, blocks - 2)
     step(None, None, blocks - 1)
+    leave(1, blocks - 2, 2).start()
+    leave(0, 0, blocks - 2).wait()
+    leave(1, blocks - 2, 2).wait()
 
 
 def table_rows(got, head, middle, tail):
@@ -131,13 +140,15 @@
         rows_kernel,
         out_shape=jax.ShapeDtypeStruct((senders, own, WIDTH), jnp.bfloat16),
         in_specs=[pl.BlockSpec(memory_space=pl.ANY), vmem, pl.BlockSpec(memory_space=pl.ANY), vmem],
-        out_specs=vmem,
+        out_specs=pl.BlockSpec(memory_space=pl.ANY),
         scratch_shapes=[
             pltpu.VMEM((BLOCK * 8, 256), jnp.bfloat16),
             pltpu.VMEM((BLOCK, 128), jnp.float32),
             pltpu.VMEM(middle.shape, middle.dtype),
             pltpu.SMEM(got.shape, got.dtype),
+            pltpu.VMEM((senders, own, WIDTH), jnp.bfloat16),
             pltpu.SemaphoreType.DMA((FETCHES + 1,)),
+            pltpu.SemaphoreType.DMA((2,)),
         ],
         compiler_params=pltpu.CompilerParams(vmem_limit_bytes=50 << 20),
         cost_estimate=pl.CostEstimate(

time: 91.8 us -> 91.5 us (level)
  no operation moved by 1% of the time
where the time goes in v11:
time: 91.5 us; the launch traced here: 91.1 us
  Pallas kernels  44.4 us (49%)
  starting transfers between devices  17.9 us (20%)
  between operations  14.1 us (15%)
  waiting for transfers between devices  11.5 us (13%)
  local copies, waits for them, and re-layouts  1.96 us (2%)
  other arithmetic  1.21 us (1%)
    pallas_call x1, Pallas kernels, table_rows(): pl.pallas_call(rows_kernel, out_shape=jax.ShapeDtypeStruct((senders, own,...  36.7 us
    all_to_all x1, starting transfers between devices, body(): got = lax.all_to_all(sent, 'table', split_axis=0, concat_axis=0, tiled=True)  8.59 us
    ppermute x3, starting transfers between devices, body(): lax.ppermute(other, 'dp', [(i, (i + k) % n_data) for i in range(n_data)])  5.31 us
    pallas_call x1, Pallas kernels, partial_product(): pl.pallas_call(product_kernel, out_shape=[jax.ShapeDtypeStruct((width, hi...  5.09 us
    all_to_all x1, waiting for transfers between devices, body(): got = lax.all_to_all(sent, 'table', split_axis=0, concat_axis=0, tiled=True)  4.92 us
    all_to_all x1, starting transfers between devices, body(): lax.all_to_all(rows, 'table', split_axis=0, concat_axis=0, tiled=True)  3.99 us
    all_to_all x1, waiting for transfers between devices, body(): lax.all_to_all(rows, 'table', split_axis=0, concat_axis=0, tiled=True)  2.72 us
    ppermute x3, waiting for transfers between devices, body(): lax.ppermute(other, 'dp', [(i, (i + k) % n_data) for i in range(n_data)])  2.69 us
  transfers between devices with their start and end apart: 6, of which 6 were waited for; matrix products, arithmetic and copies ran while one was open for 3% of the time, Pallas kernels for 48%

profile of v11, /device:TPU:1, one launch (start us, length us, event | category | flops | bytes accessed | tf_op | source)
XLA Modules:
  0.0 91.1 jit_solution(16631367407191420220)
XLA Ops:
  7.2 0.0 all-gather.2.cloned.1.call-start
  7.2 0.7 all-gather.2.cloned.1.call-update
  7.9 1.6 %shard_map.77 = s32[32,3,2,128]{3,2,1,0:T(2,128)} custom-call(s32[32,3,2,128]{3,2,1,0:T(2,128)} %bitcast.11, s32[32,128]{1,0:T(8,128)} %bitcast.12), custom_call_target="tpu_custom_call" | custom-call | tf_op jit(solution)/shard_map/pallas_call | solution.py:228
  9.5 8.6 %all-to-all-start = ((s32[32,3,2,128]{3,2,1,0:T(2,128)}), s32[32,3,2,128]{3,2,1,0:T(2,128)S(1)}, u32[]{:S(2)}, u32[]{:S(2)}) async-start(s32[32,3,2,128]{3,2,1,0:T(2,128)} %shard_map.77), calls=%async_computation | async-start | bytes 196608 | tf_op jit(solution)/shard_map/all_to_all | solution.py:274
  18.1 1.1 %copy.8 = bf16[1,250,512]{1,2,0:T(8,128)(2,1)S(1)} copy(bf16[1,250,512]{2,1,0:T(8,128)(2,1)} %param.8) | data formatting | bytes 512000 | tf_op args[2]
  19.2 0.3 copy.9
  19.5 0.1 copy.11
  19.6 0.4 copy.12
  20.1 0.3 fusion.6.first_ref
  20.3 0.3 fusion.4.last_ref
  20.6 4.9 %all-to-all-done.got_ref = s32[32,3,2,128]{3,2,1,0:T(2,128)S(1)} async-done(((s32[32,3,2,128]{3,2,1,0:T(2,128)}), s32[32,3,2,128]{3,2,1,0:T(2,128)S(1)}, u32[]{:S(2)}, u32[]{:S(2)}) %all-to-all-start) | async-done | bytes 98336 | tf_op jit(solution)/shard_map/all_to_all | solution.py:274
  25.5 36.7 %shard_map.78 = bf16[32,128,128]{2,1,0:T(8,128)(2,1)} custom-call(s32[32,3,2,128]{3,2,1,0:T(2,128)S(1)} %all-to-all-done.got_ref, f32[258,8,128]{2,1,0:T(8,128)S(1)} %fusion.6.first_ref, bf16[250,64,128]{2,1,0:T(8,128)(2,1)} %bitcast.13, bf16[250,16,128]{2,1,0:T(8,128)(2,1)S(1)} %fusion.4.last_ref), custom_call_target="tpu_custom_call" | custom-call | flops 16384000000 | bytes 6291456 | tf_op jit(solution)/shard_map/pallas_call | solution.py:139
  62.2 4.0 %all-to-all-start.1 = ((bf16[32,128,128]{2,1,0:T(8,128)(2,1)}), bf16[32,128,128]{2,1,0:T(8,128)(2,1)S(1)}, u32[]{:S(2)}, u32[]{:S(2)}) async-start(bf16[32,128,128]{2,1,0:T(8,128)(2,1)} %shard_map.78), calls=%async_computation.1 | async-start | bytes 2097152 | tf_op jit(solution)/shard_map/all_to_all | solution.py:285
  66.2 0.5 all-gather.2.cloned.1.call-done.grad_ref
  66.7 5.1 %shard_map.79 = (f32[128,256]{1,0:T(8,128)S(1)}, bf16[128,256]{1,0:T(8,128)(2,1)S(1)}, bf16[128,256]{1,0:T(8,128)(2,1)S(1)}, bf16[128,256]{1,0:T(8,128)(2,1)S(1)}) custom-call(s32[1]{0:T(128)} %bitcast.6.place_ref, bf16[4096,128]{1,0:T(8,128)(2,1)} %bitcast.7.rows_ref, bf16[4096,1024]{1,0:T(8,128)(2,1)} %all-gather.2.cloned.1.call-done.grad_ref), custom_call_target="tpu_custom_call" | custom-call | flops 1073741824 | bytes 9437184 | tf_op jit(solution)/shard_map/pallas_call | solution.py:196
  71.8 1.3 %collective-permute-start = (bf16[128,256]{1,0:T(8,128)(2,1)S(1)}, bf16[128,256]{1,0:T(8,128)(2,1)S(1)}, u32[]{:S(2)}, u32[]{:S(2)}) collective-permute-start(bf16[128,256]{1,0:T(8,128)(2,1)S(1)} %get-tuple-element.9), channel_id=1, source_target_pairs={{0,32},{32,64},{64,96},{96,0},{1,33},{33,65},{65,97},{97,1},{2,34}... | collective-permute-start | bytes 196616 | tf_op jit(solution)/shard_map/ppermute | solution.py:290
  73.1 3.2 %collective-permute-start.1 = (bf16[128,256]{1,0:T(8,128)(2,1)S(1)}, bf16[128,256]{1,0:T(8,128)(2,1)S(1)}, u32[]{:S(2)}, u32[]{:S(2)}) collective-permute-start(bf16[128,256]{1,0:T(8,128)(2,1)S(1)} %get-tuple-element.10), channel_id=1, source_target_pairs={{0,64},{32,96},{64,0},{96,32},{1,65},{33,97},{65,1},{97,33},{2,66}... | collective-permute-start | bytes 196616 | tf_op jit(solution)/shard_map/ppermute | solution.py:290
  76.4 0.7 collective-permute-start.2
  77.1 0.3 collective-permute-done
  77.4 2.3 %collective-permute-done.1 = bf16[128,256]{1,0:T(8,128)(2,1)S(1)} collective-permute-done((bf16[128,256]{1,0:T(8,128)(2,1)S(1)}, bf16[128,256]{1,0:T(8,128)(2,1)S(1)}, u32[]{:S(2)}, u32[]{:S(2)}) %collective-permute-start.1) | collective-permute-done | bytes 65568 | tf_op jit(solution)/shard_map/ppermute | solution.py:290
  79.7 0.1 collective-permute-done.2
  79.8 0.7 convert_add_fusion
  80.5 2.7 %all-to-all-done.1.blocks_ref = bf16[32,128,128]{2,1,0:T(8,128)(2,1)S(1)} async-done(((bf16[32,128,128]{2,1,0:T(8,128)(2,1)}), bf16[32,128,128]{2,1,0:T(8,128)(2,1)S(1)}, u32[]{:S(2)}, u32[]{:S(2)}) %all-to-all-start.1) | async-done | bytes 1048608 | tf_op jit(solution)/shard_map/all_to_all | solution.py:285
  83.2 1.0 %shard_map.80 = bf16[128,4096]{1,0:T(8,128)(2,1)} custom-call(bf16[32,128,128]{2,1,0:T(8,128)(2,1)S(1)} %all-to-all-done.1.blocks_ref), custom_call_target="tpu_custom_call" | custom-call | tf_op jit(solution)/shard_map/pallas_call | solution.py:253
  (2 shorter events, 0.0 us)
Async XLA Ops:
  7.2 12.3 %copy-start = (bf16[1,250,512]{2,1,0:T(8,128)(2,1)S(1)}, bf16[1,250,512]{2,1,0:T(8,128)(2,1)}, u32[]{:S(2)}) copy-start(bf16[1,250,512]{2,1,0:T(8,128)(2,1)} %param.10) | copy-start | bytes 768004
  7.2 59.5 %all-gather.2.cloned.1.call-start = ((), (), s32[]{:S(2)}) async-start(), calls=%async_computation.2 | async-start | bytes 8650752 | tf_op jit(solution)/shard_map/all_gather | solution.py:271
  9.5 16.1 %all-to-all-start = ((s32[32,3,2,128]{3,2,1,0:T(2,128)}), s32[32,3,2,128]{3,2,1,0:T(2,128)S(1)}, u32[]{:S(2)}, u32[]{:S(2)}) async-start(s32[32,3,2,128]{3,2,1,0:T(2,128)} %shard_map.77), calls=%async_computation | async-start | bytes 196608 | tf_op jit(solution)/shard_map/all_to_all | solution.py:274
  62.2 21.0 %all-to-all-start.1 = ((bf16[32,128,128]{2,1,0:T(8,128)(2,1)}), bf16[32,128,128]{2,1,0:T(8,128)(2,1)S(1)}, u32[]{:S(2)}, u32[]{:S(2)}) async-start(bf16[32,128,128]{2,1,0:T(8,128)(2,1)} %shard_map.78), calls=%async_computation.1 | async-start | bytes 2097152 | tf_op jit(solution)/shard_map/all_to_all | solution.py:285
  71.8 5.6 %collective-permute-start = (bf16[128,256]{1,0:T(8,128)(2,1)S(1)}, bf16[128,256]{1,0:T(8,128)(2,1)S(1)}, u32[]{:S(2)}, u32[]{:S(2)}) collective-permute-start(bf16[128,256]{1,0:T(8,128)(2,1)S(1)} %get-tuple-element.9), channel_id=1, source_target_pairs={{0,32},{32,64},{64,96},{96,0},{1,33},{33,65},{65,97},{97,1},{2,34}... | collective-permute-start | bytes 196616 | tf_op jit(solution)/shard_map/ppermute | solution.py:290
  73.1 6.5 %collective-permute-start.1 = (bf16[128,256]{1,0:T(8,128)(2,1)S(1)}, bf16[128,256]{1,0:T(8,128)(2,1)S(1)}, u32[]{:S(2)}, u32[]{:S(2)}) collective-permute-start(bf16[128,256]{1,0:T(8,128)(2,1)S(1)} %get-tuple-element.10), channel_id=1, source_target_pairs={{0,64},{32,96},{64,0},{96,32},{1,65},{33,97},{65,1},{97,33},{2,66}... | collective-permute-start | bytes 196616 | tf_op jit(solution)/shard_map/ppermute | solution.py:290
  76.4 3.4 %collective-permute-start.2 = (bf16[128,256]{1,0:T(8,128)(2,1)S(1)}, bf16[128,256]{1,0:T(8,128)(2,1)S(1)}, u32[]{:S(2)}, u32[]{:S(2)}) collective-permute-start(bf16[128,256]{1,0:T(8,128)(2,1)S(1)} %get-tuple-element.11), channel_id=1, source_target_pairs={{0,96},{32,0},{64,32},{96,64},{1,97},{33,1},{65,33},{97,65},{2,98}... | collective-permute-start | bytes 196616 | tf_op jit(solution)/shard_map/ppermute | solution.py:290
Sparse Core Ops, SparseCore 0:
  10.3 56.3 all-gather.1

commit v12 on v11

--- a/solution.py
+++ b/solution.py
@@ -191,7 +191,7 @@
 def partial_product(rows, grad, place, parts):
     samples, width = rows.shape
     hidden_units = grad.shape[1]
-    size = min(samples, 512)
+    size = min(samples, 256)
     vmem = pl.BlockSpec(memory_space=pltpu.VMEM)
     return pl.pallas_call(
         product_kernel,

time: 91.5 us -> 91.5 us (level)
  no operation moved by 1% of the time
where the time goes in v12:
time: 91.5 us; the launch traced here: 91.1 us
  Pallas kernels  44.4 us (49%)
  starting transfers between devices  17.9 us (20%)
  between operations  14.1 us (15%)
  waiting for transfers between devices  11.6 us (13%)
  local copies, waits for them, and re-layouts  1.96 us (2%)
  other arithmetic  1.21 us (1%)
    pallas_call x1, Pallas kernels, table_rows(): pl.pallas_call(rows_kernel, out_shape=jax.ShapeDtypeStruct((senders, own,...  36.7 us
    all_to_all x1, starting transfers between devices, body(): got = lax.all_to_all(sent, 'table', split_axis=0, concat_axis=0, tiled=True)  8.59 us
    ppermute x3, starting transfers between devices, body(): lax.ppermute(other, 'dp', [(i, (i + k) % n_data) for i in range(n_data)])  5.3 us
    pallas_call x1, Pallas kernels, partial_product(): pl.pallas_call(product_kernel, out_shape=[jax.ShapeDtypeStruct((width, hi...  5.05 us
    all_to_all x1, waiting for transfers between devices, body(): got = lax.all_to_all(sent, 'table', split_axis=0, concat_axis=0, tiled=True)  4.92 us
    all_to_all x1, starting transfers between devices, body(): lax.all_to_all(rows, 'table', split_axis=0, concat_axis=0, tiled=True)  3.99 us
    all_to_all x1, waiting for transfers between devices, body(): lax.all_to_all(rows, 'table', split_axis=0, concat_axis=0, tiled=True)  2.78 us
    ppermute x3, waiting for transfers between devices, body(): lax.ppermute(other, 'dp', [(i, (i + k) % n_data) for i in range(n_data)])  2.7 us
  transfers between devices with their start and end apart: 6, of which 6 were waited for; matrix products, arithmetic and copies ran while one was open for 3% of the time, Pallas kernels for 48%

profile of v12, /device:TPU:1, one launch (start us, length us, event | category | flops | bytes accessed | tf_op | source)
XLA Modules:
  0.0 91.1 jit_solution(15054904094046235817)
XLA Ops:
  7.2 0.0 all-gather.2.cloned.1.call-start
  7.2 0.7 all-gather.2.cloned.1.call-update
  7.9 1.6 %shard_map.77 = s32[32,3,2,128]{3,2,1,0:T(2,128)} custom-call(s32[32,3,2,128]{3,2,1,0:T(2,128)} %bitcast.11, s32[32,128]{1,0:T(8,128)} %bitcast.12), custom_call_target="tpu_custom_call" | custom-call | tf_op jit(solution)/shard_map/pallas_call | solution.py:228
  9.5 8.6 %all-to-all-start = ((s32[32,3,2,128]{3,2,1,0:T(2,128)}), s32[32,3,2,128]{3,2,1,0:T(2,128)S(1)}, u32[]{:S(2)}, u32[]{:S(2)}) async-start(s32[32,3,2,128]{3,2,1,0:T(2,128)} %shard_map.77), calls=%async_computation | async-start | bytes 196608 | tf_op jit(solution)/shard_map/all_to_all | solution.py:274
  18.1 1.1 %copy.8 = bf16[1,250,512]{1,2,0:T(8,128)(2,1)S(1)} copy(bf16[1,250,512]{2,1,0:T(8,128)(2,1)} %param.8) | data formatting | bytes 512000 | tf_op args[2]
  19.2 0.3 copy.9
  19.5 0.1 copy.11
  19.6 0.4 copy.12
  20.1 0.3 fusion.6.first_ref
  20.3 0.3 fusion.4.last_ref
  20.6 4.9 %all-to-all-done.got_ref = s32[32,3,2,128]{3,2,1,0:T(2,128)S(1)} async-done(((s32[32,3,2,128]{3,2,1,0:T(2,128)}), s32[32,3,2,128]{3,2,1,0:T(2,128)S(1)}, u32[]{:S(2)}, u32[]{:S(2)}) %all-to-all-start) | async-done | bytes 98336 | tf_op jit(solution)/shard_map/all_to_all | solution.py:274
  25.5 36.7 %shard_map.78 = bf16[32,128,128]{2,1,0:T(8,128)(2,1)} custom-call(s32[32,3,2,128]{3,2,1,0:T(2,128)S(1)} %all-to-all-done.got_ref, f32[258,8,128]{2,1,0:T(8,128)S(1)} %fusion.6.first_ref, bf16[250,64,128]{2,1,0:T(8,128)(2,1)} %bitcast.13, bf16[250,16,128]{2,1,0:T(8,128)(2,1)S(1)} %fusion.4.last_ref), custom_call_target="tpu_custom_call" | custom-call | flops 16384000000 | bytes 6291456 | tf_op jit(solution)/shard_map/pallas_call | solution.py:139
  62.2 4.0 %all-to-all-start.1 = ((bf16[32,128,128]{2,1,0:T(8,128)(2,1)}), bf16[32,128,128]{2,1,0:T(8,128)(2,1)S(1)}, u32[]{:S(2)}, u32[]{:S(2)}) async-start(bf16[32,128,128]{2,1,0:T(8,128)(2,1)} %shard_map.78), calls=%async_computation.1 | async-start | bytes 2097152 | tf_op jit(solution)/shard_map/all_to_all | solution.py:285
  66.2 0.5 all-gather.2.cloned.1.call-done.grad_ref
  66.7 5.0 %shard_map.79 = (f32[128,256]{1,0:T(8,128)S(1)}, bf16[128,256]{1,0:T(8,128)(2,1)S(1)}, bf16[128,256]{1,0:T(8,128)(2,1)S(1)}, bf16[128,256]{1,0:T(8,128)(2,1)S(1)}) custom-call(s32[1]{0:T(128)} %bitcast.6.place_ref, bf16[4096,128]{1,0:T(8,128)(2,1)} %bitcast.7.rows_ref, bf16[4096,1024]{1,0:T(8,128)(2,1)} %all-gather.2.cloned.1.call-done.grad_ref), custom_call_target="tpu_custom_call" | custom-call | flops 1073741824 | bytes 9437184 | tf_op jit(solution)/shard_map/pallas_call | solution.py:196
  71.8 1.3 %collective-permute-start = (bf16[128,256]{1,0:T(8,128)(2,1)S(1)}, bf16[128,256]{1,0:T(8,128)(2,1)S(1)}, u32[]{:S(2)}, u32[]{:S(2)}) collective-permute-start(bf16[128,256]{1,0:T(8,128)(2,1)S(1)} %get-tuple-element.9), channel_id=1, source_target_pairs={{0,32},{32,64},{64,96},{96,0},{1,33},{33,65},{65,97},{97,1},{2,34}... | collective-permute-start | bytes 196616 | tf_op jit(solution)/shard_map/ppermute | solution.py:290
  73.1 3.2 %collective-permute-start.1 = (bf16[128,256]{1,0:T(8,128)(2,1)S(1)}, bf16[128,256]{1,0:T(8,128)(2,1)S(1)}, u32[]{:S(2)}, u32[]{:S(2)}) collective-permute-start(bf16[128,256]{1,0:T(8,128)(2,1)S(1)} %get-tuple-element.10), channel_id=1, source_target_pairs={{0,64},{32,96},{64,0},{96,32},{1,65},{33,97},{65,1},{97,33},{2,66}... | collective-permute-start | bytes 196616 | tf_op jit(solution)/shard_map/ppermute | solution.py:290
  76.3 0.7 collective-permute-start.2
  77.1 0.3 collective-permute-done
  77.3 2.3 %collective-permute-done.1 = bf16[128,256]{1,0:T(8,128)(2,1)S(1)} collective-permute-done((bf16[128,256]{1,0:T(8,128)(2,1)S(1)}, bf16[128,256]{1,0:T(8,128)(2,1)S(1)}, u32[]{:S(2)}, u32[]{:S(2)}) %collective-permute-start.1) | collective-permute-done | bytes 65568 | tf_op jit(solution)/shard_map/ppermute | solution.py:290
  79.6 0.1 collective-permute-done.2
  79.8 0.7 convert_add_fusion
  80.4 2.8 %all-to-all-done.1.blocks_ref = bf16[32,128,128]{2,1,0:T(8,128)(2,1)S(1)} async-done(((bf16[32,128,128]{2,1,0:T(8,128)(2,1)}), bf16[32,128,128]{2,1,0:T(8,128)(2,1)S(1)}, u32[]{:S(2)}, u32[]{:S(2)}) %all-to-all-start.1) | async-done | bytes 1048608 | tf_op jit(solution)/shard_map/all_to_all | solution.py:285
  83.2 1.0 %shard_map.80 = bf16[128,4096]{1,0:T(8,128)(2,1)} custom-call(bf16[32,128,128]{2,1,0:T(8,128)(2,1)S(1)} %all-to-all-done.1.blocks_ref), custom_call_target="tpu_custom_call" | custom-call | tf_op jit(solution)/shard_map/pallas_call | solution.py:253
  (2 shorter events, 0.0 us)
Async XLA Ops:
  7.2 12.3 %copy-start = (bf16[1,250,512]{2,1,0:T(8,128)(2,1)S(1)}, bf16[1,250,512]{2,1,0:T(8,128)(2,1)}, u32[]{:S(2)}) copy-start(bf16[1,250,512]{2,1,0:T(8,128)(2,1)} %param.10) | copy-start | bytes 768004
  7.2 59.5 %all-gather.2.cloned.1.call-start = ((), (), s32[]{:S(2)}) async-start(), calls=%async_computation.2 | async-start | bytes 8650752 | tf_op jit(solution)/shard_map/all_gather | solution.py:271
  9.5 16.1 %all-to-all-start = ((s32[32,3,2,128]{3,2,1,0:T(2,128)}), s32[32,3,2,128]{3,2,1,0:T(2,128)S(1)}, u32[]{:S(2)}, u32[]{:S(2)}) async-start(s32[32,3,2,128]{3,2,1,0:T(2,128)} %shard_map.77), calls=%async_computation | async-start | bytes 196608 | tf_op jit(solution)/shard_map/all_to_all | solution.py:274
  62.2 21.0 %all-to-all-start.1 = ((bf16[32,128,128]{2,1,0:T(8,128)(2,1)}), bf16[32,128,128]{2,1,0:T(8,128)(2,1)S(1)}, u32[]{:S(2)}, u32[]{:S(2)}) async-start(bf16[32,128,128]{2,1,0:T(8,128)(2,1)} %shard_map.78), calls=%async_computation.1 | async-start | bytes 2097152 | tf_op jit(solution)/shard_map/all_to_all | solution.py:285
  71.8 5.6 %collective-permute-start = (bf16[128,256]{1,0:T(8,128)(2,1)S(1)}, bf16[128,256]{1,0:T(8,128)(2,1)S(1)}, u32[]{:S(2)}, u32[]{:S(2)}) collective-permute-start(bf16[128,256]{1,0:T(8,128)(2,1)S(1)} %get-tuple-element.9), channel_id=1, source_target_pairs={{0,32},{32,64},{64,96},{96,0},{1,33},{33,65},{65,97},{97,1},{2,34}... | collective-permute-start | bytes 196616 | tf_op jit(solution)/shard_map/ppermute | solution.py:290
  73.1 6.5 %collective-permute-start.1 = (bf16[128,256]{1,0:T(8,128)(2,1)S(1)}, bf16[128,256]{1,0:T(8,128)(2,1)S(1)}, u32[]{:S(2)}, u32[]{:S(2)}) collective-permute-start(bf16[128,256]{1,0:T(8,128)(2,1)S(1)} %get-tuple-element.10), channel_id=1, source_target_pairs={{0,64},{32,96},{64,0},{96,32},{1,65},{33,97},{65,1},{97,33},{2,66}... | collective-permute-start | bytes 196616 | tf_op jit(solution)/shard_map/ppermute | solution.py:290
  76.3 3.4 %collective-permute-start.2 = (bf16[128,256]{1,0:T(8,128)(2,1)S(1)}, bf16[128,256]{1,0:T(8,128)(2,1)S(1)}, u32[]{:S(2)}, u32[]{:S(2)}) collective-permute-start(bf16[128,256]{1,0:T(8,128)(2,1)S(1)} %get-tuple-element.11), channel_id=1, source_target_pairs={{0,96},{32,0},{64,32},{96,64},{1,97},{33,1},{65,33},{97,65},{2,98}... | collective-permute-start | bytes 196616 | tf_op jit(solution)/shard_map/ppermute | solution.py:290
Sparse Core Ops, SparseCore 0:
  10.3 56.3 all-gather.1
